TPU v7x, 256 devices: a whole 4x4x8 slice. The times are simulated.
256 devices in a mesh: row: 16 (over y_hi, x, core), col: 16 (over y_lo, z).
Axes of the slice: x: 4, y: 4 (y_hi: 2, y_lo: 2; y = y_hi * 2 + y_lo), z: 8, core: 2. Of those that a mesh axis runs over, the one named last changes fastest.
Arguments:
- pool: bfloat16 [32768, 128], P(('row', 'col')), may hold values from -6 to 6
- targets: bfloat16 [32768], P(('row', 'col')), may hold values from -15 to 15
- picks: int32 [4096], P(('row', 'col')), may hold values from 0 to 127
- inducing: float32 [8192, 128], replicated, may hold values from -6 to 6
- inv_sq_lengths: float32 [128], replicated, may hold values from 0.04 to 0.12
- prec_old: float32 [8192, 8192], P('row', 'col'), may hold values from -1 to 6, as said below
- mean_old: float32 [8192], P('row'), may hold values from -6 to 6
- panel: int32 [1], replicated, may hold values from 0 to 31
Outputs:
- prec_new: float32 [8192, 8192], P('row', 'col')
- mean_new: float32 [8192], P('row')
Inputs may be any that keep to these rules, and one draw needn't show every extreme that they name: `picks`: each entry indexes a row of the dataset block held by the same device as the entry. `prec_old`: symmetric and positive definite.
All inputs are finite; a program needn't handle non-finite values.
Results may differ from a plain program's by a relative error of at most 0.0028.
Values may be sent and summed in bfloat16 or wider, within the bound.
No kernel may reach another device: no remote copies, remote signals or barrier semaphores. Data moves between devices by JAX's collectives and lax.ppermute only.
A program may use at most 128 MiB of HBM per device.

v0:
```python
import jax
import jax.numpy as jnp
from jax import lax
from jax.sharding import Mesh
from jax.sharding import PartitionSpec as P

M = 8192
PB = 256
ROW_COL = ("row_0", "row_1", "row_2", "col_0", "col_1")
ROW = ("row_0", "row_1", "row_2")
COL = ("col_0", "col_1")


RATE = 0.5
EPSILON = 1e-05


def over_axes(value, axes):
    for axis in axes:
        value = lax.psum(value, axis)
    return value


def side_by_side(arrays, axis, dim, along):
    columns = [a.reshape(*a.shape[:along], -1) for a in arrays]
    both = jnp.concatenate(columns, axis=along)
    out, at, finished = (lax.all_gather(both, axis, axis=dim, tiled=True), 0, [])
    for a, column in zip(arrays, columns):
        slab = out[..., at : at + column.shape[along]]
        finished.append(slab.reshape(*slab.shape[:along], *a.shape[along:]))
        at += column.shape[along]
    return tuple(finished)


def in_blocks(value, dim, devices):
    shape = value.shape
    blocks = value.reshape(*shape[:dim], devices, shape[dim] // devices, *shape[dim + 1 :])
    return jnp.moveaxis(blocks, dim, 0)


def summed_on_arrival(value, axis, dim):
    blocks = in_blocks(value, dim, lax.axis_size(axis))
    arrived = lax.all_to_all(blocks, axis, split_axis=0, concat_axis=0, tiled=True)
    return arrived.sum(axis=0)


def picked(value, axis, root):
    return lax.dynamic_index_in_dim(lax.all_gather(value, axis), root, 0, keepdims=False)


def kernel_block(points, weights, sample_x):
    sample_f = sample_x.astype(jnp.float32)
    point_sq = jnp.sum(points * points * weights, axis=1)
    sample_sq = jnp.sum(sample_f * sample_f * weights, axis=1)
    cross_term = lax.dot_general(
        points * weights, sample_f, (((1,), (1,)), ((), ())), precision=lax.Precision.HIGHEST
    )
    return jnp.exp(-0.5 * (point_sq[:, None] + sample_sq[None, :] - 2.0 * cross_term)).astype(
        jnp.bfloat16
    )


def local_diag(gram_tile, row_base, col_base):
    row_ids = row_base + jnp.arange(gram_tile.shape[0], dtype=jnp.int32)
    col_ids = col_base + jnp.arange(gram_tile.shape[1], dtype=jnp.int32)
    on_diag = row_ids[:, None] == col_ids[None, :]
    return jnp.sum(jnp.where(on_diag, gram_tile, 0.0))


def diag_total(gram_tile, row_base, col_base):
    return over_axes(local_diag(gram_tile, row_base, col_base), ROW_COL)


def local(pool, targets, picks, inducing, inv_sq_lengths, prec_old, mean_old, panel):
    n_rows = lax.axis_size(ROW)
    n_cols = lax.axis_size(COL)
    my_row = lax.axis_index(ROW)
    my_col = lax.axis_index(COL)
    tile_rows, tile_cols = prec_old.shape
    batch_count = picks.shape[0] * n_rows * n_cols
    row_base = my_row * tile_rows
    col_base = my_col * tile_cols
    samples = jnp.take(pool, picks, axis=0)
    values = jnp.take(targets, picks, axis=0)
    group_x, group_y = side_by_side((samples, values), COL, 0, 1)
    features = kernel_block(inducing, inv_sq_lengths, group_x)
    feat_cols = lax.dynamic_slice_in_dim(features, col_base, tile_cols, 0)
    own_y = values.astype(jnp.float32)
    power_sum = over_axes(jnp.sum(own_y * own_y), ROW_COL)
    gram_tile = lax.psum_scatter(
        lax.dot_general(
            features, feat_cols, (((1,), (1,)), ((), ())), preferred_element_type=jnp.float32
        ),
        ROW,
        scatter_dimension=0,
        tiled=True,
    )
    fit_part = summed_on_arrival(
        jnp.dot(features, group_y, preferred_element_type=jnp.float32), ROW, 0
    )
    trace_sum = diag_total(gram_tile, row_base, col_base)
    trace_scale = trace_sum / M
    joined = (1.0 - RATE) * prec_old + RATE * gram_tile / trace_scale
    mean_mid = (1.0 - RATE) * mean_old + RATE * fit_part / jnp.sqrt(
        trace_scale * (power_sum / batch_count + EPSILON)
    )
    panel_start = panel[0] * PB
    owner_row = panel_start // tile_rows
    owner_col = panel_start // tile_cols
    offset_row = panel_start - owner_row * tile_rows
    offset_col = panel_start - owner_col * tile_cols
    zero_index = jnp.zeros((), jnp.int32)
    col_piece = lax.dynamic_slice(joined, (zero_index, offset_col), (tile_rows, PB))
    got_cols = picked(col_piece, COL, owner_col)
    row_piece = lax.dynamic_slice(joined, (offset_row, zero_index), (PB, tile_cols))
    mean_piece = lax.dynamic_slice(mean_mid, (offset_row,), (PB,))
    diag_piece = lax.dynamic_slice(got_cols, (offset_row, zero_index), (PB, PB))
    got_rows, got_mean, got_block = (
        picked(row_piece, ROW, owner_row),
        picked(mean_piece, ROW, owner_row),
        picked(diag_piece, ROW, owner_row),
    )
    factor = jnp.linalg.cholesky(got_block)
    identity = jnp.eye(PB, dtype=jnp.float32)
    inv_factor = lax.linalg.triangular_solve(factor, identity, left_side=True, lower=True)
    wide_rows = lax.dot_general(
        got_cols, inv_factor, (((1,), (1,)), ((), ())), precision=lax.Precision.HIGHEST
    )
    solved_rows = jnp.dot(inv_factor, got_rows, precision=lax.Precision.HIGHEST)
    head_part = jnp.dot(inv_factor, got_mean, precision=lax.Precision.HIGHEST)
    updated = joined - jnp.dot(wide_rows, solved_rows, precision=lax.Precision.HIGHEST)
    in_col = my_col == owner_col
    in_row = my_row == owner_row
    updated = jnp.where(
        in_col, lax.dynamic_update_slice(updated, wide_rows, (zero_index, offset_col)), updated
    )
    updated = jnp.where(
        in_row, lax.dynamic_update_slice(updated, solved_rows, (offset_row, zero_index)), updated
    )
    updated = jnp.where(
        jnp.logical_and(in_row, in_col),
        lax.dynamic_update_slice(updated, factor, (offset_row, offset_col)),
        updated,
    )
    mean_next = mean_mid - jnp.dot(wide_rows, head_part, precision=lax.Precision.HIGHEST)
    mean_next = jnp.where(
        in_row, lax.dynamic_update_slice(mean_next, head_part, (offset_row,)), mean_next
    )
    return (updated, mean_next)


def solution(mesh):
    split = Mesh(mesh.devices.reshape(2, 4, 2, 2, 8), ("row_0", "row_1", "row_2", "col_0", "col_1"))
    return jax.shard_map(
        local,
        mesh=split,
        in_specs=(P(ROW_COL, None), P(ROW_COL), P(ROW_COL), P(), P(), P(ROW, COL), P(ROW), P()),
        out_specs=(P(ROW, COL), P(ROW)),
        check_vma=False,
    )
```

profile of v0, /device:TPU:1, one launch (start us, length us, event | category | flops | bytes accessed | tf_op | source)
XLA Modules:
  0.0 518.6 jit_solution(1494398708425106980)
XLA Ops:
  7.9 1.3 gather_fusion.1
  9.2 1.3 multiply_reduce_fusion.2
  11.3 30.8 %all_gather.25 = bf16[256,129]{1,0:T(8,128)(2,1)S(1)} all-gather(bf16[16,129]{1,0:T(8,128)(2,1)S(1)} %pad_maximum_fusion.4), channel_id=1, replica_groups=mesh['row_0'=2,'row_1'=4,'row_2'=2,'col_0'=2,'col_1'=8] {'col_0','col_1'}, dimensions={0}, use_global_device_ids=true | all-gather | bytes 70176 | tf_op jit(solution)/shard_map/all_gather | solution.py:27
  42.8 3.3 multiply_reduce_fusion
  46.2 5.9 %fusion.3 = bf16[8192,256]{1,0:T(8,128)(2,1)S(1)} fusion(f32[8192,128]{1,0:T(8,128)} %param.11, f32[256]{0:T(256)S(1)} %multiply_reduce_fusion.1, f32[8192]{0:T(1024)S(1)} %multiply_reduce_fusion, f32[128]{0:T(128)S(1)} %copy-done.5, bf16[256,129]{1,0:T(8,128)(2,1)S(1)} %all_gather.25), kind=kOutput, calls=%fused_computation.8 | convolution fusion | flops 3232759808 | bytes 8488448 | tf_op jit(solution)/shard_map/dot_general | solution.py:55
  52.1 1.9 copy-done.1
  54.0 8.1 %fusion.14 = f32[8192,512]{1,0:T(8,128)} fusion(bf16[8192,256]{1,0:T(8,128)(2,1)S(1)} %fusion.3, s32[]{:T(128)S(6)} %select_n.109), kind=kOutput, calls=%fused_computation.33 | convolution fusion | flops 2147483648 | bytes 21233668 | tf_op jit(solution)/shard_map/dot_general | solution.py:91
  62.9 156.7 %reduce-scatter.2.cloned.1.call-done = f32[512,512]{1,0:T(8,128)} async-done(((f32[8192,512]{1,0:T(8,128)}), f32[512,512]{1,0:T(8,128)}) %reduce-scatter.2.cloned.1.call-update) | async-done | bytes 1048592 | tf_op jit(solution)/shard_map/reduce_scatter | solution.py:90
  219.6 2.2 select_reduce_fusion
  221.8 5.9 %all-reduce.5 = (f32[]{:T(128)}, f32[]{:T(128)}) all-reduce(f32[]{:T(128)} %select_reduce_fusion, f32[]{:T(128)} %get-tuple-element.28), channel_id=1, replica_groups=mesh['row_0'=2,'row_1'=4,'row_2'=2,'col_0'=2,'col_1'=8] {'row_0'}, use_global_device_ids=true, to_apply=%region_4.5 | all-reduce | flops 2 | bytes 16 | tf_op jit(solution)/shard_map/psum | solution.py:20
  227.6 7.2 %all-reduce.2 = (f32[]{:T(128)}, f32[]{:T(128)}) all-reduce(f32[]{:T(128)} %get-tuple-element.26, f32[]{:T(128)} %get-tuple-element.27), channel_id=1, replica_groups=mesh['row_0'=2,'row_1'=4,'row_2'=2,'col_0'=2,'col_1'=8] {'row_1'}, use_global_device_ids=true, to_apply=%region_5.6 | all-reduce | flops 2 | bytes 16 | tf_op jit(solution)/shard_map/psum | solution.py:20
  234.8 7.7 %all-reduce.4 = (f32[]{:T(128)}, f32[]{:T(128)}) all-reduce(f32[]{:T(128)} %get-tuple-element.20, f32[]{:T(128)} %get-tuple-element.21), channel_id=1, replica_groups=mesh['row_0'=2,'row_1'=4,'row_2'=2,'col_0'=2,'col_1'=8] {'row_2'}, use_global_device_ids=true, to_apply=%region_6.7 | all-reduce | flops 2 | bytes 16 | tf_op jit(solution)/shard_map/psum | solution.py:20
  242.5 4.4 all-reduce.3
  246.9 14.3 %all-reduce.1 = (f32[]{:T(128)}, f32[]{:T(128)}) all-reduce(f32[]{:T(128)} %get-tuple-element.22, f32[]{:T(128)} %get-tuple-element.23), channel_id=1, replica_groups=mesh['row_0'=2,'row_1'=4,'row_2'=2,'col_0'=2,'col_1'=8] {'col_1'}, use_global_device_ids=true, to_apply=%region_8.9 | all-reduce | flops 2 | bytes 16 | tf_op jit(solution)/shard_map/psum | solution.py:20
  261.9 1.5 divide_add_fusion
  264.3 100.1 %all-gather.10.cloned.1.call-done = f32[8192,256]{1,0:T(8,128)} async-done(((f32[512,256]{1,0:T(8,128)}), f32[8192,256]{1,0:T(8,128)}) %all-gather.10.cloned.1.call-update) | async-done | bytes 8388624 | tf_op jit(solution)/shard_map/all_gather | solution.py:48
  364.4 1.7 constant_dynamic-slice_fusion.4
  367.2 3.4 fusion.37
  371.2 7.3 %all-to-all-start = ((f32[16,1,512]{2,1,0:T(1,128)}), f32[16,1,512]{2,1,0:T(1,128)S(1)}, u32[]{:S(2)}, u32[]{:S(2)}) async-start(f32[16,1,512]{2,1,0:T(1,128)} %all_to_all.6), calls=%async_computation.1 | async-start | bytes 65536 | tf_op jit(solution)/shard_map/all_to_all | solution.py:43
  378.5 7.2 %all-to-all-done = f32[16,1,512]{2,1,0:T(1,128)S(1)} async-done(((f32[16,1,512]{2,1,0:T(1,128)}), f32[16,1,512]{2,1,0:T(1,128)S(1)}, u32[]{:S(2)}, u32[]{:S(2)}) %all-to-all-start) | async-done | bytes 32800 | tf_op jit(solution)/shard_map/all_to_all | solution.py:43
  386.6 20.6 %all-gather.3 = f32[16,1,256]{2,1,0:T(1,128)S(1)} all-gather(f32[1,1,256]{2,1,0:T(1,128)S(1)} %bitcast.74), channel_id=4, replica_groups=mesh['row_0'=2,'row_1'=4,'row_2'=2,'col_0'=2,'col_1'=8] {'row_0','row_1'..., dimensions={0}, use_global_device_ids=true | all-gather | bytes 17408 | tf_op jit(solution)/shard_map/all_gather | solution.py:48
  407.2 19.5 %all-gather.8.cloned.1.call-done = f32[16,256,256]{2,1,0:T(8,128)} async-done(((f32[1,256,256]{2,1,0:T(8,128)}), f32[16,256,256]{2,1,0:T(8,128)}) %all-gather.8.cloned.1.call-update) | async-done | bytes 4194320 | tf_op jit(solution)/shard_map/all_gather | solution.py:48
  428.9 11.7 %cholesky.50 = f32[128,128]{1,0:T(8,128)S(1)} custom-call(f32[128,128]{1,0:T(8,128)S(1)} %cholesky.118), custom_call_target="Cholesky" | custom-call | tf_op jit(solution)/shard_map/jit(cholesky)/cholesky | solution.py:123
  440.6 9.8 %custom-call.14 = f32[1,128,128]{1,2,0:T(8,128)S(1)} custom-call(f32[1,128,128]{2,1,0:T(8,128)S(1)} %get-tuple-element.35), custom_call_target="InvertDiagBlocksLowerTriangular" | custom-call | tf_op jit(solution)/shard_map/jit(cholesky)/cholesky | solution.py:123
  450.9 11.7 %cholesky.105 = f32[128,128]{1,0:T(8,128)S(1)} custom-call(f32[128,128]{1,0:T(8,128)S(1)} %convolution_subtract_fusion.2), custom_call_target="Cholesky" | custom-call | tf_op jit(solution)/shard_map/jit(cholesky)/cholesky | solution.py:123
  465.3 4.0 while.1
  466.0 1.3 bitcast_dynamic-update-slice_fusion.2
  468.0 1.3 bitcast_dynamic-update-slice_fusion.2
  469.3 19.7 %custom-call.15 = f32[2,128,128]{1,2,0:T(8,128)S(1)} custom-call(f32[2,128,128]{2,1,0:T(8,128)S(1)} %get-tuple-element.9), custom_call_target="InvertDiagBlocksLowerTriangular" | custom-call | tf_op jit(solution)/shard_map/triangular_solve | solution.py:125
  490.1 1.7 fusion.8
  492.4 15.1 %all-gather.12.cloned.1.call-done = f32[4096,512]{1,0:T(8,128)} async-done(((f32[256,512]{1,0:T(8,128)}), f32[4096,512]{1,0:T(8,128)}) %all-gather.12.cloned.1.call-update) | async-done | bytes 8388624 | tf_op jit(solution)/shard_map/all_gather | solution.py:48
  507.4 1.7 fusion.6
  (70 shorter events, 14.9 us)
Async XLA Ops:
  7.2 3.4 copy-start
  7.2 39.0 %copy-start.5 = (f32[128]{0:T(128)S(1)}, f32[128]{0:T(128)}, u32[]{:S(2)}) copy-start(f32[128]{0:T(128)} %param.12) | copy-start | bytes 1540
  7.2 212.4 %reduce-scatter.2.cloned.1.call-start = ((), (), s32[]{:S(2)}) async-start(), calls=%async_computation.2 | async-start | bytes 17825792 | tf_op jit(solution)/shard_map/reduce_scatter | solution.py:90
  52.1 1.9 copy-start.1
  62.1 199.8 %copy-start.3 = (f32[512,512]{1,0:T(8,128)S(1)}, f32[512,512]{1,0:T(8,128)}, u32[]{:S(2)}) copy-start(f32[512,512]{1,0:T(8,128)} %param.13) | copy-start | bytes 3145732
  62.1 302.3 %all-gather.10.cloned.1.call-start = ((), (), s32[]{:S(2)}) async-start(), calls=%async_computation.4 | async-start | bytes 8912896 | tf_op jit(solution)/shard_map/all_gather | solution.py:48
  263.4 123.1 %copy-start.6 = (f32[512]{0:T(512)S(1)}, f32[512]{0:T(512)}, u32[]{:S(2)}) copy-start(f32[512]{0:T(512)} %param.14) | copy-start | bytes 6148
  264.3 162.5 %all-gather.8.cloned.1.call-start = ((), (), s32[]{:S(2)}) async-start(), calls=%async_computation.3 | async-start | bytes 4456448 | tf_op jit(solution)/shard_map/all_gather | solution.py:48
  366.1 141.3 %all-gather.12.cloned.1.call-start = ((), (), s32[]{:S(2)}) async-start(), calls=%async_computation.5 | async-start | bytes 8912896 | tf_op jit(solution)/shard_map/all_gather | solution.py:48
  371.2 14.6 %all-to-all-start = ((f32[16,1,512]{2,1,0:T(1,128)}), f32[16,1,512]{2,1,0:T(1,128)S(1)}, u32[]{:S(2)}, u32[]{:S(2)}) async-start(f32[16,1,512]{2,1,0:T(1,128)} %all_to_all.6), calls=%async_computation.1 | async-start | bytes 65536 | tf_op jit(solution)/shard_map/all_to_all | solution.py:43
  510.5 0.6 copy-start.4
  511.1 1.0 copy-start.2
Sparse Core Ops, SparseCore 0:
  62.2 157.3 reduce-scatter.1
  264.4 100.0 all-gather.9
  367.2 59.5 all-gather.7
  429.9 77.4 all-gather.11
where the time goes:
time: 519 us
  waiting for transfers between devices  299 us (58%)
  blocking collectives  90.9 us (18%)
  other arithmetic  65.6 us (13%)
  matrix products  23.8 us (5%)
  between operations  17.4 us (3%)
  local copies, waits for them, and re-layouts  14.6 us (3%)
  starting transfers between devices  7.43 us (1%)
    reduce_scatter x1, waiting for transfers between devices, local(): lax.psum_scatter(lax.dot_general(features, feat_cols, (((1,), (1,)), ((),...  157 us
    all_gather x3, waiting for transfers between devices, picked(): lax.all_gather(value, axis)  135 us
    psum x5, blocking collectives, over_axes(): value = lax.psum(value, axis)  39.5 us
    another operation x7, other arithmetic, local(): factor = jnp.linalg.cholesky(got_block)  34.6 us
    all_gather x1, blocking collectives, side_by_side(): lax.all_gather(both, axis, axis=dim, tiled=True)  30.8 us
    all_gather x1, blocking collectives, picked(): lax.all_gather(value, axis)  20.6 us
    another operation x3, other arithmetic, local(): lax.linalg.triangular_solve(factor, identity, left_side=True, lower=True)  19.7 us
  transfers between devices with their start and end apart: 5, of which 5 were waited for; matrix products, arithmetic and copies ran while one was open for 13% of the time, Pallas kernels for 0%

commit v1 on v0

v1 whole, which is shorter than its diff:
```python
import functools
import math

import jax
import jax.numpy as jnp
from jax import lax
from jax.experimental import pallas as pl
from jax.experimental.pallas import tpu as pltpu
from jax.sharding import Mesh
from jax.sharding import PartitionSpec as P

M = 8192
F = 128
PB = 256
TILE = 512
B_TOTAL = 4096
HALF = 2048
CHUNK = 512
ROW = ("yh", "x", "core")
COL = ("yl", "z")
XY = ("yh", "x", "yl")
ALL = ROW + COL
RATE = 0.5
EPSILON = 1e-05
LOG2E = math.log2(math.e)
F32 = jnp.float32
BF16 = jnp.bfloat16
NT = (((1,), (1,)), ((), ()))
HIGHEST = lax.Precision.HIGHEST


def swapped(value, axis, size, bit):
    return lax.ppermute(value, axis, [(i, i ^ bit) for i in range(size)])


def split2(value):
    high = lax.reduce_precision(value, 8, 7)
    return high.astype(BF16), (value - high).astype(BF16)


def split3(value):
    high = lax.reduce_precision(value, 8, 7)
    rest = value - high
    mid = lax.reduce_precision(rest, 8, 7)
    return high.astype(BF16), mid.astype(BF16), (rest - mid).astype(BF16)


def packed(value):
    high, low = split2(value)
    return jnp.concatenate([high[..., :128], high[..., 128:], low[..., :128], low[..., 128:]], axis=-2)


def unpacked(rows):
    n = rows.shape[-2] // 4
    q = rows.astype(F32)
    left = q[..., :n, :] + q[..., 2 * n : 3 * n, :]
    right = q[..., n : 2 * n, :] + q[..., 3 * n :, :]
    return jnp.concatenate([left, right], axis=-1)


def joined_along(value, axis, size, bit, at):
    other = swapped(value, axis, size, bit)
    mine_first = (lax.axis_index(axis) // bit) % 2 == 0
    first = jnp.where(mine_first, value, other)
    second = jnp.where(mine_first, other, value)
    return jnp.stack([first, second], axis=at)


def rows_in_order(chunks):
    return chunks.reshape(8, 2, 32, PB).transpose(1, 0, 2, 3).reshape(TILE, PB)


def own_trace(inducing, weights, samples):
    sample_f = samples.astype(F32)
    point_sq = lax.dot_general(weights[None, :], inducing * inducing, NT, precision=HIGHEST)
    sample_sq = jnp.sum(sample_f * sample_f * weights, axis=1)
    cross = lax.dot_general(sample_f * weights, inducing, NT, precision=HIGHEST)
    feat = jnp.exp(-0.5 * (point_sq + sample_sq[:, None] - 2.0 * cross))
    feat = lax.reduce_precision(feat, 8, 7)
    return jnp.sum(feat * feat)


def pieces(value):
    high = value.astype(BF16)
    rest = value - high.astype(F32)
    mid = rest.astype(BF16)
    return high, mid, (rest - mid.astype(F32)).astype(BF16)


def gram_kernel(first, idx_ref, pr_ref, pc_ref, pp_ref, w_ref, x_ref, y_ref, *refs):
    if first:
        grc_ref, gp_ref, fit_ref, paug, xaug = refs
    else:
        grc_in, gp_in, fit_in, grc_ref, gp_ref, fit_ref, paug, xaug = refs
    step = pl.program_id(0)
    lane = lax.broadcasted_iota(jnp.int32, (1, 128), 1)

    @pl.when(step == 0)
    def _():
        w = w_ref[...]
        at = 0
        for ref in (pr_ref, pc_ref, pp_ref):
            pts = ref[...]
            n = pts.shape[0]
            p1, p2, p3 = pieces(pts * w * LOG2E)
            sq = jnp.sum(pts * pts * w, axis=1, keepdims=True) * (-0.5 * LOG2E)
            s1, s2, s3 = (s.astype(F32) for s in pieces(sq))
            extra = jnp.where(lane == 0, s1, jnp.where(lane == 1, s2, jnp.where(lane == 2, s3, 0.0)))
            extra = extra + jnp.where((lane >= 3) & (lane < 6), 1.0, 0.0)
            paug[at : at + n, 0:128] = p1
            paug[at : at + n, 128:256] = p2
            paug[at : at + n, 256:384] = p3
            paug[at : at + n, 384:512] = extra.astype(BF16)
            at += n
        if first:
            grc_ref[...] = jnp.zeros_like(grc_ref)
            gp_ref[...] = jnp.zeros_like(gp_ref)
            fit_ref[...] = jnp.zeros_like(fit_ref)
        else:
            grc_ref[...] = grc_in[...]
            gp_ref[...] = gp_in[...]
            fit_ref[...] = fit_in[...]

    x = x_ref[...]
    xf = x.astype(F32)
    sq = jnp.sum(xf * xf * w_ref[...], axis=1, keepdims=True) * (-0.5 * LOG2E)
    s1, s2, s3 = (s.astype(F32) for s in pieces(sq))
    extra = jnp.where(lane == 3, s1, jnp.where(lane == 4, s2, jnp.where(lane == 5, s3, 0.0)))
    extra = extra + jnp.where(lane < 3, 1.0, 0.0)
    xaug[:, 0:128] = x
    xaug[:, 128:256] = x
    xaug[:, 256:384] = x
    xaug[:, 384:512] = extra.astype(BF16)
    xa = xaug[...]

    def feats(at, n):
        e = lax.dot_general(paug[at : at + n, :], xa, NT, preferred_element_type=F32)
        return jnp.exp2(e).astype(BF16)

    f_r = feats(0, TILE)
    f_c = feats(TILE, TILE)
    f_p = feats(2 * TILE, PB)
    grc_ref[...] += lax.dot_general(f_r, f_c, NT, preferred_element_type=F32)
    gp_ref[0:TILE, :] += lax.dot_general(f_r, f_p, NT, preferred_element_type=F32)
    gp_ref[TILE : 2 * TILE, :] += lax.dot_general(f_c, f_p, NT, preferred_element_type=F32)
    gp_ref[2 * TILE :, :] += lax.dot_general(f_p, f_p, NT, preferred_element_type=F32)
    y = y_ref[...].reshape(CHUNK // 128, 128).astype(F32)
    for at, f in ((0, f_r), (TILE, f_p)):
        acc = fit_ref[at : at + f.shape[0], :]
        for k in range(CHUNK // 128):
            acc = acc + f[:, 128 * k : 128 * (k + 1)].astype(F32) * y[k : k + 1, :]
        fit_ref[at : at + f.shape[0], :] = acc


def gram_part(idx, inducing, weights, x, y, carry):
    first = carry is None
    whole = lambda shape: pl.BlockSpec(shape, lambda i, idx: (0,) * len(shape))
    shapes = ((TILE, TILE), (2 * TILE + PB, PB), (TILE + PB, 128))
    in_specs = [
        pl.BlockSpec((TILE, F), lambda i, idx: (idx[0], 0)),
        pl.BlockSpec((TILE, F), lambda i, idx: (idx[1], 0)),
        pl.BlockSpec((PB, F), lambda i, idx: (idx[2], 0)),
        whole((1, F)),
        pl.BlockSpec((CHUNK, F), lambda i, idx: (i, 0)),
        pl.BlockSpec((1, CHUNK // 128, 128), lambda i, idx: (i, 0, 0)),
    ]
    args = [idx, inducing, inducing, inducing, weights[None, :], x, y.reshape(-1, CHUNK // 128, 128)]
    if not first:
        in_specs += [whole(s) for s in shapes]
        args += list(carry)
    return pl.pallas_call(
        functools.partial(gram_kernel, first),
        grid_spec=pltpu.PrefetchScalarGridSpec(
            num_scalar_prefetch=1,
            grid=(x.shape[0] // CHUNK,),
            in_specs=in_specs,
            out_specs=[whole(s) for s in shapes],
            scratch_shapes=[pltpu.VMEM((2 * TILE + PB, 512), BF16), pltpu.VMEM((CHUNK, 512), BF16)],
        ),
        out_shape=[jax.ShapeDtypeStruct(s, F32) for s in shapes],
        compiler_params=pltpu.CompilerParams(vmem_limit_bytes=48 * 1024 * 1024),
        name="gram_part",
    )(*args)


def factor_kernel(scale_ref, prec_ref, gram_ref, low_ref, inv_ref, work):
    row_id = lax.broadcasted_iota(jnp.int32, (PB, PB), 0)
    col_id = lax.broadcasted_iota(jnp.int32, (PB, PB), 1)
    work[:, 0:PB] = RATE * prec_ref[...] + scale_ref[0] * gram_ref[...]
    work[:, PB:] = jnp.where(row_id == col_id, 1.0, 0.0)
    sub = lax.broadcasted_iota(jnp.int32, (8, 2 * PB), 0)
    lane = lax.broadcasted_iota(jnp.int32, (8, 2 * PB), 1)

    def block(b, _):
        base = pl.multiple_of(8 * b, 8)
        blk = work[pl.ds(base, 8), :]
        for j in range(8):
            at = base + j
            col = jnp.sum(jnp.where(lane == at, blk, 0.0), axis=1, keepdims=True)
            piv = col[j : j + 1, :]
            row = blk[j : j + 1, :] * lax.rsqrt(piv)
            coef = col * lax.rsqrt(piv)
            blk = jnp.where(sub == j, row, jnp.where(sub > j, blk - coef * row, blk))
        work[pl.ds(base, 8), :] = blk
        cols = blk[:, 0:PB].T

        trail = work[...]
        for j in range(8):
            trail = trail - jnp.where(row_id[:, 0:1] >= base + 8, cols[:, j : j + 1], 0.0) * blk[j : j + 1, :]
        work[...] = trail
        return 0

    lax.fori_loop(0, PB // 8, block, 0)
    low_ref[...] = jnp.where(row_id >= col_id, work[:, 0:PB].T, 0.0)
    inv_ref[...] = jnp.where(row_id >= col_id, work[:, PB:], 0.0)


def factored(scale, prec_block, gram_block):
    shape = jax.ShapeDtypeStruct((PB, PB), F32)
    vmem = pl.BlockSpec(memory_space=pltpu.VMEM)
    return pl.pallas_call(
        factor_kernel,
        in_specs=[pl.BlockSpec(memory_space=pltpu.SMEM), vmem, vmem],
        out_specs=[vmem, vmem],
        out_shape=[shape, shape],
        scratch_shapes=[pltpu.VMEM((PB, 2 * PB), F32)],
        name="factored",
    )(scale.reshape(1), prec_block, gram_block)


def local(pool, targets, picks, inducing, inv_sq_lengths, prec_old, mean_old, panel):
    my_row = lax.axis_index(ROW)
    my_col = lax.axis_index(COL)
    my_z = lax.axis_index("z")
    my_core = lax.axis_index("core")
    my_yl = lax.axis_index("yl")
    start = panel[0] * PB
    owner = start // TILE
    offset = start - owner * TILE
    half = offset // PB
    o_yh, o_x, o_core = owner // 8, (owner // 2) % 4, owner % 2
    o_yl, o_z = owner // 8, owner % 8
    o_xy = (o_yh * 4 + o_x) * 2 + o_yl
    zero = jnp.zeros((), jnp.int32)

    samples = jnp.take(pool, picks, axis=0, mode="clip")
    lanes = jnp.arange(128, dtype=jnp.int32)
    own_y = jnp.take(targets, jnp.tile(picks, 8), mode="clip")
    y_row = jnp.where(lanes // 16 == my_z, own_y, jnp.zeros((), BF16))
    columns = lax.dynamic_slice(prec_old, (zero, offset), (TILE, PB))
    chunks = packed(columns.reshape(2, 8, 32, PB).transpose(1, 0, 2, 3).reshape(8, 64, PB))
    common = jnp.concatenate([samples, jnp.pad(y_row[None, :], ((0, 15), (0, 0)))], axis=0)
    z_out = jnp.concatenate([chunks, jnp.broadcast_to(common[None], (8, 32, 128))], axis=1)
    z_in = lax.all_to_all(z_out, "z", 0, 0, tiled=True)
    chunk_q = lax.dynamic_index_in_dim(z_in[:, :256], o_z, 0, keepdims=False)
    z_samples = z_in[:, 256:272].reshape(128, 128)
    z_y = jnp.sum(z_in[:, 272].astype(F32), axis=0).astype(BF16)

    chunk = unpacked(chunk_q)
    chunk = jnp.where(my_yl == o_yl, chunk, swapped(chunk, "yl", 2, 1))

    trace_own = own_trace(inducing, inv_sq_lengths, samples)
    mean_part = lax.dynamic_slice(mean_old, (offset,), (PB,)).reshape(2, 128)
    m_high, m_low = split2(mean_part)
    t_row = jnp.where(lanes == 0, split3(trace_own)[0], jnp.where(lanes == 1, split3(trace_own)[1], jnp.where(lanes == 2, split3(trace_own)[2], jnp.zeros((), BF16))))
    aux = jnp.concatenate([z_y[None], m_high, m_low, t_row[None], jnp.zeros((10, 128), BF16)], axis=0)
    diag_q = lax.dynamic_slice(chunk_q.reshape(4, 2, 32, 128), (zero, half, zero, zero), (4, 1, 32, 128))
    xy_out = jnp.concatenate([z_samples, aux, diag_q.reshape(128, 128)], axis=0)
    xy_in = lax.all_to_all(jnp.broadcast_to(xy_out[None], (16, 272, 128)), XY, 0, 0, tiled=True)
    own_x = xy_in[:, :128].reshape(HALF, 128)
    own_yy = xy_in[:, 128]
    chosen = lax.dynamic_index_in_dim(xy_in, o_xy, 0, keepdims=False)
    diag_mine = chosen[144:272]
    mean_mine = chosen[129:133]
    trace_xy = jnp.sum(xy_in[:, 133, 0:3].astype(F32))

    t1, t2, t3 = split3(trace_xy)
    t_row = jnp.where(lanes == 0, t1, jnp.where(lanes == 1, t2, jnp.where(lanes == 2, t3, jnp.zeros((), BF16))))
    core_out = jnp.concatenate(
        [own_x, own_yy, diag_mine, mean_mine, t_row[None], jnp.zeros((11, 128), BF16)], axis=0
    )
    core_in = swapped(core_out, "core", 2, 1)
    is_owner_core = my_core == o_core
    other_x = core_in[:HALF]
    other_yy = core_in[HALF : HALF + 16]
    tail = jnp.where(is_owner_core, core_out[HALF + 16 :], core_in[HALF + 16 :])
    diag_piece = unpacked(tail[:128])
    mean_panel = (tail[128:130].astype(F32) + tail[130:132].astype(F32)).reshape(PB)
    trace_chip = trace_xy + jnp.sum(core_in[HALF + 16 + 132, 0:3].astype(F32))

    mine = jnp.concatenate([diag_piece, jnp.full((8, PB), trace_chip, F32)], axis=0)
    for k, bit in enumerate((4, 2, 1)):
        mine = joined_along(mine, "z", 8, bit, k)
    mine = mine.reshape(8, 40, PB)
    prec_block = mine[:, :32].reshape(PB, PB)
    trace_scale = jnp.sum(mine[:, 32, 0]) / M

    crossed = lax.ppermute(chunk, ALL, [(16 * i + j, 16 * j + i) for i in range(16) for j in range(16)])
    got_r = chunk
    for k, bit in enumerate((1, 2, 4)):
        got_r = joined_along(got_r, "z", 8, bit, 0)
    got_r = rows_in_order(got_r.reshape(8, 64, PB))
    got_c = joined_along(crossed, "x", 4, 2, 0)
    got_c = joined_along(got_c, "x", 4, 1, 1)
    got_c = joined_along(got_c, "core", 2, 1, 2)
    got_c = rows_in_order(got_c.reshape(8, 64, PB))

    idx = jnp.stack([my_row, my_col, panel[0]]).astype(jnp.int32)
    carry = gram_part(idx, inducing, inv_sq_lengths, own_x, own_yy, None)
    gram, gram_p, fit = gram_part(idx, inducing, inv_sq_lengths, other_x, other_yy, carry)
    fit = jnp.sum(fit, axis=1)
    all_y = jnp.concatenate([own_yy, other_yy], axis=0).astype(F32)
    power_sum = jnp.sum(all_y * all_y)

    scale = RATE / trace_scale
    mean_scale = RATE / jnp.sqrt(trace_scale * (power_sum / B_TOTAL + EPSILON))
    factor, inv_factor = factored(scale, prec_block, gram_p[2 * TILE :])
    joined = RATE * prec_old + scale * gram
    joined_r = RATE * got_r + scale * gram_p[:TILE]
    joined_c = RATE * got_c + scale * gram_p[TILE : 2 * TILE]
    mean_mid = RATE * mean_old + mean_scale * fit[:TILE]
    mean_p = RATE * mean_panel + mean_scale * fit[TILE:]
    wide_r = lax.dot_general(joined_r, inv_factor, NT, precision=HIGHEST)
    wide_ct = lax.dot_general(inv_factor, joined_c, NT, precision=HIGHEST)
    head = jnp.sum(inv_factor * mean_p[None, :], axis=1)
    updated = joined - jnp.dot(wide_r, wide_ct, precision=HIGHEST)
    in_col = my_col == owner
    in_row = my_row == owner
    updated = jnp.where(in_col, lax.dynamic_update_slice(updated, wide_r, (zero, offset)), updated)
    updated = jnp.where(in_row, lax.dynamic_update_slice(updated, wide_ct, (offset, zero)), updated)
    updated = jnp.where(
        jnp.logical_and(in_row, in_col), lax.dynamic_update_slice(updated, factor, (offset, offset)), updated
    )
    mean_next = mean_mid - jnp.sum(wide_r * head[None, :], axis=1)
    mean_next = jnp.where(in_row, lax.dynamic_update_slice(mean_next, head, (offset,)), mean_next)
    return (updated, mean_next)


def solution(mesh):
    split = Mesh(mesh.devices.reshape(2, 4, 2, 2, 8), ALL)
    return jax.shard_map(
        local,
        mesh=split,
        in_specs=(P(ALL, None), P(ALL), P(ALL), P(), P(), P(ROW, COL), P(ROW), P()),
        out_specs=(P(ROW, COL), P(ROW)),
        check_vma=False,
    )
```

time: 519 us -> 173 us (0.33)
  the two profiles are of different devices: /device:TPU:1 before, /device:TPU:44 now
where the time goes in v1:
time: 173 us; the launch traced here: 172 us
  Pallas kernels  57 us (33%)
  starting transfers between devices  36.4 us (21%)
  waiting for transfers between devices  28.1 us (16%)
  between operations  14.8 us (9%)
  local copies, waits for them, and re-layouts  14 us (8%)
  matrix products  13.4 us (8%)
  other arithmetic  8.78 us (5%)
    pallas_call x1, Pallas kernels, factored(): pl.pallas_call(factor_kernel, in_specs=[pl.BlockSpec(memory_space=pltpu.S...  39.6 us
    ppermute x11, waiting for transfers between devices, swapped(): return lax.ppermute(value, axis, [(i, i ^ bit) for i in range(size)])  21.2 us
    pallas_call x2, Pallas kernels, gram_part(): pl.pallas_call(functools.partial(gram_kernel, first), grid_spec=pltpu.Pre...  17.4 us
    ppermute x11, starting transfers between devices, swapped(): return lax.ppermute(value, axis, [(i, i ^ bit) for i in range(size)])  16.2 us
    all_to_all x1, starting transfers between devices, local(): z_in = lax.all_to_all(z_out, 'z', 0, 0, tiled=True)  8.57 us
    all_to_all x1, starting transfers between devices, local(): lax.all_to_all(jnp.broadcast_to(xy_out[None], (16, 272, 128)), XY, 0, 0,...  8.17 us
    dot_general x1, matrix products, own_trace(): lax.dot_general(weights[None, :], inducing * inducing, NT, precision=HIGH...  6.02 us
    ppermute x1, waiting for transfers between devices, local(): lax.ppermute(chunk, ALL, [(16 * i + j, 16 * j + i) for i in range(16) for...  4.99 us
  transfers between devices with their start and end apart: 14, of which 5 were waited for; matrix products, arithmetic and copies ran while one was open for 11% of the time, Pallas kernels for 10%

profile of v1, /device:TPU:44, one launch (start us, length us, event | category | flops | bytes accessed | tf_op | source)
XLA Modules:
  0.0 172.5 jit_solution(6520799498619280237)
XLA Ops:
  1.4 1.1 constant_dynamic-slice_fusion.3
  5.4 1.2 gather_fusion.1
  7.9 8.6 %all-to-all-start = ((bf16[8,288,128]{2,1,0:T(8,128)(2,1)}), bf16[8,288,128]{2,1,0:T(8,128)(2,1)S(1)}, u32[]{:S(2)}, u32[]{:S(2)}) async-start(bf16[8,288,128]{2,1,0:T(8,128)(2,1)} %broadcast_dynamic-update-slice_fusion), calls=%async_computation | async-start | bytes 1179648 | tf_op jit(solution)/shard_map/all_to_all | solution.py:254
  16.6 6.0 %fusion.5 = f32[1,8192]{1,0:T(1,128)S(1)} fusion(f32[8192,128]{1,0:T(8,128)} %pp_ref.3, f32[128]{0:T(128)S(1)} %copy-done.1), kind=kOutput, calls=%fused_computation.8 | convolution fusion | flops 13631488 | bytes 4227584 | tf_op jit(solution)/shard_map/dot_general | solution.py:75
  22.6 4.1 %fusion.7 = f32[]{:T(128)} fusion(f32[8192,128]{1,0:T(8,128)S(1)} %copy-done.3, f32[16]{0:T(128)S(1)} %fusion.13, f32[8192]{0:T(1024)S(1)} %bitcast.112, bf16[16,128]{1,0:T(8,128)(2,1)S(1)} %gather_fusion, f32[128]{0:T(128)S(1)} %copy-done.1), kind=kOutput, calls=%fused_computation.13 | convolution fusion | flops 202248192 | bytes 4231748 | tf_op jit(solution)/shard_map/dot_general | solution.py:77
  32.0 1.9 %all-to-all-done = bf16[8,288,128]{2,1,0:T(8,128)(2,1)S(1)} async-done(((bf16[8,288,128]{2,1,0:T(8,128)(2,1)}), bf16[8,288,128]{2,1,0:T(8,128)(2,1)S(1)}, u32[]{:S(2)}, u32[]{:S(2)}) %all-to-all-start) | async-done | bytes 589856 | tf_op jit(solution)/shard_map/all_to_all | solution.py:254
  34.8 1.2 broadcast_in_dim.79
  35.9 8.2 %all-to-all-start.1 = ((bf16[16,272,128]{2,1,0:T(8,128)(2,1)}), bf16[16,272,128]{2,1,0:T(8,128)(2,1)S(1)}, u32[]{:S(2)}, u32[]{:S(2)}) async-start(bf16[16,272,128]{2,1,0:T(8,128)(2,1)} %broadcast_in_dim.79), calls=%async_computation.1 | async-start | bytes 2228224 | tf_op jit(solution)/shard_map/all_to_all | solution.py:269
  44.1 3.4 %collective-permute-start.8 = (f32[64,256]{1,0:T(8,128)S(1)}, f32[64,256]{1,0:T(8,128)S(1)}, u32[]{:S(2)}, u32[]{:S(2)}) collective-permute-start(f32[64,256]{1,0:T(8,128)S(1)} %broadcast_select_fusion), channel_id=1, source_target_pairs={{0,0},{1,16},{2,32},{3,48},{4,64},{5,80},{6,96},{7,112},{8,128},{9... | collective-permute-start | bytes 196616 | tf_op jit(solution)/shard_map/ppermute | solution.py:298
  47.6 3.5 %collective-permute-start.5 = (f32[64,256]{1,0:T(8,128)S(1)}, f32[64,256]{1,0:T(8,128)S(1)}, u32[]{:S(2)}, u32[]{:S(2)}) collective-permute-start(f32[64,256]{1,0:T(8,128)S(1)} %broadcast_select_fusion), channel_id=1, source_target_pairs={{0,1},{1,0},{2,3},{3,2},{4,5},{5,4},{6,7},{7,6},{8,9},{9,8},{10,11... | collective-permute-start | bytes 196616 | tf_op jit(solution)/shard_map/ppermute | solution.py:33
  51.1 5.0 %collective-permute-done.8 = f32[64,256]{1,0:T(8,128)S(1)} collective-permute-done((f32[64,256]{1,0:T(8,128)S(1)}, f32[64,256]{1,0:T(8,128)S(1)}, u32[]{:S(2)}, u32[]{:S(2)}) %collective-permute-start.8) | collective-permute-done | bytes 65568 | tf_op jit(solution)/shard_map/ppermute | solution.py:298
  56.5 5.8 %collective-permute-done.9 = f32[64,256]{1,0:T(8,128)S(1)} collective-permute-done((f32[64,256]{1,0:T(8,128)S(1)}, f32[64,256]{1,0:T(8,128)S(1)}, u32[]{:S(2)}, u32[]{:S(2)}) %collective-permute-start.9) | collective-permute-done | bytes 65568 | tf_op jit(solution)/shard_map/ppermute | solution.py:33
  62.3 2.0 %collective-permute-start.10 = (f32[2,64,256]{2,1,0:T(8,128)S(1)}, f32[2,64,256]{2,1,0:T(8,128)S(1)}, u32[]{:S(2)}, u32[]{:S(2)}) collective-permute-start(f32[2,64,256]{2,1,0:T(8,128)S(1)} %pad_maximum_fusion.5), channel_id=1, source_target_pairs={{0,32},{32,0},{64,96},{96,64},{1,33},{33,1},{65,97},{97,65},{2,34}... | collective-permute-start | bytes 393224 | tf_op jit(solution)/shard_map/ppermute | solution.py:33
  70.9 1.9 %collective-permute-start.7 = (f32[2,2,64,256]{3,2,0,1:T(8,128)S(1)}, f32[2,2,64,256]{3,2,0,1:T(8,128)}, u32[]{:S(2)}, u32[]{:S(2)}) collective-permute-start(f32[2,2,64,256]{3,2,0,1:T(8,128)S(1)} %pad_maximum_fusion.1), channel_id=1, source_target_pairs={{0,4},{1,5},{2,6},{3,7},{4,0},{5,1},{6,2},{7,3},{8,12},{9,13},{10,... | collective-permute-start | bytes 786440 | tf_op jit(solution)/shard_map/ppermute | solution.py:33
  74.9 4.4 %collective-permute-start.1 = (f32[40,256]{1,0:T(8,128)S(1)}, f32[40,256]{1,0:T(8,128)S(1)}, u32[]{:S(2)}, u32[]{:S(2)}) collective-permute-start(f32[40,256]{1,0:T(8,128)S(1)} %select_maximum_fusion), channel_id=1, source_target_pairs={{0,4},{1,5},{2,6},{3,7},{4,0},{5,1},{6,2},{7,3},{8,12},{9,13},{10,... | collective-permute-start | bytes 122888 | tf_op jit(solution)/shard_map/ppermute | solution.py:33
  79.3 11.0 %collective-permute-done.7 = f32[2,2,64,256]{3,2,0,1:T(8,128)} collective-permute-done((f32[2,2,64,256]{3,2,0,1:T(8,128)S(1)}, f32[2,2,64,256]{3,2,0,1:T(8,128)}, u32[]{:S(2)}, u32[]{:S(2)}) %collective-permute-start.7) | collective-permute-done | bytes 262176 | tf_op jit(solution)/shard_map/ppermute | solution.py:33
  90.3 1.0 select_bitcast_fusion.3
  91.6 0.8 copy.38
  92.4 4.4 %collective-permute-done.2 = f32[2,40,256]{2,1,0:T(8,128)S(1)} collective-permute-done((f32[2,40,256]{2,1,0:T(8,128)S(1)}, f32[2,40,256]{2,1,0:T(8,128)S(1)}, u32[]{:S(2)}, u32[]{:S(2)}) %collective-permute-start.2) | collective-permute-done | bytes 81952 | tf_op jit(solution)/shard_map/ppermute | solution.py:33
  96.9 3.0 %collective-permute-start.3 = (f32[2,2,40,256]{3,2,0,1:T(8,128)S(1)}, f32[2,2,40,256]{3,2,0,1:T(8,128)}, u32[]{:S(2)}, u32[]{:S(2)}) collective-permute-start(f32[2,2,40,256]{3,2,0,1:T(8,128)S(1)} %pad_maximum_fusion.3), channel_id=1, source_target_pairs={{0,1},{1,0},{2,3},{3,2},{4,5},{5,4},{6,7},{7,6},{8,9},{9,8},{10,11... | collective-permute-start | bytes 491528 | tf_op jit(solution)/shard_map/ppermute | solution.py:33
  100.0 0.8 copy.40
  100.9 8.7 %gram_part.2 = (f32[512,512]{1,0:T(8,128)S(1)}, f32[1280,256]{1,0:T(8,128)S(1)}, f32[768,128]{1,0:T(8,128)S(1)}) custom-call(s32[3]{0:T(128)S(1)} %pad_add_fusion.idx_ref, f32[8192,128]{1,0:T(8,128)} %pp_ref.3, f32[8192,128]{1,0:T(8,128)} %pp_ref.3, f32[8192,128]{1,0:T(8,128)} %pp_ref.3, f32[1,128]{1,0:T(1,128)S(1)} %bitcast.103, ...), custom_call_target="tpu_custom_call" | custom-call | tf_op jit(solution)/shard_map/gram_part/pallas_call | solution.py:171
  109.7 8.7 %gram_part.3 = (f32[512,512]{1,0:T(8,128)S(1)}, f32[1280,256]{1,0:T(8,128)S(1)}, f32[768,128]{1,0:T(8,128)S(1)}) custom-call(s32[3]{0:T(128)S(1)} %pad_add_fusion.idx_ref, f32[8192,128]{1,0:T(8,128)} %pp_ref.3, f32[8192,128]{1,0:T(8,128)} %pp_ref.3, f32[8192,128]{1,0:T(8,128)} %pp_ref.3, f32[1,128]{1,0:T(1,128)S(1)} %bitcast.104, ...), custom_call_target="tpu_custom_call" | custom-call | tf_op jit(solution)/shard_map/gram_part/pallas_call | solution.py:171
  120.5 0.9 select_bitcast_fusion.5
  122.2 0.7 slice.178
  123.6 39.6 %factored.1 = (f32[256,256]{1,0:T(8,128)}, f32[256,256]{1,0:T(8,128)}) custom-call(f32[1]{0:T(128)} %bitcast.41.scale_ref, f32[256,256]{1,0:T(8,128)} %bitcast.110, f32[256,256]{1,0:T(8,128)} %slice.144.gram_ref), custom_call_target="tpu_custom_call" | custom-call | tf_op jit(solution)/shard_map/factored/pallas_call | solution.py:221
  163.2 1.1 multiply_reduce_fusion.1
  164.4 1.4 bitcast_add_fusion
  165.8 1.6 fusion.22
  168.0 1.0 copy.41
  169.0 1.0 fusion.23
  171.5 1.0 copy-done.4
  (113 shorter events, 12.4 us)
Async XLA Ops:
  0.6 6.0 %copy-start = (bf16[128,128]{1,0:T(8,128)(2,1)S(1)}, bf16[128,128]{1,0:T(8,128)(2,1)}, u32[]{:S(2)}) copy-start(bf16[128,128]{1,0:T(8,128)(2,1)} %param.8) | copy-start | bytes 98308
  0.6 4.7 %copy-start.11 = (s32[16]{0:T(128)S(1)}, s32[16]{0:T(128)}, u32[]{:S(2)}) copy-start(s32[16]{0:T(128)} %param.10) | copy-start | bytes 196
  0.7 4.7 %copy-start.2 = (bf16[128]{0:T(256)(128)(2,1)S(1)}, bf16[128]{0:T(256)(128)(2,1)}, u32[]{:S(2)}) copy-start(bf16[128]{0:T(256)(128)(2,1)} %param.9) | copy-start | bytes 772
  0.7 15.8 %copy-start.1 = (f32[128]{0:T(128)S(1)}, f32[128]{0:T(128)}, u32[]{:S(2)}) copy-start(f32[128]{0:T(128)} %param.12) | copy-start | bytes 1540
  7.9 26.0 %all-to-all-start = ((bf16[8,288,128]{2,1,0:T(8,128)(2,1)}), bf16[8,288,128]{2,1,0:T(8,128)(2,1)S(1)}, u32[]{:S(2)}, u32[]{:S(2)}) async-start(bf16[8,288,128]{2,1,0:T(8,128)(2,1)} %broadcast_dynamic-update-slice_fusion), calls=%async_computation | async-start | bytes 1179648 | tf_op jit(solution)/shard_map/all_to_all | solution.py:254
  16.5 6.1 %copy-start.3 = (f32[8192,128]{1,0:T(8,128)S(1)}, f32[8192,128]{1,0:T(8,128)}, u32[]{:S(2)}) copy-start(f32[8192,128]{1,0:T(8,128)} %pp_ref.3) | copy-start | bytes 12582916
  16.6 15.3 %copy-start.9 = (f32[512]{0:T(512)S(1)}, f32[512]{0:T(512)}, u32[]{:S(2)}) copy-start(f32[512]{0:T(512)} %param.14) | copy-start | bytes 6148
  34.0 10.1 %collective-permute-start.4 = (f32[64,256]{1,0:T(8,128)S(1)}, f32[64,256]{1,0:T(8,128)S(1)}, u32[]{:S(2)}, u32[]{:S(2)}) collective-permute-start(f32[64,256]{1,0:T(8,128)S(1)} %pad_maximum_fusion.7), channel_id=1, source_target_pairs={{0,8},{8,0},{1,9},{9,1},{2,10},{10,2},{3,11},{11,3},{4,12},{12,4},... | collective-permute-start | bytes 196616 | tf_op jit(solution)/shard_map/ppermute | solution.py:33
  35.9 28.4 %all-to-all-start.1 = ((bf16[16,272,128]{2,1,0:T(8,128)(2,1)}), bf16[16,272,128]{2,1,0:T(8,128)(2,1)S(1)}, u32[]{:S(2)}, u32[]{:S(2)}) async-start(bf16[16,272,128]{2,1,0:T(8,128)(2,1)} %broadcast_in_dim.79), calls=%async_computation.1 | async-start | bytes 2228224 | tf_op jit(solution)/shard_map/all_to_all | solution.py:269
  44.1 12.0 %collective-permute-start.8 = (f32[64,256]{1,0:T(8,128)S(1)}, f32[64,256]{1,0:T(8,128)S(1)}, u32[]{:S(2)}, u32[]{:S(2)}) collective-permute-start(f32[64,256]{1,0:T(8,128)S(1)} %broadcast_select_fusion), channel_id=1, source_target_pairs={{0,0},{1,16},{2,32},{3,48},{4,64},{5,80},{6,96},{7,112},{8,128},{9... | collective-permute-start | bytes 196616 | tf_op jit(solution)/shard_map/ppermute | solution.py:298
  47.6 8.6 %collective-permute-start.5 = (f32[64,256]{1,0:T(8,128)S(1)}, f32[64,256]{1,0:T(8,128)S(1)}, u32[]{:S(2)}, u32[]{:S(2)}) collective-permute-start(f32[64,256]{1,0:T(8,128)S(1)} %broadcast_select_fusion), channel_id=1, source_target_pairs={{0,1},{1,0},{2,3},{3,2},{4,5},{5,4},{6,7},{7,6},{8,9},{9,8},{10,11... | collective-permute-start | bytes 196616 | tf_op jit(solution)/shard_map/ppermute | solution.py:33
  56.1 6.1 %collective-permute-start.9 = (f32[64,256]{1,0:T(8,128)S(1)}, f32[64,256]{1,0:T(8,128)S(1)}, u32[]{:S(2)}, u32[]{:S(2)}) collective-permute-start(f32[64,256]{1,0:T(8,128)S(1)} %collective-permute-done.8), channel_id=1, source_target_pairs={{0,64},{32,96},{64,0},{96,32},{1,65},{33,97},{65,1},{97,33},{2,66}... | collective-permute-start | bytes 196616 | tf_op jit(solution)/shard_map/ppermute | solution.py:33
  56.2 14.7 %collective-permute-start.6 = (f32[2,64,256]{2,1,0:T(8,128)S(1)}, f32[2,64,256]{2,1,0:T(8,128)S(1)}, u32[]{:S(2)}, u32[]{:S(2)}) collective-permute-start(f32[2,64,256]{2,1,0:T(8,128)S(1)} %pad_maximum_fusion.4), channel_id=1, source_target_pairs={{0,2},{1,3},{2,0},{3,1},{4,6},{5,7},{6,4},{7,5},{8,10},{9,11},{10,... | collective-permute-start | bytes 393224 | tf_op jit(solution)/shard_map/ppermute | solution.py:33
  62.3 10.5 %collective-permute-start.10 = (f32[2,64,256]{2,1,0:T(8,128)S(1)}, f32[2,64,256]{2,1,0:T(8,128)S(1)}, u32[]{:S(2)}, u32[]{:S(2)}) collective-permute-start(f32[2,64,256]{2,1,0:T(8,128)S(1)} %pad_maximum_fusion.5), channel_id=1, source_target_pairs={{0,32},{32,0},{64,96},{96,64},{1,33},{33,1},{65,97},{97,65},{2,34}... | collective-permute-start | bytes 393224 | tf_op jit(solution)/shard_map/ppermute | solution.py:33
  70.5 2.4 %collective-permute-start = (bf16[2208,128]{1,0:T(8,128)(2,1)S(1)}, bf16[2208,128]{1,0:T(8,128)(2,1)S(1)}, u32[]{:S(2)}, u32[]{:S(2)}) collective-permute-start(bf16[2208,128]{1,0:T(8,128)(2,1)S(1)} %concatenate.31), channel_id=1, source_target_pairs={{0,16},{16,0},{1,17},{17,1},{2,18},{18,2},{3,19},{19,3},{4,20},{20... | collective-permute-start | bytes 1695752 | tf_op jit(solution)/shard_map/ppermute | solution.py:33
  70.9 19.4 %collective-permute-start.7 = (f32[2,2,64,256]{3,2,0,1:T(8,128)S(1)}, f32[2,2,64,256]{3,2,0,1:T(8,128)}, u32[]{:S(2)}, u32[]{:S(2)}) collective-permute-start(f32[2,2,64,256]{3,2,0,1:T(8,128)S(1)} %pad_maximum_fusion.1), channel_id=1, source_target_pairs={{0,4},{1,5},{2,6},{3,7},{4,0},{5,1},{6,2},{7,3},{8,12},{9,13},{10,... | collective-permute-start | bytes 786440 | tf_op jit(solution)/shard_map/ppermute | solution.py:33
  72.8 27.1 %collective-permute-start.11 = (f32[2,2,64,256]{3,2,0,1:T(8,128)S(1)}, f32[2,2,64,256]{3,2,0,1:T(8,128)S(1)}, u32[]{:S(2)}, u32[]{:S(2)}) collective-permute-start(f32[2,2,64,256]{3,2,0,1:T(8,128)S(1)} %pad_maximum_fusion.2), channel_id=1, source_target_pairs={{0,16},{16,0},{1,17},{17,1},{2,18},{18,2},{3,19},{19,3},{4,20},{20... | collective-permute-start | bytes 786440 | tf_op jit(solution)/shard_map/ppermute | solution.py:33
  74.9 16.4 %collective-permute-start.1 = (f32[40,256]{1,0:T(8,128)S(1)}, f32[40,256]{1,0:T(8,128)S(1)}, u32[]{:S(2)}, u32[]{:S(2)}) collective-permute-start(f32[40,256]{1,0:T(8,128)S(1)} %select_maximum_fusion), channel_id=1, source_target_pairs={{0,4},{1,5},{2,6},{3,7},{4,0},{5,1},{6,2},{7,3},{8,12},{9,13},{10,... | collective-permute-start | bytes 122888 | tf_op jit(solution)/shard_map/ppermute | solution.py:33
  91.4 5.4 %collective-permute-start.2 = (f32[2,40,256]{2,1,0:T(8,128)S(1)}, f32[2,40,256]{2,1,0:T(8,128)S(1)}, u32[]{:S(2)}, u32[]{:S(2)}) collective-permute-start(f32[2,40,256]{2,1,0:T(8,128)S(1)} %pad_maximum_fusion.6), channel_id=1, source_target_pairs={{0,2},{1,3},{2,0},{3,1},{4,6},{5,7},{6,4},{7,5},{8,10},{9,11},{10,... | collective-permute-start | bytes 245768 | tf_op jit(solution)/shard_map/ppermute | solution.py:33
  96.9 23.7 %collective-permute-start.3 = (f32[2,2,40,256]{3,2,0,1:T(8,128)S(1)}, f32[2,2,40,256]{3,2,0,1:T(8,128)}, u32[]{:S(2)}, u32[]{:S(2)}) collective-permute-start(f32[2,2,40,256]{3,2,0,1:T(8,128)S(1)} %pad_maximum_fusion.3), channel_id=1, source_target_pairs={{0,1},{1,0},{2,3},{3,2},{4,5},{5,4},{6,7},{7,6},{8,9},{9,8},{10,11... | collective-permute-start | bytes 491528 | tf_op jit(solution)/shard_map/ppermute | solution.py:33
  163.2 4.1 %copy-start.6 = (f32[256,256]{1,0:T(8,128)S(1)}, f32[256,256]{1,0:T(8,128)}, u32[]{:S(2)}) copy-start(f32[256,256]{1,0:T(8,128)} %get-tuple-element.15) | copy-start | bytes 786436
  164.4 5.7 %copy-start.5 = (f32[512,512]{1,0:T(8,128)S(1)}, f32[512,512]{1,0:T(8,128)}, u32[]{:S(2)}) copy-start(f32[512,512]{1,0:T(8,128)} %param.13) | copy-start | bytes 3145732
  169.0 1.4 copy-start.7
  170.1 1.0 copy-start.8
  170.9 0.6 copy-start.10
  171.5 1.0 copy-start.4

commit v2 on v1

v2 whole, which is shorter than its diff:
```python
import functools
import math

import jax
import jax.numpy as jnp
from jax import lax
from jax.experimental import pallas as pl
from jax.experimental.pallas import tpu as pltpu
from jax.sharding import Mesh
from jax.sharding import PartitionSpec as P

M = 8192
F = 128
PB = 256
TILE = 512
B_TOTAL = 4096
HALF = 2048
CHUNK = 512
ROW = ("yh", "x", "core")
COL = ("yl", "z")
XY = ("yh", "x", "yl")
ALL = ROW + COL
RATE = 0.5
EPSILON = 1e-05
LOG2E = math.log2(math.e)
F32 = jnp.float32
BF16 = jnp.bfloat16
NT = (((1,), (1,)), ((), ()))
HIGHEST = lax.Precision.HIGHEST


def swapped(value, axis, size, bit):
    return lax.ppermute(value, axis, [(i, i ^ bit) for i in range(size)])


def split2(value):
    high = lax.reduce_precision(value, 8, 7)
    return high.astype(BF16), (value - high).astype(BF16)


def split3(value):
    high = lax.reduce_precision(value, 8, 7)
    rest = value - high
    mid = lax.reduce_precision(rest, 8, 7)
    return high.astype(BF16), mid.astype(BF16), (rest - mid).astype(BF16)


def pieces(value):
    high = value.astype(BF16)
    rest = value - high.astype(F32)
    mid = rest.astype(BF16)
    return high, mid, (rest - mid.astype(F32)).astype(BF16)


def scaled_points(pts, w):
    scaled = pts * w * LOG2E
    high = scaled.astype(BF16)
    low = (scaled - high.astype(F32)).astype(BF16)
    return high, low, jnp.sum(pts * pts * w, axis=1, keepdims=True) * (-0.5 * LOG2E)


def sample_terms(x, w):
    xf = x.astype(F32)
    return jnp.sum((xf * xf * w).T, axis=0, keepdims=True) * (-0.5 * LOG2E)


def split_rows(out, at, n, value):
    high = value.astype(BF16)
    low = (value - high.astype(F32)).astype(BF16)
    for k, part in enumerate((high[:, :128], high[:, 128:], low[:, :128], low[:, 128:])):
        out[at + k * n : at + (k + 1) * n, :] = part


def pack_kernel(idx_ref, picks_ref, pool_ref, targets_ref, prec_ref, out_ref):
    sub = lax.broadcasted_iota(jnp.int32, (16, 128), 0)
    lane = lax.broadcasted_iota(jnp.int32, (16, 128), 1)
    at = jnp.zeros((16, 128), jnp.int32)
    for n in range(16):
        at = jnp.where(sub == n, picks_ref[n], at)
    hot = jnp.where(at == lane, 1.0, 0.0)
    samples = jnp.dot(hot.astype(BF16), pool_ref[...], preferred_element_type=F32).astype(BF16)
    y = jnp.sum(hot * targets_ref[...].astype(F32), axis=1, keepdims=True)
    y_row = jnp.sum(jnp.where(lane == 16 * idx_ref[1] + sub, y, 0.0), axis=0, keepdims=True)
    y_rows = jnp.where(sub == 0, y_row, 0.0).astype(BF16)
    for j in range(8):
        chunk = jnp.concatenate([prec_ref[32 * j : 32 * j + 32, :], prec_ref[PB + 32 * j : PB + 32 * j + 32, :]], axis=0)
        split_rows(out_ref.at[j], 0, 64, chunk)
        out_ref[j, 256:272, :] = samples
        out_ref[j, 272:288, :] = y_rows


def pack(idx, picks, pool, targets, prec_old):
    return pl.pallas_call(
        pack_kernel,
        grid_spec=pltpu.PrefetchScalarGridSpec(
            num_scalar_prefetch=2,
            grid=(1,),
            in_specs=[
                pl.BlockSpec((128, 128), lambda i, idx, picks: (0, 0)),
                pl.BlockSpec((1, 128), lambda i, idx, picks: (0, 0)),
                pl.BlockSpec((TILE, PB), lambda i, idx, picks: (0, idx[0])),
            ],
            out_specs=pl.BlockSpec((8, 288, 128), lambda i, idx, picks: (0, 0, 0)),
        ),
        out_shape=jax.ShapeDtypeStruct((8, 288, 128), BF16),
        name="pack",
    )(idx, picks, pool, targets[None, :], prec_old)


def trace_kernel(ind_ref, w_ref, x_ref, out_ref, paug, xaug, total):
    step = pl.program_id(0)
    w = w_ref[...]
    x = x_ref[0]

    @pl.when(step == 0)
    def _():
        total[...] = jnp.zeros_like(total)
        xaug[:, 0:128] = x
        xaug[:, 128:256] = x

    high, low, own = scaled_points(ind_ref[...], w)
    paug[:, 0:128] = high
    paug[:, 128:256] = low
    e = lax.dot_general(paug[...], xaug[...], NT, preferred_element_type=F32)
    f = jnp.exp2(e + own + sample_terms(x, w)).astype(BF16).astype(F32)
    total[:, 0:16] += jnp.sum((f * f).reshape(128, 8, 16), axis=0)

    @pl.when(step == pl.num_programs(0) - 1)
    def _():
        sub = lax.broadcasted_iota(jnp.int32, (16, 128), 0)
        h, m, l = (p.astype(F32) for p in pieces(jnp.sum(total[...], axis=0, keepdims=True)))
        out_ref[...] = jnp.where(sub == 0, h, jnp.where(sub == 1, m, jnp.where(sub == 2, l, 0.0))).astype(BF16)


def trace_rows(inducing, weights, packed):
    return pl.pallas_call(
        trace_kernel,
        grid=(M // 1024,),
        in_specs=[
            pl.BlockSpec((1024, F), lambda i: (i, 0)),
            pl.BlockSpec((1, F), lambda i: (0, 0)),
            pl.BlockSpec((1, 16, F), lambda i: (0, 16, 0)),
        ],
        out_specs=pl.BlockSpec((16, 128), lambda i: (0, 0)),
        out_shape=jax.ShapeDtypeStruct((16, 128), BF16),
        scratch_shapes=[pltpu.VMEM((1024, 256), BF16), pltpu.VMEM((16, 256), BF16), pltpu.VMEM((8, 128), F32)],
        cost_estimate=pl.CostEstimate(flops=4_000_000_000, bytes_accessed=4_000_000, transcendentals=1_000_000),
        name="trace_rows",
    )(inducing, weights[None, :], packed)


def relay_kernel(idx_ref, z_ref, t_ref, mean_ref, out_ref, chunk_ref):
    src, half = idx_ref[0], idx_ref[1]
    sub = lax.broadcasted_iota(jnp.int32, (16, 128), 0)
    chunk = z_ref[src, 0:256, :]
    values = chunk.astype(F32)
    chunk_ref[:, 0:128] = values[0:64] + values[128:192]
    chunk_ref[:, 128:256] = values[64:128] + values[192:256]
    y = jnp.sum(z_ref[:, 272:288, :].astype(F32), axis=0)
    means = mean_ref[pl.ds(2 * half, 2), :]
    m_high = means.astype(BF16).astype(F32)
    m_low = means - m_high
    t = t_ref[...].astype(F32)
    aux = jnp.where(sub == 0, y, 0.0)
    for k, row in enumerate((m_high[0:1], m_high[1:2], m_low[0:1], m_low[1:2], t[0:1], t[1:2], t[2:3])):
        aux = jnp.where(sub == k + 1, row, aux)
    aux = aux.astype(BF16)
    for k in range(4):
        @pl.when(half == 0)
        def _():
            out_ref[0, 144 + 32 * k : 176 + 32 * k, :] = chunk[64 * k : 64 * k + 32]

        @pl.when(half == 1)
        def _():
            out_ref[0, 144 + 32 * k : 176 + 32 * k, :] = chunk[64 * k + 32 : 64 * k + 64]

    out_ref[0, 0:128, :] = z_ref[:, 256:272, :].reshape(128, 128)
    out_ref[0, 128:144, :] = aux
    whole = out_ref[0]
    for k in range(1, 16):
        out_ref[k] = whole


def relay(idx, z_in, t_rows, mean_old):
    vmem = pl.BlockSpec(memory_space=pltpu.VMEM)
    return pl.pallas_call(
        relay_kernel,
        in_specs=[pl.BlockSpec(memory_space=pltpu.SMEM), vmem, vmem, vmem],
        out_specs=[vmem, vmem],
        out_shape=[jax.ShapeDtypeStruct((16, 272, 128), BF16), jax.ShapeDtypeStruct((64, PB), F32)],
        name="relay",
    )(idx, z_in, t_rows, mean_old.reshape(4, 128))


def gram_kernel(first, idx_ref, pr_ref, pc_ref, pp_ref, w_ref, x_ref, y_ref, *refs):
    if first:
        grc_ref, gp_ref, fit_ref, paug, own, xaug = refs
    else:
        grc_in, gp_in, fit_in, grc_ref, gp_ref, fit_ref, paug, own, xaug = refs
    step = pl.program_id(0)

    @pl.when(step == 0)
    def _():
        at = 0
        for ref in (pr_ref, pc_ref, pp_ref):
            n = ref.shape[0]
            high, low, term = scaled_points(ref[...], w_ref[...])
            paug[at : at + n, 0:128] = high
            paug[at : at + n, 128:256] = low
            own[at : at + n, :] = jnp.broadcast_to(term, (n, 128))
            at += n
        if first:
            grc_ref[...] = jnp.zeros_like(grc_ref)
            gp_ref[...] = jnp.zeros_like(gp_ref)
            fit_ref[...] = jnp.zeros_like(fit_ref)
        else:
            grc_ref[...] = grc_in[...]
            gp_ref[...] = gp_in[...]
            fit_ref[...] = fit_in[...]

    x = x_ref[...]
    xaug[:, 0:128] = x
    xaug[:, 128:256] = x
    xa = xaug[...]
    sample_term = sample_terms(x, w_ref[...])

    def feats(at, n):
        e = lax.dot_general(paug[at : at + n, :], xa, NT, preferred_element_type=F32)
        term = own[at : at + n, :]
        e = e + jnp.concatenate([term] * (CHUNK // 128), axis=1) + sample_term
        return jnp.exp2(e).astype(BF16)

    f_r = feats(0, TILE)
    f_c = feats(TILE, TILE)
    f_p = feats(2 * TILE, PB)
    grc_ref[...] += lax.dot_general(f_r, f_c, NT, preferred_element_type=F32)
    gp_ref[0:TILE, :] += lax.dot_general(f_r, f_p, NT, preferred_element_type=F32)
    gp_ref[TILE : 2 * TILE, :] += lax.dot_general(f_c, f_p, NT, preferred_element_type=F32)
    gp_ref[2 * TILE :, :] += lax.dot_general(f_p, f_p, NT, preferred_element_type=F32)
    y = y_ref[...].reshape(CHUNK // 128, 128).astype(F32)
    for at, f in ((0, f_r), (TILE, f_p)):
        acc = fit_ref[at : at + f.shape[0], :]
        for k in range(CHUNK // 128):
            acc = acc + f[:, 128 * k : 128 * (k + 1)].astype(F32) * y[k : k + 1, :]
        fit_ref[at : at + f.shape[0], :] = acc


def gram_part(idx, inducing, weights, x, y, carry):
    first = carry is None
    whole = lambda shape: pl.BlockSpec(shape, lambda i, idx: (0,) * len(shape))
    shapes = ((TILE, TILE), (2 * TILE + PB, PB), (TILE + PB, 128))
    in_specs = [
        pl.BlockSpec((TILE, F), lambda i, idx: (idx[0], 0)),
        pl.BlockSpec((TILE, F), lambda i, idx: (idx[1], 0)),
        pl.BlockSpec((PB, F), lambda i, idx: (idx[2], 0)),
        whole((1, F)),
        pl.BlockSpec((CHUNK, F), lambda i, idx: (i, 0)),
        pl.BlockSpec((1, CHUNK // 128, 128), lambda i, idx: (i, 0, 0)),
    ]
    args = [idx, inducing, inducing, inducing, weights[None, :], x, y.reshape(-1, CHUNK // 128, 128)]
    if not first:
        in_specs += [whole(s) for s in shapes]
        args += list(carry)
    return pl.pallas_call(
        functools.partial(gram_kernel, first),
        grid_spec=pltpu.PrefetchScalarGridSpec(
            num_scalar_prefetch=1,
            grid=(x.shape[0] // CHUNK,),
            in_specs=in_specs,
            out_specs=[whole(s) for s in shapes],
            scratch_shapes=[
                pltpu.VMEM((2 * TILE + PB, 256), BF16),
                pltpu.VMEM((2 * TILE + PB, 128), F32),
                pltpu.VMEM((CHUNK, 256), BF16),
            ],
        ),
        out_shape=[jax.ShapeDtypeStruct(s, F32) for s in shapes],
        compiler_params=pltpu.CompilerParams(vmem_limit_bytes=48 * 1024 * 1024),
        cost_estimate=pl.CostEstimate(flops=12_000_000_000, bytes_accessed=8_000_000, transcendentals=2_600_000),
        name="gram_part",
    )(*args)


def trace_scale_of(diag_ref):
    traces = jnp.zeros((1, 128), F32)
    for j in range(8):
        traces = traces + (diag_ref[j, 32:33, 0:128] + diag_ref[j, 33:34, 0:128])
    return jnp.sum(traces, axis=1, keepdims=True) * (1.0 / M)


def factor_kernel(diag_ref, gp_ref, low_ref, inv_ref, work, cols, dinv, mrow):
    row_id = lax.broadcasted_iota(jnp.int32, (PB, PB), 0)
    col_id = lax.broadcasted_iota(jnp.int32, (PB, PB), 1)
    scale = trace_scale_of(diag_ref)
    scale = RATE / scale
    for j in range(8):
        rows = slice(32 * j, 32 * j + 32)
        work[rows, 0:PB] = RATE * diag_ref[j, 0:32, :] + scale * gp_ref[2 * TILE + 32 * j : 2 * TILE + 32 * j + 32, :]
    work[:, PB:] = jnp.where(row_id == col_id, 1.0, 0.0)
    for b in range(PB // 8):
        base = 8 * b
        tile = base // 128 * 128
        spans = [t for t in range(0, 2 * PB, 128) if (tile <= t < PB) or PB <= t <= PB + base]
        d8 = work[base : base + 8, tile : tile + 128]
        for k in range(8):
            cols[8 * k : 8 * k + 8, :] = jnp.broadcast_to(d8[:, base - tile + k : base - tile + k + 1], (8, 128))
        d = {(i, k): cols[8 * k + i : 8 * k + i + 1, :] for k in range(8) for i in range(k, 8)}
        low = {}
        rs = {}
        m = {}
        for k in range(8):
            rs[k] = lax.rsqrt(d[k, k])
            for i in range(k + 1, 8):
                low[i, k] = d[i, k] * rs[k]
            for i in range(k + 1, 8):
                for j in range(k + 1, i + 1):
                    d[i, j] = d[i, j] - low[i, k] * low[j, k]
            m[k, k] = rs[k]
            for j in range(k):
                acc = low[k, j] * m[j, j]
                for t in range(j + 1, k):
                    acc = acc + low[k, t] * m[t, j]
                m[k, j] = -acc * rs[k]
        zero = jnp.zeros((1, 128), F32)
        for j in range(8):
            for i in range(8):
                mrow[8 * j + i : 8 * j + i + 1, :] = m[i, j] if i >= j else zero
        for i in range(8):
            for j in range(i, 8):
                acc = m[j, i] * m[j, j]
                for t in range(j + 1, 8):
                    acc = acc + m[t, i] * m[t, j]
                dinv[8 * j + i : 8 * j + i + 1, :] = acc
                if i != j:
                    dinv[8 * i + j : 8 * i + j + 1, :] = acc
        t_rows = {}
        for s in spans:
            u = None
            tt = None
            for j in range(8):
                r = work[base + j : base + j + 1, s : s + 128]
                if b + 1 < PB // 8:
                    q = dinv[8 * j : 8 * j + 8, :] * r
                    tt = q if tt is None else tt + q
                q = mrow[8 * j : 8 * j + 8, :] * r
                u = q if u is None else u + q
            t_rows[s] = tt
            work[base : base + 8, s : s + 128] = u
        for s in spans:
            if t_rows[s] is not None:
                cols[64 + 8 * (s // 128) : 72 + 8 * (s // 128), :] = t_rows[s]
        for g in range(b + 1, PB // 8):
            rows = slice(8 * g, 8 * g + 8)
            a = work[rows, tile : tile + 128]
            coef = [jnp.broadcast_to(a[:, base - tile + k : base - tile + k + 1], (8, 128)) for k in range(8)]
            for s in spans:
                v = work[rows, s : s + 128]
                for k in range(8):
                    v = v - coef[k] * cols[64 + 8 * (s // 128) + k : 65 + 8 * (s // 128) + k, :]
                work[rows, s : s + 128] = v
    low_ref[...] = jnp.where(row_id >= col_id, work[:, 0:PB].T, 0.0)
    inv_ref[...] = jnp.where(row_id >= col_id, work[:, PB:], 0.0)


def factored(diag, gram_p):
    vmem = pl.BlockSpec(memory_space=pltpu.VMEM)
    shape = jax.ShapeDtypeStruct((PB, PB), F32)
    return pl.pallas_call(
        factor_kernel,
        in_specs=[vmem, vmem],
        out_specs=[vmem, vmem],
        out_shape=[shape, shape],
        scratch_shapes=[
            pltpu.VMEM((PB, 2 * PB), F32),
            pltpu.VMEM((96, 128), F32),
            pltpu.VMEM((64, 128), F32),
            pltpu.VMEM((64, 128), F32),
        ],
        cost_estimate=pl.CostEstimate(flops=16_000_000_000, bytes_accessed=1_000_000, transcendentals=1000),
        name="factored",
    )(diag, gram_p)


def finish_kernel(
    idx_ref, diag_ref, y_ref, mo_ref, low_ref, inv_ref, gram_ref, gp_ref, fit_ref, gr_ref, gc_ref, prec_ref,
    out_ref, mean_ref, jr, jc,
):
    my_z, my_xc, half, in_row, in_col = (idx_ref[k] for k in range(5))
    trace_scale = trace_scale_of(diag_ref)
    scale = RATE / trace_scale
    ys = y_ref[...].astype(F32)
    power = jnp.sum(jnp.sum(ys * ys, axis=0, keepdims=True), axis=1, keepdims=True)
    mean_scale = RATE / jnp.sqrt(trace_scale * (power * (1.0 / B_TOTAL) + EPSILON))
    inv = inv_ref[...]
    for j in range(8):
        for h in range(2):
            at = h * PB + 32 * j
            rows = slice(at, at + 32)
            part = slice(32 * h, 32 * h + 32)
            jr[rows, :] = RATE * gr_ref[j ^ my_z, part, :] + scale * gp_ref[rows, :]
            jc[rows, :] = RATE * gc_ref[j ^ my_xc, part, :] + scale * gp_ref[TILE + at : TILE + at + 32, :]
    wide_r = lax.dot_general(jr[...], inv, NT, precision=HIGHEST, preferred_element_type=F32)
    wide_ct = lax.dot_general(inv, jc[...], NT, precision=HIGHEST, preferred_element_type=F32)
    taken = jnp.dot(wide_r, wide_ct, precision=HIGHEST, preferred_element_type=F32)
    out_ref[...] = RATE * prec_ref[...] + scale * gram_ref[...] - taken
    mean_p = RATE * diag_ref[0, 34:35, :] + mean_scale * jnp.sum(fit_ref[TILE:, :].T, axis=0, keepdims=True)
    mean_mid = RATE * mo_ref[...] + mean_scale * jnp.sum(fit_ref[0:TILE, :].T, axis=0, keepdims=True)
    head = lax.dot_general(mean_p, inv, NT, precision=HIGHEST, preferred_element_type=F32)
    mean_ref[...] = mean_mid - lax.dot_general(head, wide_r, NT, precision=HIGHEST, preferred_element_type=F32)
    for h in range(2):
        span = slice(h * PB, h * PB + PB)

        @pl.when((in_col == 1) & (half == h))
        def _():
            out_ref[:, span] = wide_r

        @pl.when((in_row == 1) & (half == h))
        def _():
            out_ref[span, :] = wide_ct
            mean_ref[:, span] = head

        @pl.when((in_row == 1) & (in_col == 1) & (half == h))
        def _():
            out_ref[span, span] = low_ref[...]


def finish(idx, *args):
    vmem = pl.BlockSpec(memory_space=pltpu.VMEM)
    return pl.pallas_call(
        finish_kernel,
        in_specs=[pl.BlockSpec(memory_space=pltpu.SMEM)] + [vmem] * len(args),
        out_specs=[vmem, vmem],
        out_shape=[jax.ShapeDtypeStruct((TILE, TILE), F32), jax.ShapeDtypeStruct((1, TILE), F32)],
        scratch_shapes=[pltpu.VMEM((TILE, PB), F32), pltpu.VMEM((TILE, PB), F32)],
        compiler_params=pltpu.CompilerParams(vmem_limit_bytes=48 * 1024 * 1024),
        cost_estimate=pl.CostEstimate(flops=4_000_000_000, bytes_accessed=4_000_000, transcendentals=1000),
        name="finish",
    )(idx, *args)


def local(pool, targets, picks, inducing, inv_sq_lengths, prec_old, mean_old, panel):
    my_row = lax.axis_index(ROW)
    my_col = lax.axis_index(COL)
    my_z = lax.axis_index("z")
    my_x = lax.axis_index("x")
    my_core = lax.axis_index("core")
    my_yl = lax.axis_index("yl")
    owner = panel[0] // 2
    half = panel[0] - 2 * owner
    o_yh, o_x, o_core = owner // 8, (owner // 2) % 4, owner % 2
    o_yl, o_z = owner // 8, owner % 8
    o_xy = (o_yh * 4 + o_x) * 2 + o_yl

    def ints(*values):
        lanes = jnp.arange(len(values), dtype=jnp.int32)
        out = jnp.zeros(len(values), jnp.int32)
        for k, v in enumerate(values):
            out = jnp.where(lanes == k, v.astype(jnp.int32), out)
        return out

    z_out = pack(ints(half, my_z), picks, pool, targets, prec_old)
    z_in = lax.all_to_all(z_out, "z", 0, 0, tiled=True)
    t_rows = trace_rows(inducing, inv_sq_lengths, z_out)

    xy_out, chunk = relay(ints(o_z, half), z_in, t_rows, mean_old)
    xy_in = lax.all_to_all(xy_out, XY, 0, 0, tiled=True)
    chunk = jnp.where(my_yl == o_yl, chunk, swapped(chunk, "yl", 2, 1))
    xy_in, chunk = lax.optimization_barrier((xy_in, chunk))

    own_x = xy_in[:, :128].reshape(HALF, 128)
    own_yy = xy_in[:, 128]
    chosen = lax.dynamic_index_in_dim(xy_in, o_xy, 0, keepdims=False).astype(F32)
    trace_xy = jnp.sum(xy_in[:, 133:136].astype(F32), axis=(0, 1))
    diag_piece = jnp.concatenate(
        [chosen[144:176] + chosen[208:240], chosen[176:208] + chosen[240:272]], axis=1
    )
    mean_panel = (chosen[129:131] + chosen[131:133]).reshape(1, PB)
    wide_trace = jnp.pad(trace_xy[None, :], ((0, 0), (0, 128)))
    mine = jnp.concatenate([diag_piece, wide_trace, mean_panel, jnp.zeros((6, PB), F32)], axis=0)
    blocks = lax.all_to_all(jnp.broadcast_to(mine[None], (8, 40, PB)), "z", 0, 0, tiled=True)
    core_in = swapped(jnp.concatenate([own_x, own_yy], axis=0), "core", 2, 1)
    far_r = swapped(chunk, "z", 8, 4)
    crossed = lax.ppermute(chunk, ALL, [(16 * i + j, 16 * j + i) for i in range(16) for j in range(16)])
    idx = ints(my_row, my_col, panel[0])
    carry = gram_part(idx, inducing, inv_sq_lengths, own_x, own_yy, None)
    carry, blocks, core_in, far_r, crossed, chunk, own_yy = lax.optimization_barrier(
        (carry, blocks, core_in, far_r, crossed, chunk, own_yy)
    )

    other_x = core_in[:HALF]
    other_yy = core_in[HALF : HALF + 16]
    blocks_in = swapped(blocks, "core", 2, 1)
    two_r = jnp.stack([chunk, far_r])
    two_r = jnp.stack([two_r, swapped(two_r, "z", 8, 2)], axis=1)
    two_c = jnp.stack([crossed, swapped(crossed, "core", 2, 1)])
    gram, gram_p, fit = gram_part(idx, inducing, inv_sq_lengths, other_x, other_yy, carry)
    here = my_core == o_core
    diag = jnp.concatenate(
        [
            jnp.where(here, blocks[:, :32], blocks_in[:, :32]),
            blocks[:, 32:33],
            blocks_in[:, 32:33],
            jnp.where(here, blocks[:, 33:34], blocks_in[:, 33:34]),
            jnp.zeros((8, 5, PB), F32),
        ],
        axis=1,
    )
    gram, gram_p, fit, diag, two_r, two_c = lax.optimization_barrier((gram, gram_p, fit, diag, two_r, two_c))

    got_r = jnp.stack([two_r, swapped(two_r, "z", 8, 1)], axis=2)
    got_c = jnp.stack([two_c] + [swapped(two_c, "x", 4, k) for k in (1, 2, 3)])
    factor, inv_factor = factored(diag, gram_p)
    all_y = jnp.concatenate([own_yy, other_yy], axis=0)
    in_row = my_row == owner
    in_col = my_col == owner
    updated, mean_next = finish(
        ints(my_z, 2 * my_x + my_core, half, in_row, in_col),
        diag,
        all_y,
        mean_old.reshape(1, TILE),
        factor,
        inv_factor,
        gram,
        gram_p,
        fit,
        got_r.reshape(8, 64, PB),
        got_c.reshape(8, 64, PB),
        prec_old,
    )
    return (updated, mean_next.reshape(TILE))


def solution(mesh):
    split = Mesh(mesh.devices.reshape(2, 4, 2, 2, 8), ALL)
    return jax.shard_map(
        local,
        mesh=split,
        in_specs=(P(ALL, None), P(ALL), P(ALL), P(), P(), P(ROW, COL), P(ROW), P()),
        out_specs=(P(ROW, COL), P(ROW)),
        check_vma=False,
    )
```

time: 173 us -> 127 us (0.73)
  the two profiles are of different devices: /device:TPU:44 before, /device:TPU:1 now
where the time goes in v2:
time: 127 us; the launch traced here: 126 us
  Pallas kernels  44.2 us (35%)
  starting transfers between devices  38 us (30%)
  waiting for transfers between devices  28.9 us (23%)
  local copies, waits for them, and re-layouts  10 us (8%)
  other arithmetic  3.32 us (3%)
  between operations  1.7 us (1%)
    pallas_call x2, Pallas kernels, gram_part(): pl.pallas_call(functools.partial(gram_kernel, first), grid_spec=pltpu.Pre...  14.8 us
    ppermute x10, starting transfers between devices, swapped(): return lax.ppermute(value, axis, [(i, i ^ bit) for i in range(size)])  13.6 us
    pallas_call x1, Pallas kernels, factored(): pl.pallas_call(factor_kernel, in_specs=[vmem, vmem], out_specs=[vmem, vme...  13.1 us
    all_to_all x1, waiting for transfers between devices, local(): z_in = lax.all_to_all(z_out, 'z', 0, 0, tiled=True)  11.7 us
    all_to_all x1, waiting for transfers between devices, local(): xy_in = lax.all_to_all(xy_out, XY, 0, 0, tiled=True)  9.1 us
    all_to_all x1, starting transfers between devices, local(): z_in = lax.all_to_all(z_out, 'z', 0, 0, tiled=True)  9 us
    ppermute x10, waiting for transfers between devices, swapped(): return lax.ppermute(value, axis, [(i, i ^ bit) for i in range(size)])  7.45 us
    pallas_call x1, Pallas kernels, trace_rows(): pl.pallas_call(trace_kernel, grid=(M // 1024,), in_specs=[pl.BlockSpec((1...  7.07 us
  transfers between devices with their start and end apart: 14, of which 4 were waited for; matrix products, arithmetic and copies ran while one was open for 1% of the time, Pallas kernels for 28%

profile of v2, /device:TPU:1, one launch (start us, length us, event | category | flops | bytes accessed | tf_op | source)
XLA Modules:
  0.0 126.2 jit_solution(2131380473314380107)
XLA Ops:
  1.8 2.7 %pack.1.x_ref = bf16[8,288,128]{2,1,0:T(8,128)(2,1)} custom-call(s32[2]{0:T(128)} %compare_select_fusion.10.idx_ref, s32[16]{0:T(128)} %picks_ref.1, bf16[128,128]{1,0:T(8,128)(2,1)} %pool_ref.1, bf16[1,128]{1,0:T(2,128)(2,1)} %bitcast.62, f32[512,512]{1,0:T(8,128)} %prec_ref.3), custom_call_target="tpu_custom_call" | custom-call | tf_op jit(solution)/shard_map/pack/pallas_call | solution.py:93
  4.5 9.0 %all-to-all-start = ((bf16[8,288,128]{2,1,0:T(8,128)(2,1)}), bf16[8,288,128]{2,1,0:T(8,128)(2,1)S(1)}, u32[]{:S(2)}, u32[]{:S(2)}) async-start(bf16[8,288,128]{2,1,0:T(8,128)(2,1)} %pack.1.x_ref), calls=%async_computation | async-start | bytes 1179648 | tf_op jit(solution)/shard_map/all_to_all | solution.py:462
  14.1 7.1 %trace_rows.1.t_ref = bf16[16,128]{1,0:T(8,128)(2,1)} custom-call(f32[8192,128]{1,0:T(8,128)} %pp_ref.3, f32[1,128]{1,0:T(1,128)} %bitcast.46, bf16[8,288,128]{2,1,0:T(8,128)(2,1)} %pack.1.x_ref), custom_call_target="tpu_custom_call" | custom-call | flops 4000000000 | bytes 4000000 | tf_op jit(solution)/shard_map/trace_rows/pallas_call | solution.py:136
  21.1 11.7 %all-to-all-done.z_ref = bf16[8,288,128]{2,1,0:T(8,128)(2,1)S(1)} async-done(((bf16[8,288,128]{2,1,0:T(8,128)(2,1)}), bf16[8,288,128]{2,1,0:T(8,128)(2,1)S(1)}, u32[]{:S(2)}, u32[]{:S(2)}) %all-to-all-start) | async-done | bytes 589856 | tf_op jit(solution)/shard_map/all_to_all | solution.py:462
  32.9 0.8 copy-done.10
  33.7 2.3 %relay.1 = (bf16[16,272,128]{2,1,0:T(8,128)(2,1)}, f32[64,256]{1,0:T(8,128)}) custom-call(s32[2]{0:T(128)} %compare_select_fusion.11.idx_ref, bf16[8,288,128]{2,1,0:T(8,128)(2,1)} %copy-done.10, bf16[16,128]{1,0:T(8,128)(2,1)} %trace_rows.1.t_ref, f32[4,128]{1,0:T(4,128)} %bitcast.44), custom_call_target="tpu_custom_call" | custom-call | tf_op jit(solution)/shard_map/relay/pallas_call | solution.py:186
  35.9 6.9 %all-to-all-start.1 = ((bf16[16,272,128]{2,1,0:T(8,128)(2,1)}), bf16[16,272,128]{2,1,0:T(8,128)(2,1)S(1)}, u32[]{:S(2)}, u32[]{:S(2)}) async-start(bf16[16,272,128]{2,1,0:T(8,128)(2,1)} %get-tuple-element.31), calls=%async_computation.1 | async-start | bytes 2228224 | tf_op jit(solution)/shard_map/all_to_all | solution.py:466
  43.0 1.3 %collective-permute-start = (f32[64,256]{1,0:T(8,128)S(1)}, f32[64,256]{1,0:T(8,128)S(1)}, u32[]{:S(2)}, u32[]{:S(2)}) collective-permute-start(f32[64,256]{1,0:T(8,128)S(1)} %copy-done.11), channel_id=1, source_target_pairs={{0,8},{8,0},{1,9},{9,1},{2,10},{10,2},{3,11},{11,3},{4,12},{12,4},... | collective-permute-start | bytes 196616 | tf_op jit(solution)/shard_map/ppermute | solution.py:33
  44.4 7.4 %collective-permute-done = f32[64,256]{1,0:T(8,128)S(1)} collective-permute-done((f32[64,256]{1,0:T(8,128)S(1)}, f32[64,256]{1,0:T(8,128)S(1)}, u32[]{:S(2)}, u32[]{:S(2)}) %collective-permute-start) | collective-permute-done | bytes 65568 | tf_op jit(solution)/shard_map/ppermute | solution.py:33
  51.8 9.1 %all-to-all-done.1 = bf16[16,272,128]{2,1,0:T(8,128)(2,1)S(1)} async-done(((bf16[16,272,128]{2,1,0:T(8,128)(2,1)}), bf16[16,272,128]{2,1,0:T(8,128)(2,1)S(1)}, u32[]{:S(2)}, u32[]{:S(2)}) %all-to-all-start.1) | async-done | bytes 1114144 | tf_op jit(solution)/shard_map/all_to_all | solution.py:466
  61.4 2.6 %collective-permute-start.3 = (f32[64,256]{1,0:T(8,128)S(1)}, f32[64,256]{1,0:T(8,128)S(1)}, u32[]{:S(2)}, u32[]{:S(2)}) collective-permute-start(f32[64,256]{1,0:T(8,128)S(1)} %broadcast_select_fusion), channel_id=1, source_target_pairs={{0,0},{1,16},{2,32},{3,48},{4,64},{5,80},{6,96},{7,112},{8,128},{9... | collective-permute-start | bytes 196616 | tf_op jit(solution)/shard_map/ppermute | solution.py:483
  64.1 0.8 broadcast_in_dim.75
  64.9 6.0 %all-to-all-start.2 = ((f32[8,40,256]{2,1,0:T(8,128)}), f32[8,40,256]{2,1,0:T(8,128)}, u32[]{:S(2)}, u32[]{:S(2)}) async-start(f32[8,40,256]{2,1,0:T(8,128)} %broadcast_in_dim.75), calls=%async_computation.2 | async-start | bytes 655360 | tf_op jit(solution)/shard_map/all_to_all | solution.py:480
  70.9 2.4 %collective-permute-start.1 = (bf16[2064,128]{1,0:T(8,128)(2,1)S(1)}, bf16[2064,128]{1,0:T(8,128)(2,1)}, u32[]{:S(2)}, u32[]{:S(2)}) collective-permute-start(bf16[2064,128]{1,0:T(8,128)(2,1)S(1)} %pad_maximum_fusion), channel_id=1, source_target_pairs={{0,16},{16,0},{1,17},{17,1},{2,18},{18,2},{3,19},{19,3},{4,20},{20... | collective-permute-start | bytes 1585160 | tf_op jit(solution)/shard_map/ppermute | solution.py:33
  73.2 7.4 %gram_part.2 = (f32[512,512]{1,0:T(8,128)S(1)}, f32[1280,256]{1,0:T(8,128)S(1)}, f32[768,128]{1,0:T(8,128)S(1)}) custom-call(s32[3]{0:T(128)S(1)} %compare_select_fusion.2.idx_ref, f32[8192,128]{1,0:T(8,128)} %pp_ref.3, f32[8192,128]{1,0:T(8,128)} %pp_ref.3, f32[8192,128]{1,0:T(8,128)} %pp_ref.3, f32[1,128]{1,0:T(1,128)S(1)} %bitcast.47, ...), custom_call_target="tpu_custom_call" | custom-call | flops 12000000000 | bytes 8000000 | tf_op jit(solution)/shard_map/gram_part/pallas_call | solution.py:264
  80.7 0.6 all-to-all-done.2
  81.3 1.1 slice.66.x_ref
  82.4 0.7 slice.67
  83.0 3.9 %collective-permute-start.4 = (f32[8,40,256]{2,1,0:T(8,128)}, f32[8,40,256]{2,1,0:T(8,128)S(1)}, u32[]{:S(2)}, u32[]{:S(2)}) collective-permute-start(f32[8,40,256]{2,1,0:T(8,128)} %all-to-all-done.2), channel_id=1, source_target_pairs={{0,16},{16,0},{1,17},{17,1},{2,18},{18,2},{3,19},{19,3},{4,20},{20... | collective-permute-start | bytes 983048 | tf_op jit(solution)/shard_map/ppermute | solution.py:33
  87.2 1.2 copy-done.9
  88.4 7.4 %gram_part.3 = (f32[512,512]{1,0:T(8,128)S(1)}, f32[1280,256]{1,0:T(8,128)S(1)}, f32[768,128]{1,0:T(8,128)S(1)}) custom-call(s32[3]{0:T(128)S(1)} %compare_select_fusion.2.idx_ref, f32[8192,128]{1,0:T(8,128)} %pp_ref.3, f32[8192,128]{1,0:T(8,128)} %pp_ref.3, f32[8192,128]{1,0:T(8,128)} %pp_ref.3, f32[1,128]{1,0:T(1,128)S(1)} %bitcast.48, ...), custom_call_target="tpu_custom_call" | custom-call | flops 12000000000 | bytes 8000000 | tf_op jit(solution)/shard_map/gram_part/pallas_call | solution.py:264
  95.8 1.1 copy-done.4
  96.9 1.0 slice_select_fusion
  97.9 0.9 broadcast_select_fusion.1
  98.9 1.4 %concatenate.18.diag_ref = f32[8,40,256]{2,1,0:T(8,128)} concatenate(f32[8,32,256]{2,1,0:T(8,128)S(1)} %slice_select_fusion, f32[8,1,256]{2,1,0:T(1,128)S(1)} %get-tuple-element.63, f32[8,1,256]{2,1,0:T(1,128)S(1)} %get-tuple-element.64, f32[8,1,256]{2,1,0:T(1,128)S(1)} %get-tuple-element.62, f32[8,5,256]{2,1,0:T(8,128)S(1)} %broadcast_in_dim.76), dimensions={1} | concatenate | bytes 655360 | tf_op jit(solution)/shard_map/concatenate | solution.py:498
  100.3 1.2 collective-permute-start.10
  101.5 3.9 %collective-permute-start.9 = (f32[2,64,256]{2,1,0:T(8,128)S(1)}, f32[2,64,256]{2,1,0:T(8,128)S(1)}, u32[]{:S(2)}, u32[]{:S(2)}) collective-permute-start(f32[2,64,256]{2,1,0:T(8,128)S(1)} %pad_maximum_fusion.5), channel_id=1, source_target_pairs={{0,64},{32,96},{64,0},{96,32},{1,65},{33,97},{65,1},{97,33},{2,66}... | collective-permute-start | bytes 393224 | tf_op jit(solution)/shard_map/ppermute | solution.py:33
  105.4 0.6 collective-permute-start.7
  106.0 13.1 %factored.1 = (f32[256,256]{1,0:T(8,128)}, f32[256,256]{1,0:T(8,128)}) custom-call(f32[8,40,256]{2,1,0:T(8,128)} %concatenate.18.diag_ref, f32[1280,256]{1,0:T(8,128)} %copy-done.4), custom_call_target="tpu_custom_call" | custom-call | flops 16000000000 | bytes 1000000 | tf_op jit(solution)/shard_map/factored/pallas_call | solution.py:368
  119.4 1.1 copy-done.5
  120.9 0.9 copy-done.7
  121.9 4.3 %finish.1 = (f32[512,512]{1,0:T(8,128)}, f32[1,512]{1,0:T(1,128)}) custom-call(s32[5]{0:T(128)S(1)} %compare_select_fusion.7.idx_ref, f32[8,40,256]{2,1,0:T(8,128)S(1)} %copy-done.1, bf16[32,128]{1,0:T(8,128)(2,1)S(1)} %pad_maximum_fusion.6.y_ref, f32[1,512]{1,0:T(1,128)S(1)} %bitcast.45, f32[256,256]{1,0:T(8,128)S(1)} %copy-done.6, ...), custom_call_target="tpu_custom_call" | custom-call | flops 4000000000 | bytes 4000000 | tf_op jit(solution)/shard_map/finish/pallas_call | solution.py:429
  (57 shorter events, 2.7 us)
Async XLA Ops:
  4.5 28.4 %all-to-all-start = ((bf16[8,288,128]{2,1,0:T(8,128)(2,1)}), bf16[8,288,128]{2,1,0:T(8,128)(2,1)S(1)}, u32[]{:S(2)}, u32[]{:S(2)}) async-start(bf16[8,288,128]{2,1,0:T(8,128)(2,1)} %pack.1.x_ref), calls=%async_computation | async-start | bytes 1179648 | tf_op jit(solution)/shard_map/all_to_all | solution.py:462
  32.9 0.8 copy-start.10
  35.9 7.1 %copy-start.11 = (f32[64,256]{1,0:T(8,128)S(1)}, f32[64,256]{1,0:T(8,128)}, u32[]{:S(2)}) copy-start(f32[64,256]{1,0:T(8,128)} %get-tuple-element.32) | copy-start | bytes 196612
  35.9 25.0 %all-to-all-start.1 = ((bf16[16,272,128]{2,1,0:T(8,128)(2,1)}), bf16[16,272,128]{2,1,0:T(8,128)(2,1)S(1)}, u32[]{:S(2)}, u32[]{:S(2)}) async-start(bf16[16,272,128]{2,1,0:T(8,128)(2,1)} %get-tuple-element.31), calls=%async_computation.1 | async-start | bytes 2228224 | tf_op jit(solution)/shard_map/all_to_all | solution.py:466
  43.0 8.8 %collective-permute-start = (f32[64,256]{1,0:T(8,128)S(1)}, f32[64,256]{1,0:T(8,128)S(1)}, u32[]{:S(2)}, u32[]{:S(2)}) collective-permute-start(f32[64,256]{1,0:T(8,128)S(1)} %copy-done.11), channel_id=1, source_target_pairs={{0,8},{8,0},{1,9},{9,1},{2,10},{10,2},{3,11},{11,3},{4,12},{12,4},... | collective-permute-start | bytes 196616 | tf_op jit(solution)/shard_map/ppermute | solution.py:33
  61.3 11.9 %copy-start.3 = (f32[128]{0:T(128)S(1)}, f32[128]{0:T(128)}, u32[]{:S(2)}) copy-start(f32[128]{0:T(128)} %param.12) | copy-start | bytes 1540
  61.3 19.3 %collective-permute-start.2 = (f32[64,256]{1,0:T(8,128)S(1)}, f32[64,256]{1,0:T(8,128)S(1)}, u32[]{:S(2)}, u32[]{:S(2)}) collective-permute-start(f32[64,256]{1,0:T(8,128)S(1)} %broadcast_select_fusion), channel_id=1, source_target_pairs={{0,4},{1,5},{2,6},{3,7},{4,0},{5,1},{6,2},{7,3},{8,12},{9,13},{10,... | collective-permute-start | bytes 196616 | tf_op jit(solution)/shard_map/ppermute | solution.py:33
  61.4 19.2 %collective-permute-start.3 = (f32[64,256]{1,0:T(8,128)S(1)}, f32[64,256]{1,0:T(8,128)S(1)}, u32[]{:S(2)}, u32[]{:S(2)}) collective-permute-start(f32[64,256]{1,0:T(8,128)S(1)} %broadcast_select_fusion), channel_id=1, source_target_pairs={{0,0},{1,16},{2,32},{3,48},{4,64},{5,80},{6,96},{7,112},{8,128},{9... | collective-permute-start | bytes 196616 | tf_op jit(solution)/shard_map/ppermute | solution.py:483
  64.9 16.4 %all-to-all-start.2 = ((f32[8,40,256]{2,1,0:T(8,128)}), f32[8,40,256]{2,1,0:T(8,128)}, u32[]{:S(2)}, u32[]{:S(2)}) async-start(f32[8,40,256]{2,1,0:T(8,128)} %broadcast_in_dim.75), calls=%async_computation.2 | async-start | bytes 655360 | tf_op jit(solution)/shard_map/all_to_all | solution.py:480
  70.9 9.8 %collective-permute-start.1 = (bf16[2064,128]{1,0:T(8,128)(2,1)S(1)}, bf16[2064,128]{1,0:T(8,128)(2,1)}, u32[]{:S(2)}, u32[]{:S(2)}) collective-permute-start(bf16[2064,128]{1,0:T(8,128)(2,1)S(1)} %pad_maximum_fusion), channel_id=1, source_target_pairs={{0,16},{16,0},{1,17},{17,1},{2,18},{18,2},{3,19},{19,3},{4,20},{20... | collective-permute-start | bytes 1585160 | tf_op jit(solution)/shard_map/ppermute | solution.py:33
  80.6 6.5 %copy-start.8 = (f32[512,512]{1,0:T(8,128)}, f32[512,512]{1,0:T(8,128)S(1)}, u32[]{:S(2)}) copy-start(f32[512,512]{1,0:T(8,128)S(1)} %get-tuple-element.39.refs_0_) | copy-start | bytes 3145732
  83.0 13.9 %collective-permute-start.4 = (f32[8,40,256]{2,1,0:T(8,128)}, f32[8,40,256]{2,1,0:T(8,128)S(1)}, u32[]{:S(2)}, u32[]{:S(2)}) collective-permute-start(f32[8,40,256]{2,1,0:T(8,128)} %all-to-all-done.2), channel_id=1, source_target_pairs={{0,16},{16,0},{1,17},{17,1},{2,18},{18,2},{3,19},{19,3},{4,20},{20... | collective-permute-start | bytes 983048 | tf_op jit(solution)/shard_map/ppermute | solution.py:33
  87.0 9.9 %collective-permute-start.5 = (f32[2,64,256]{2,1,0:T(8,128)S(1)}, f32[2,64,256]{2,1,0:T(8,128)S(1)}, u32[]{:S(2)}, u32[]{:S(2)}) collective-permute-start(f32[2,64,256]{2,1,0:T(8,128)S(1)} %get-tuple-element.68), channel_id=1, source_target_pairs={{0,2},{1,3},{2,0},{3,1},{4,6},{5,7},{6,4},{7,5},{8,10},{9,11},{10,... | collective-permute-start | bytes 393224 | tf_op jit(solution)/shard_map/ppermute | solution.py:33
  87.1 9.8 %collective-permute-start.6 = (f32[64,256]{1,0:T(8,128)S(1)}, f32[64,256]{1,0:T(8,128)S(1)}, u32[]{:S(2)}, u32[]{:S(2)}) collective-permute-start(f32[64,256]{1,0:T(8,128)S(1)} %collective-permute-done.3), channel_id=1, source_target_pairs={{0,16},{16,0},{1,17},{17,1},{2,18},{18,2},{3,19},{19,3},{4,20},{20... | collective-permute-start | bytes 196616 | tf_op jit(solution)/shard_map/ppermute | solution.py:33
  87.2 1.2 copy-start.9
  95.8 1.1 copy-start.4
  100.3 18.8 %collective-permute-start.10 = (f32[2,64,256]{2,1,0:T(8,128)S(1)}, f32[2,64,256]{2,1,0:T(8,128)S(1)}, u32[]{:S(2)}, u32[]{:S(2)}) collective-permute-start(f32[2,64,256]{2,1,0:T(8,128)S(1)} %pad_maximum_fusion.5), channel_id=1, source_target_pairs={{0,96},{32,64},{64,32},{96,0},{1,97},{33,65},{65,33},{97,1},{2,98}... | collective-permute-start | bytes 393224 | tf_op jit(solution)/shard_map/ppermute | solution.py:33
  101.5 17.7 %collective-permute-start.9 = (f32[2,64,256]{2,1,0:T(8,128)S(1)}, f32[2,64,256]{2,1,0:T(8,128)S(1)}, u32[]{:S(2)}, u32[]{:S(2)}) collective-permute-start(f32[2,64,256]{2,1,0:T(8,128)S(1)} %pad_maximum_fusion.5), channel_id=1, source_target_pairs={{0,64},{32,96},{64,0},{96,32},{1,65},{33,97},{65,1},{97,33},{2,66}... | collective-permute-start | bytes 393224 | tf_op jit(solution)/shard_map/ppermute | solution.py:33
  105.4 13.8 %collective-permute-start.8 = (f32[2,64,256]{2,1,0:T(8,128)S(1)}, f32[2,64,256]{2,1,0:T(8,128)S(1)}, u32[]{:S(2)}, u32[]{:S(2)}) collective-permute-start(f32[2,64,256]{2,1,0:T(8,128)S(1)} %pad_maximum_fusion.5), channel_id=1, source_target_pairs={{0,32},{32,0},{64,96},{96,64},{1,33},{33,1},{65,97},{97,65},{2,34}... | collective-permute-start | bytes 393224 | tf_op jit(solution)/shard_map/ppermute | solution.py:33
  105.4 13.9 %collective-permute-start.7 = (f32[2,2,64,256]{3,2,0,1:T(8,128)S(1)}, f32[2,2,64,256]{3,2,0,1:T(8,128)S(1)}, u32[]{:S(2)}, u32[]{:S(2)}) collective-permute-start(f32[2,2,64,256]{3,2,0,1:T(8,128)S(1)} %pad_maximum_fusion.3), channel_id=1, source_target_pairs={{0,1},{1,0},{2,3},{3,2},{4,5},{5,4},{6,7},{7,6},{8,9},{9,8},{10,11... | collective-permute-start | bytes 786440 | tf_op jit(solution)/shard_map/ppermute | solution.py:33
  119.1 1.3 %copy-start.5 = (f32[1280,256]{1,0:T(8,128)S(1)}, f32[1280,256]{1,0:T(8,128)}, u32[]{:S(2)}) copy-start(f32[1280,256]{1,0:T(8,128)} %copy-done.4) | copy-start | bytes 3932164
  119.2 1.6 %copy-start = (f32[512,512]{1,0:T(8,128)S(1)}, f32[512,512]{1,0:T(8,128)}, u32[]{:S(2)}) copy-start(f32[512,512]{1,0:T(8,128)} %prec_ref.3) | copy-start | bytes 3145732
  119.2 1.6 %copy-start.1 = (f32[8,40,256]{2,1,0:T(8,128)S(1)}, f32[8,40,256]{2,1,0:T(8,128)}, u32[]{:S(2)}) copy-start(f32[8,40,256]{2,1,0:T(8,128)} %concatenate.18.diag_ref) | copy-start | bytes 983044
  119.2 1.6 %copy-start.2 = (f32[512]{0:T(512)S(1)}, f32[512]{0:T(512)}, u32[]{:S(2)}) copy-start(f32[512]{0:T(512)} %param.14) | copy-start | bytes 6148
  119.2 1.7 %copy-start.6 = (f32[256,256]{1,0:T(8,128)S(1)}, f32[256,256]{1,0:T(8,128)}, u32[]{:S(2)}) copy-start(f32[256,256]{1,0:T(8,128)} %get-tuple-element.52.low_ref) | copy-start | bytes 786436
  120.9 0.9 copy-start.7

commit v3 on v2

--- a/solution.py
+++ b/solution.py
@@ -83,7 +83,7 @@
     y_row = jnp.sum(jnp.where(lane == 16 * idx_ref[1] + sub, y, 0.0), axis=0, keepdims=True)
     y_rows = jnp.where(sub == 0, y_row, 0.0).astype(BF16)
     for j in range(8):
-        chunk = jnp.concatenate([prec_ref[32 * j : 32 * j + 32, :], prec_ref[PB + 32 * j : PB + 32 * j + 32, :]], axis=0)
+        chunk = jnp.concatenate([prec_ref[128 * q + 16 * j : 128 * q + 16 * j + 16, :] for q in range(4)], axis=0)
         split_rows(out_ref.at[j], 0, 64, chunk)
         out_ref[j, 256:272, :] = samples
         out_ref[j, 272:288, :] = y_rows
@@ -150,35 +150,35 @@
 
 
 def relay_kernel(idx_ref, z_ref, t_ref, mean_ref, out_ref, chunk_ref):
-    src, half = idx_ref[0], idx_ref[1]
+    src, half, my_z = idx_ref[0], idx_ref[1], idx_ref[2]
     sub = lax.broadcasted_iota(jnp.int32, (16, 128), 0)
-    chunk = z_ref[src, 0:256, :]
-    values = chunk.astype(F32)
+    lane = lax.broadcasted_iota(jnp.int32, (16, 128), 1)
+    values = z_ref[src, 0:256, :].astype(F32)
     chunk_ref[:, 0:128] = values[0:64] + values[128:192]
     chunk_ref[:, 128:256] = values[64:128] + values[192:256]
+    parts, diagonals = [], []
+    for k in range(2):
+        left, right = values[128 * k : 128 * k + 64], values[128 * k + 64 : 128 * k + 128]
+        top = jnp.where(half == 0, left[0:16], left[32:48])
+        low_left = jnp.where(half == 0, left[16:32], left[48:64])
+        low_right = jnp.where(half == 0, right[16:32], right[48:64])
+        own = 16 * my_z + sub
+        parts += [low_left, jnp.where(lane <= own, top, low_right)]
+        diagonals.append(jnp.sum(jnp.where(lane == own, low_right, 0.0), axis=0, keepdims=True))
     y = jnp.sum(z_ref[:, 272:288, :].astype(F32), axis=0)
     means = mean_ref[pl.ds(2 * half, 2), :]
     m_high = means.astype(BF16).astype(F32)
     m_low = means - m_high
     t = t_ref[...].astype(F32)
     aux = jnp.where(sub == 0, y, 0.0)
-    for k, row in enumerate((m_high[0:1], m_high[1:2], m_low[0:1], m_low[1:2], t[0:1], t[1:2], t[2:3])):
+    rows = (m_high[0:1], m_high[1:2], m_low[0:1], m_low[1:2], t[0:1], t[1:2], t[2:3], *diagonals)
+    for k, row in enumerate(rows):
         aux = jnp.where(sub == k + 1, row, aux)
-    aux = aux.astype(BF16)
-    for k in range(4):
-        @pl.when(half == 0)
-        def _():
-            out_ref[0, 144 + 32 * k : 176 + 32 * k, :] = chunk[64 * k : 64 * k + 32]
-
-        @pl.when(half == 1)
-        def _():
-            out_ref[0, 144 + 32 * k : 176 + 32 * k, :] = chunk[64 * k + 32 : 64 * k + 64]
-
-    out_ref[0, 0:128, :] = z_ref[:, 256:272, :].reshape(128, 128)
-    out_ref[0, 128:144, :] = aux
-    whole = out_ref[0]
-    for k in range(1, 16):
-        out_ref[k] = whole
+    whole = jnp.concatenate([p.astype(BF16) for p in (aux, *parts)], axis=0)
+    samples = z_ref[:, 256:272, :].reshape(128, 128)
+    for k in range(16):
+        out_ref[k, 0:128, :] = samples
+        out_ref[k, 128:208, :] = whole
 
 
 def relay(idx, z_in, t_rows, mean_old):
@@ -187,16 +187,12 @@
         relay_kernel,
         in_specs=[pl.BlockSpec(memory_space=pltpu.SMEM), vmem, vmem, vmem],
         out_specs=[vmem, vmem],
-        out_shape=[jax.ShapeDtypeStruct((16, 272, 128), BF16), jax.ShapeDtypeStruct((64, PB), F32)],
+        out_shape=[jax.ShapeDtypeStruct((16, 208, 128), BF16), jax.ShapeDtypeStruct((64, PB), F32)],
         name="relay",
     )(idx, z_in, t_rows, mean_old.reshape(4, 128))
 
 
-def gram_kernel(first, idx_ref, pr_ref, pc_ref, pp_ref, w_ref, x_ref, y_ref, *refs):
-    if first:
-        grc_ref, gp_ref, fit_ref, paug, own, xaug = refs
-    else:
-        grc_in, gp_in, fit_in, grc_ref, gp_ref, fit_ref, paug, own, xaug = refs
+def gram_kernel(idx_ref, pr_ref, pc_ref, pp_ref, w_ref, x_ref, y_ref, grc_ref, gp_ref, fit_ref, paug, own, xaug, ys):
     step = pl.program_id(0)
 
     @pl.when(step == 0)
@@ -209,16 +205,15 @@
             paug[at : at + n, 128:256] = low
             own[at : at + n, :] = jnp.broadcast_to(term, (n, 128))
             at += n
-        if first:
-            grc_ref[...] = jnp.zeros_like(grc_ref)
-            gp_ref[...] = jnp.zeros_like(gp_ref)
-            fit_ref[...] = jnp.zeros_like(fit_ref)
-        else:
-            grc_ref[...] = grc_in[...]
-            gp_ref[...] = gp_in[...]
-            fit_ref[...] = fit_in[...]
-
-    x = x_ref[...]
+        y_all = (y_ref[:, 0, :] if len(y_ref.shape) == 3 else y_ref[...]).astype(F32)
+        for k in range(4):
+            ys[k, 0:4, :] = y_all[4 * k : 4 * k + 4]
+        grc_ref[...] = jnp.zeros_like(grc_ref)
+        gp_ref[...] = jnp.zeros_like(gp_ref)
+        fit_ref[...] = jnp.zeros_like(fit_ref)
+        fit_ref[TILE + PB : TILE + PB + 1, :] = jnp.sum(y_all * y_all, axis=0, keepdims=True)
+
+    x = x_ref[...].reshape(CHUNK, F)
     xaug[:, 0:128] = x
     xaug[:, 128:256] = x
     xa = xaug[...]
@@ -237,7 +232,7 @@
     gp_ref[0:TILE, :] += lax.dot_general(f_r, f_p, NT, preferred_element_type=F32)
     gp_ref[TILE : 2 * TILE, :] += lax.dot_general(f_c, f_p, NT, preferred_element_type=F32)
     gp_ref[2 * TILE :, :] += lax.dot_general(f_p, f_p, NT, preferred_element_type=F32)
-    y = y_ref[...].reshape(CHUNK // 128, 128).astype(F32)
+    y = ys[step]
     for at, f in ((0, f_r), (TILE, f_p)):
         acc = fit_ref[at : at + f.shape[0], :]
         for k in range(CHUNK // 128):
@@ -245,57 +240,62 @@
         fit_ref[at : at + f.shape[0], :] = acc
 
 
-def gram_part(idx, inducing, weights, x, y, carry):
-    first = carry is None
-    whole = lambda shape: pl.BlockSpec(shape, lambda i, idx: (0,) * len(shape))
-    shapes = ((TILE, TILE), (2 * TILE + PB, PB), (TILE + PB, 128))
-    in_specs = [
-        pl.BlockSpec((TILE, F), lambda i, idx: (idx[0], 0)),
-        pl.BlockSpec((TILE, F), lambda i, idx: (idx[1], 0)),
-        pl.BlockSpec((PB, F), lambda i, idx: (idx[2], 0)),
-        whole((1, F)),
-        pl.BlockSpec((CHUNK, F), lambda i, idx: (i, 0)),
-        pl.BlockSpec((1, CHUNK // 128, 128), lambda i, idx: (i, 0, 0)),
-    ]
-    args = [idx, inducing, inducing, inducing, weights[None, :], x, y.reshape(-1, CHUNK // 128, 128)]
-    if not first:
-        in_specs += [whole(s) for s in shapes]
-        args += list(carry)
+def gram_part(idx, inducing, weights, source, x_spec, y_spec):
+    shapes = ((TILE, TILE), (2 * TILE + PB, PB), (TILE + PB + 8, 128))
     return pl.pallas_call(
-        functools.partial(gram_kernel, first),
+        gram_kernel,
         grid_spec=pltpu.PrefetchScalarGridSpec(
             num_scalar_prefetch=1,
-            grid=(x.shape[0] // CHUNK,),
-            in_specs=in_specs,
-            out_specs=[whole(s) for s in shapes],
+            grid=(HALF // CHUNK,),
+            in_specs=[
+                pl.BlockSpec((TILE, F), lambda i, idx: (idx[0], 0)),
+                pl.BlockSpec((TILE, F), lambda i, idx: (idx[1], 0)),
+                pl.BlockSpec((PB, F), lambda i, idx: (idx[2], 0)),
+                pl.BlockSpec((1, F), lambda i, idx: (0, 0)),
+                x_spec,
+                y_spec,
+            ],
+            out_specs=[pl.BlockSpec(s, lambda i, idx: (0, 0)) for s in shapes],
             scratch_shapes=[
                 pltpu.VMEM((2 * TILE + PB, 256), BF16),
                 pltpu.VMEM((2 * TILE + PB, 128), F32),
                 pltpu.VMEM((CHUNK, 256), BF16),
+                pltpu.VMEM((4, 8, 128), F32),
             ],
         ),
         out_shape=[jax.ShapeDtypeStruct(s, F32) for s in shapes],
         compiler_params=pltpu.CompilerParams(vmem_limit_bytes=48 * 1024 * 1024),
         cost_estimate=pl.CostEstimate(flops=12_000_000_000, bytes_accessed=8_000_000, transcendentals=2_600_000),
         name="gram_part",
-    )(*args)
-
-
-def trace_scale_of(diag_ref):
+    )(idx, inducing, inducing, inducing, weights[None, :], source, source)
+
+
+def trace_scale_of(near_ref, far_ref):
     traces = jnp.zeros((1, 128), F32)
     for j in range(8):
-        traces = traces + (diag_ref[j, 32:33, 0:128] + diag_ref[j, 33:34, 0:128])
+        traces = traces + (near_ref[j, 16:17, 0:128] + far_ref[j, 16:17, 0:128])
     return jnp.sum(traces, axis=1, keepdims=True) * (1.0 / M)
 
 
-def factor_kernel(diag_ref, gp_ref, low_ref, inv_ref, work, cols, dinv, mrow):
+def factor_kernel(idx_ref, near_ref, far_ref, gp1_ref, gp2_ref, low_ref, inv_ref, work, cols, dinv, mrow):
+    here = idx_ref[0] == 1
     row_id = lax.broadcasted_iota(jnp.int32, (PB, PB), 0)
     col_id = lax.broadcasted_iota(jnp.int32, (PB, PB), 1)
-    scale = trace_scale_of(diag_ref)
-    scale = RATE / scale
-    for j in range(8):
-        rows = slice(32 * j, 32 * j + 32)
-        work[rows, 0:PB] = RATE * diag_ref[j, 0:32, :] + scale * gp_ref[2 * TILE + 32 * j : 2 * TILE + 32 * j + 32, :]
+    low = lax.broadcasted_iota(jnp.int32, (128, 128), 0)
+    lane = lax.broadcasted_iota(jnp.int32, (128, 128), 1)
+    scale = RATE / trace_scale_of(near_ref, far_ref)
+    blocks = [jnp.where(here, near_ref[j], far_ref[j]) for j in range(8)]
+    both = jnp.concatenate([b[0:16, 0:128] for b in blocks], axis=0)
+    low_left = jnp.concatenate([b[0:16, 128:256] for b in blocks], axis=0)
+    diagonal = jnp.concatenate([jnp.broadcast_to(b[16:17, 128:256], (16, 128)) for b in blocks], axis=0)
+    on = low == lane
+    under = jnp.where(low > lane, both, 0.0)
+    over = jnp.where(low < lane, both, 0.0)
+    gram = scale * (gp1_ref[2 * TILE :, :] + gp2_ref[2 * TILE :, :])
+    work[0:128, 0:128] = RATE * (under + under.T + jnp.where(on, both, 0.0)) + gram[0:128, 0:128]
+    work[0:128, 128:256] = RATE * low_left.T + gram[0:128, 128:256]
+    work[128:256, 0:128] = RATE * low_left + gram[128:256, 0:128]
+    work[128:256, 128:256] = RATE * (over + over.T + jnp.where(on, diagonal, 0.0)) + gram[128:256, 128:256]
     work[:, PB:] = jnp.where(row_id == col_id, 1.0, 0.0)
     for b in range(PB // 8):
         base = 8 * b
@@ -305,21 +305,21 @@
         for k in range(8):
             cols[8 * k : 8 * k + 8, :] = jnp.broadcast_to(d8[:, base - tile + k : base - tile + k + 1], (8, 128))
         d = {(i, k): cols[8 * k + i : 8 * k + i + 1, :] for k in range(8) for i in range(k, 8)}
-        low = {}
+        lo = {}
         rs = {}
         m = {}
         for k in range(8):
             rs[k] = lax.rsqrt(d[k, k])
             for i in range(k + 1, 8):
-                low[i, k] = d[i, k] * rs[k]
+                lo[i, k] = d[i, k] * rs[k]
             for i in range(k + 1, 8):
                 for j in range(k + 1, i + 1):
-                    d[i, j] = d[i, j] - low[i, k] * low[j, k]
+                    d[i, j] = d[i, j] - lo[i, k] * lo[j, k]
             m[k, k] = rs[k]
             for j in range(k):
-                acc = low[k, j] * m[j, j]
+                acc = lo[k, j] * m[j, j]
                 for t in range(j + 1, k):
-                    acc = acc + low[k, t] * m[t, j]
+                    acc = acc + lo[k, t] * m[t, j]
                 m[k, j] = -acc * rs[k]
         zero = jnp.zeros((1, 128), F32)
         for j in range(8):
@@ -362,12 +362,12 @@
     inv_ref[...] = jnp.where(row_id >= col_id, work[:, PB:], 0.0)
 
 
-def factored(diag, gram_p):
+def factored(idx, near, far, gp1, gp2):
     vmem = pl.BlockSpec(memory_space=pltpu.VMEM)
     shape = jax.ShapeDtypeStruct((PB, PB), F32)
     return pl.pallas_call(
         factor_kernel,
-        in_specs=[vmem, vmem],
+        in_specs=[pl.BlockSpec(memory_space=pltpu.SMEM), vmem, vmem, vmem, vmem],
         out_specs=[vmem, vmem],
         out_shape=[shape, shape],
         scratch_shapes=[
@@ -378,33 +378,34 @@
         ],
         cost_estimate=pl.CostEstimate(flops=16_000_000_000, bytes_accessed=1_000_000, transcendentals=1000),
         name="factored",
-    )(diag, gram_p)
+    )(idx, near, far, gp1, gp2)
 
 
 def finish_kernel(
-    idx_ref, diag_ref, y_ref, mo_ref, low_ref, inv_ref, gram_ref, gp_ref, fit_ref, gr_ref, gc_ref, prec_ref,
-    out_ref, mean_ref, jr, jc,
+    idx_ref, near_ref, far_ref, mo_ref, low_ref, inv_ref, g1_ref, g2_ref, gp1_ref, gp2_ref, fit1_ref, fit2_ref,
+    gr_ref, gc_ref, prec_ref, out_ref, mean_ref, jr, jc,
 ):
-    my_z, my_xc, half, in_row, in_col = (idx_ref[k] for k in range(5))
-    trace_scale = trace_scale_of(diag_ref)
+    my_z, my_xc, half, in_row, in_col, here = (idx_ref[k] for k in range(6))
+    trace_scale = trace_scale_of(near_ref, far_ref)
     scale = RATE / trace_scale
-    ys = y_ref[...].astype(F32)
-    power = jnp.sum(jnp.sum(ys * ys, axis=0, keepdims=True), axis=1, keepdims=True)
+    fit = fit1_ref[...] + fit2_ref[...]
+    power = jnp.sum(fit[TILE + PB : TILE + PB + 1, :], axis=1, keepdims=True)
     mean_scale = RATE / jnp.sqrt(trace_scale * (power * (1.0 / B_TOTAL) + EPSILON))
     inv = inv_ref[...]
     for j in range(8):
-        for h in range(2):
-            at = h * PB + 32 * j
-            rows = slice(at, at + 32)
-            part = slice(32 * h, 32 * h + 32)
-            jr[rows, :] = RATE * gr_ref[j ^ my_z, part, :] + scale * gp_ref[rows, :]
-            jc[rows, :] = RATE * gc_ref[j ^ my_xc, part, :] + scale * gp_ref[TILE + at : TILE + at + 32, :]
+        for q in range(4):
+            rows = slice(128 * q + 16 * j, 128 * q + 16 * j + 16)
+            part = slice(16 * q, 16 * q + 16)
+            far = slice(TILE + 128 * q + 16 * j, TILE + 128 * q + 16 * j + 16)
+            jr[rows, :] = RATE * gr_ref[j ^ my_z, part, :] + scale * (gp1_ref[rows, :] + gp2_ref[rows, :])
+            jc[rows, :] = RATE * gc_ref[j ^ my_xc, part, :] + scale * (gp1_ref[far, :] + gp2_ref[far, :])
     wide_r = lax.dot_general(jr[...], inv, NT, precision=HIGHEST, preferred_element_type=F32)
     wide_ct = lax.dot_general(inv, jc[...], NT, precision=HIGHEST, preferred_element_type=F32)
     taken = jnp.dot(wide_r, wide_ct, precision=HIGHEST, preferred_element_type=F32)
-    out_ref[...] = RATE * prec_ref[...] + scale * gram_ref[...] - taken
-    mean_p = RATE * diag_ref[0, 34:35, :] + mean_scale * jnp.sum(fit_ref[TILE:, :].T, axis=0, keepdims=True)
-    mean_mid = RATE * mo_ref[...] + mean_scale * jnp.sum(fit_ref[0:TILE, :].T, axis=0, keepdims=True)
+    out_ref[...] = RATE * prec_ref[...] + scale * (g1_ref[...] + g2_ref[...]) - taken
+    panel_mean = jnp.where(here == 1, near_ref[0, 17:18, :], far_ref[0, 17:18, :])
+    mean_p = RATE * panel_mean + mean_scale * jnp.sum(fit[TILE : TILE + PB].T, axis=0, keepdims=True)
+    mean_mid = RATE * mo_ref[...] + mean_scale * jnp.sum(fit[0:TILE].T, axis=0, keepdims=True)
     head = lax.dot_general(mean_p, inv, NT, precision=HIGHEST, preferred_element_type=F32)
     mean_ref[...] = mean_mid - lax.dot_general(head, wide_r, NT, precision=HIGHEST, preferred_element_type=F32)
     for h in range(2):
@@ -462,67 +463,74 @@
     z_in = lax.all_to_all(z_out, "z", 0, 0, tiled=True)
     t_rows = trace_rows(inducing, inv_sq_lengths, z_out)
 
-    xy_out, chunk = relay(ints(o_z, half), z_in, t_rows, mean_old)
+    xy_out, chunk = relay(ints(o_z, half, my_z), z_in, t_rows, mean_old)
     xy_in = lax.all_to_all(xy_out, XY, 0, 0, tiled=True)
     chunk = jnp.where(my_yl == o_yl, chunk, swapped(chunk, "yl", 2, 1))
     xy_in, chunk = lax.optimization_barrier((xy_in, chunk))
 
-    own_x = xy_in[:, :128].reshape(HALF, 128)
-    own_yy = xy_in[:, 128]
     chosen = lax.dynamic_index_in_dim(xy_in, o_xy, 0, keepdims=False).astype(F32)
     trace_xy = jnp.sum(xy_in[:, 133:136].astype(F32), axis=(0, 1))
-    diag_piece = jnp.concatenate(
-        [chosen[144:176] + chosen[208:240], chosen[176:208] + chosen[240:272]], axis=1
+    diagonal = chosen[136] + chosen[137]
+    mine = jnp.concatenate(
+        [
+            jnp.concatenate([chosen[160:176] + chosen[192:208], chosen[144:160] + chosen[176:192]], axis=1),
+            jnp.concatenate([trace_xy, diagonal])[None, :],
+            (chosen[129:131] + chosen[131:133]).reshape(1, PB),
+            jnp.zeros((6, PB), F32),
+        ],
+        axis=0,
     )
-    mean_panel = (chosen[129:131] + chosen[131:133]).reshape(1, PB)
-    wide_trace = jnp.pad(trace_xy[None, :], ((0, 0), (0, 128)))
-    mine = jnp.concatenate([diag_piece, wide_trace, mean_panel, jnp.zeros((6, PB), F32)], axis=0)
-    blocks = lax.all_to_all(jnp.broadcast_to(mine[None], (8, 40, PB)), "z", 0, 0, tiled=True)
-    core_in = swapped(jnp.concatenate([own_x, own_yy], axis=0), "core", 2, 1)
+    near = lax.all_to_all(jnp.broadcast_to(mine[None], (8, 24, PB)), "z", 0, 0, tiled=True)
+    core_out = jnp.concatenate([xy_in[:, :128].reshape(HALF, 128), xy_in[:, 128]], axis=0)
+    core_in = swapped(core_out, "core", 2, 1)
+    crossed = lax.ppermute(chunk, ALL, [(16 * i + j, 16 * j + i) for i in range(16) for j in range(16)])
     far_r = swapped(chunk, "z", 8, 4)
-    crossed = lax.ppermute(chunk, ALL, [(16 * i + j, 16 * j + i) for i in range(16) for j in range(16)])
+    xy_in, crossed = lax.optimization_barrier((xy_in, crossed))
+    two_c = jnp.stack([crossed, swapped(crossed, "core", 2, 1)])
     idx = ints(my_row, my_col, panel[0])
-    carry = gram_part(idx, inducing, inv_sq_lengths, own_x, own_yy, None)
-    carry, blocks, core_in, far_r, crossed, chunk, own_yy = lax.optimization_barrier(
-        (carry, blocks, core_in, far_r, crossed, chunk, own_yy)
+    part1 = gram_part(
+        idx,
+        inducing,
+        inv_sq_lengths,
+        xy_in,
+        pl.BlockSpec((4, 128, 128), lambda i, idx: (i, 0, 0)),
+        pl.BlockSpec((16, 16, 128), lambda i, idx: (0, 8, 0)),
     )
-
-    other_x = core_in[:HALF]
-    other_yy = core_in[HALF : HALF + 16]
-    blocks_in = swapped(blocks, "core", 2, 1)
+    part1, near, core_in, far_r, two_c, chunk = lax.optimization_barrier(
+        (part1, near, core_in, far_r, two_c, chunk)
+    )
+
+    far = swapped(near, "core", 2, 1)
     two_r = jnp.stack([chunk, far_r])
     two_r = jnp.stack([two_r, swapped(two_r, "z", 8, 2)], axis=1)
-    two_c = jnp.stack([crossed, swapped(crossed, "core", 2, 1)])
-    gram, gram_p, fit = gram_part(idx, inducing, inv_sq_lengths, other_x, other_yy, carry)
+    four_c = jnp.stack([two_c, swapped(two_c, "x", 4, 1)])
+    part2 = gram_part(
+        idx,
+        inducing,
+        inv_sq_lengths,
+        core_in,
+        pl.BlockSpec((CHUNK, 128), lambda i, idx: (i, 0)),
+        pl.BlockSpec((16, 128), lambda i, idx: (HALF // 16, 0)),
+    )
+    part1, part2, near, far, two_r, four_c = lax.optimization_barrier((part1, part2, near, far, two_r, four_c))
+
+    got_r = jnp.stack([two_r, swapped(two_r, "z", 8, 1)], axis=2)
+    got_c = jnp.stack([four_c, swapped(four_c, "x", 4, 2)])
     here = my_core == o_core
-    diag = jnp.concatenate(
-        [
-            jnp.where(here, blocks[:, :32], blocks_in[:, :32]),
-            blocks[:, 32:33],
-            blocks_in[:, 32:33],
-            jnp.where(here, blocks[:, 33:34], blocks_in[:, 33:34]),
-            jnp.zeros((8, 5, PB), F32),
-        ],
-        axis=1,
-    )
-    gram, gram_p, fit, diag, two_r, two_c = lax.optimization_barrier((gram, gram_p, fit, diag, two_r, two_c))
-
-    got_r = jnp.stack([two_r, swapped(two_r, "z", 8, 1)], axis=2)
-    got_c = jnp.stack([two_c] + [swapped(two_c, "x", 4, k) for k in (1, 2, 3)])
-    factor, inv_factor = factored(diag, gram_p)
-    all_y = jnp.concatenate([own_yy, other_yy], axis=0)
-    in_row = my_row == owner
-    in_col = my_col == owner
+    factor, inv_factor = factored(ints(here), near, far, part1[1], part2[1])
     updated, mean_next = finish(
-        ints(my_z, 2 * my_x + my_core, half, in_row, in_col),
-        diag,
-        all_y,
+        ints(my_z, 2 * my_x + my_core, half, my_row == owner, my_col == owner, here),
+        near,
+        far,
         mean_old.reshape(1, TILE),
         factor,
         inv_factor,
-        gram,
-        gram_p,
-        fit,
+        part1[0],
+        part2[0],
+        part1[1],
+        part2[1],
+        part1[2],
+        part2[2],
         got_r.reshape(8, 64, PB),
         got_c.reshape(8, 64, PB),
         prec_old,

time: 127 us -> 119 us (0.937)
  waiting for transfers between devices: 28.9 us -> 24.8 us
  local copies, waits for them, and re-layouts: 10 us -> 6.56 us
  Pallas kernels: 44.2 us -> 45.9 us
    all_to_all x1, waiting for transfers between devices: 9.1 us -> 7.08 us  [local(): xy_in = lax.all_to_all(xy_out, XY, 0, 0, tiled=True)]
    select_n x2 -> x0, other arithmetic: 1.93 us -> none  [the longest x1 0.99 us: local(): jnp.where(here, blocks[:, :32], blocks_in[:, :32])]
    slice x3 -> x1, local copies, waits for them, and re-layouts: 1.8 us -> 0.04 us  [local(): xy_in[:, :128].reshape(HALF, 128)]
    ppermute x10 -> x9, waiting for transfers between devices: 7.45 us -> 5.99 us  [swapped(): return lax.ppermute(value, axis, [(i, i ^ bit) for i in range(size)])]
    concatenate x2 -> x1, local copies, waits for them, and re-layouts: 1.47 us -> 0.07 us  [local(): jnp.concatenate([jnp.concatenate([chosen[160:176] + chosen[192:208], chos...]
    ppermute x10 -> x9, starting transfers between devices: 13.6 us -> 13.2 us  [swapped(): return lax.ppermute(value, axis, [(i, i ^ bit) for i in range(size)])]
    unnamed x24 -> x30, local copies, waits for them, and re-layouts: 5.65 us -> 5.47 us
  transfers between devices with their start and end apart: 14 -> 13, of which waited for: 4 -> 3; matrix products, arithmetic and copies ran while one was open for 1% -> 2% of each run, Pallas kernels for 28% -> 30%
where the time goes in v3:
time: 119 us
  Pallas kernels  45.9 us (39%)
  starting transfers between devices  37.6 us (32%)
  waiting for transfers between devices  24.8 us (21%)
  local copies, waits for them, and re-layouts  6.56 us (6%)
  other arithmetic  2.23 us (2%)
  between operations  1.7 us (1%)
    pallas_call x2, Pallas kernels, gram_part(): pl.pallas_call(gram_kernel, grid_spec=pltpu.PrefetchScalarGridSpec(num_sc...  14.8 us
    pallas_call x1, Pallas kernels, factored(): pl.pallas_call(factor_kernel, in_specs=[pl.BlockSpec(memory_space=pltpu.S...  13.8 us
    ppermute x9, starting transfers between devices, swapped(): return lax.ppermute(value, axis, [(i, i ^ bit) for i in range(size)])  13.2 us
    all_to_all x1, waiting for transfers between devices, local(): z_in = lax.all_to_all(z_out, 'z', 0, 0, tiled=True)  11.7 us
    all_to_all x1, starting transfers between devices, local(): z_in = lax.all_to_all(z_out, 'z', 0, 0, tiled=True)  9 us
    all_to_all x1, waiting for transfers between devices, local(): xy_in = lax.all_to_all(xy_out, XY, 0, 0, tiled=True)  7.08 us
    pallas_call x1, Pallas kernels, trace_rows(): pl.pallas_call(trace_kernel, grid=(M // 1024,), in_specs=[pl.BlockSpec((1...  7.07 us
    all_to_all x1, starting transfers between devices, local(): xy_in = lax.all_to_all(xy_out, XY, 0, 0, tiled=True)  6.89 us
  transfers between devices with their start and end apart: 13, of which 3 were waited for; matrix products, arithmetic and copies ran while one was open for 2% of the time, Pallas kernels for 30%

profile of v3, /device:TPU:1, one launch (start us, length us, event | category | flops | bytes accessed | tf_op | source)
XLA Modules:
  0.0 118.8 jit_solution(8280629342418219592)
XLA Ops:
  1.3 0.5 compare_select_fusion.1.idx_ref
  1.8 2.7 %pack.1.x_ref = bf16[8,288,128]{2,1,0:T(8,128)(2,1)} custom-call(s32[2]{0:T(128)} %compare_select_fusion.1.idx_ref, s32[16]{0:T(128)} %picks_ref.1, bf16[128,128]{1,0:T(8,128)(2,1)} %pool_ref.1, bf16[1,128]{1,0:T(2,128)(2,1)} %bitcast.60, f32[512,512]{1,0:T(8,128)} %prec_ref.3), custom_call_target="tpu_custom_call" | custom-call | tf_op jit(solution)/shard_map/pack/pallas_call | solution.py:93
  4.5 9.0 %all-to-all-start = ((bf16[8,288,128]{2,1,0:T(8,128)(2,1)}), bf16[8,288,128]{2,1,0:T(8,128)(2,1)S(1)}, u32[]{:S(2)}, u32[]{:S(2)}) async-start(bf16[8,288,128]{2,1,0:T(8,128)(2,1)} %pack.1.x_ref), calls=%async_computation | async-start | bytes 1179648 | tf_op jit(solution)/shard_map/all_to_all | solution.py:463
  13.5 0.6 compare_select_fusion.12.idx_ref
  14.1 7.1 %trace_rows.1.t_ref = bf16[16,128]{1,0:T(8,128)(2,1)} custom-call(f32[8192,128]{1,0:T(8,128)} %pp_ref.3, f32[1,128]{1,0:T(1,128)} %bitcast.43, bf16[8,288,128]{2,1,0:T(8,128)(2,1)} %pack.1.x_ref), custom_call_target="tpu_custom_call" | custom-call | flops 4000000000 | bytes 4000000 | tf_op jit(solution)/shard_map/trace_rows/pallas_call | solution.py:136
  21.2 11.7 %all-to-all-done.z_ref = bf16[8,288,128]{2,1,0:T(8,128)(2,1)S(1)} async-done(((bf16[8,288,128]{2,1,0:T(8,128)(2,1)}), bf16[8,288,128]{2,1,0:T(8,128)(2,1)S(1)}, u32[]{:S(2)}, u32[]{:S(2)}) %all-to-all-start) | async-done | bytes 589856 | tf_op jit(solution)/shard_map/all_to_all | solution.py:463
  32.9 0.8 copy-done.13
  33.7 2.1 %relay.1 = (bf16[16,208,128]{2,1,0:T(8,128)(2,1)}, f32[64,256]{1,0:T(8,128)}) custom-call(s32[3]{0:T(128)} %compare_select_fusion.12.idx_ref, bf16[8,288,128]{2,1,0:T(8,128)(2,1)} %copy-done.13, bf16[16,128]{1,0:T(8,128)(2,1)} %trace_rows.1.t_ref, f32[4,128]{1,0:T(4,128)} %bitcast.41), custom_call_target="tpu_custom_call" | custom-call | tf_op jit(solution)/shard_map/relay/pallas_call | solution.py:186
  35.8 6.9 %all-to-all-start.1 = ((bf16[16,208,128]{2,1,0:T(8,128)(2,1)}), bf16[16,208,128]{2,1,0:T(8,128)(2,1)S(1)}, u32[]{:S(2)}, u32[]{:S(2)}) async-start(bf16[16,208,128]{2,1,0:T(8,128)(2,1)} %get-tuple-element.36), calls=%async_computation.1 | async-start | bytes 1703936 | tf_op jit(solution)/shard_map/all_to_all | solution.py:467
  42.8 1.3 %collective-permute-start = (f32[64,256]{1,0:T(8,128)S(1)}, f32[64,256]{1,0:T(8,128)S(1)}, u32[]{:S(2)}, u32[]{:S(2)}) collective-permute-start(f32[64,256]{1,0:T(8,128)S(1)} %copy-done.14), channel_id=1, source_target_pairs={{0,8},{8,0},{1,9},{9,1},{2,10},{10,2},{3,11},{11,3},{4,12},{12,4},... | collective-permute-start | bytes 196616 | tf_op jit(solution)/shard_map/ppermute | solution.py:33
  44.2 6.0 %collective-permute-done = f32[64,256]{1,0:T(8,128)S(1)} collective-permute-done((f32[64,256]{1,0:T(8,128)S(1)}, f32[64,256]{1,0:T(8,128)S(1)}, u32[]{:S(2)}, u32[]{:S(2)}) %collective-permute-start) | collective-permute-done | bytes 65568 | tf_op jit(solution)/shard_map/ppermute | solution.py:33
  50.2 7.1 %all-to-all-done.1.x_ref.y_ref = bf16[16,208,128]{2,1,0:T(8,128)(2,1)S(1)} async-done(((bf16[16,208,128]{2,1,0:T(8,128)(2,1)}), bf16[16,208,128]{2,1,0:T(8,128)(2,1)S(1)}, u32[]{:S(2)}, u32[]{:S(2)}) %all-to-all-start.1) | async-done | bytes 852000 | tf_op jit(solution)/shard_map/all_to_all | solution.py:467
  57.2 3.0 %collective-permute-start.1 = (f32[64,256]{1,0:T(8,128)S(1)}, f32[64,256]{1,0:T(8,128)S(1)}, u32[]{:S(2)}, u32[]{:S(2)}) collective-permute-start(f32[64,256]{1,0:T(8,128)S(1)} %broadcast_select_fusion), channel_id=1, source_target_pairs={{0,0},{1,16},{2,32},{3,48},{4,64},{5,80},{6,96},{7,112},{8,128},{9... | collective-permute-start | bytes 196616 | tf_op jit(solution)/shard_map/ppermute | solution.py:486
  60.4 0.2 copy.23
  60.7 0.7 broadcast_in_dim.87
  61.4 5.6 %all-to-all-start.2 = ((f32[8,24,256]{2,1,0:T(8,128)}), f32[8,24,256]{2,1,0:T(8,128)S(1)}, u32[]{:S(2)}, u32[]{:S(2)}) async-start(f32[8,24,256]{2,1,0:T(8,128)} %broadcast_in_dim.87), calls=%async_computation.2 | async-start | bytes 393216 | tf_op jit(solution)/shard_map/all_to_all | solution.py:483
  67.0 0.8 pad_maximum_fusion
  67.8 2.5 %collective-permute-start.2 = (bf16[2064,128]{1,0:T(8,128)(2,1)}, bf16[2064,128]{1,0:T(8,128)(2,1)S(1)}, u32[]{:S(2)}, u32[]{:S(2)}) collective-permute-start(bf16[2064,128]{1,0:T(8,128)(2,1)} %pad_maximum_fusion), channel_id=1, source_target_pairs={{0,16},{16,0},{1,17},{17,1},{2,18},{18,2},{3,19},{19,3},{4,20},{20... | collective-permute-start | bytes 1585160 | tf_op jit(solution)/shard_map/ppermute | solution.py:33
  70.3 7.5 %gram_part.2 = (f32[512,512]{1,0:T(8,128)S(1)}, f32[1280,256]{1,0:T(8,128)S(1)}, f32[776,128]{1,0:T(8,128)S(1)}) custom-call(s32[3]{0:T(128)S(1)} %compare_select_fusion.13.idx_ref, f32[8192,128]{1,0:T(8,128)} %pp_ref.3, f32[8192,128]{1,0:T(8,128)} %pp_ref.3, f32[8192,128]{1,0:T(8,128)} %pp_ref.3, f32[1,128]{1,0:T(1,128)S(1)} %bitcast.44, ...), custom_call_target="tpu_custom_call" | custom-call | flops 12000000000 | bytes 8000000 | tf_op jit(solution)/shard_map/gram_part/pallas_call | solution.py:245
  77.9 1.1 copy-done.7
  79.0 0.1 collective-permute-start.7
  79.1 0.8 collective-permute-start.5
  79.9 2.7 %collective-permute-start.6 = (f32[2,64,256]{2,1,0:T(8,128)S(1)}, f32[2,64,256]{2,1,0:T(8,128)S(1)}, u32[]{:S(2)}, u32[]{:S(2)}) collective-permute-start(f32[2,64,256]{2,1,0:T(8,128)S(1)} %get-tuple-element.71), channel_id=1, source_target_pairs={{0,2},{1,3},{2,0},{3,1},{4,6},{5,7},{6,4},{7,5},{8,10},{9,11},{10,... | collective-permute-start | bytes 393224 | tf_op jit(solution)/shard_map/ppermute | solution.py:33
  82.7 7.3 %gram_part.3 = (f32[512,512]{1,0:T(8,128)S(1)}, f32[1280,256]{1,0:T(8,128)S(1)}, f32[776,128]{1,0:T(8,128)S(1)}) custom-call(s32[3]{0:T(128)S(1)} %compare_select_fusion.13.idx_ref, f32[8192,128]{1,0:T(8,128)} %pp_ref.3, f32[8192,128]{1,0:T(8,128)} %pp_ref.3, f32[8192,128]{1,0:T(8,128)} %pp_ref.3, f32[1,128]{1,0:T(1,128)S(1)} %bitcast.45, ...), custom_call_target="tpu_custom_call" | custom-call | flops 12000000000 | bytes 8000000 | tf_op jit(solution)/shard_map/gram_part/pallas_call | solution.py:245
  90.0 1.1 copy-done.8
  91.1 0.9 copy-done.9
  92.0 1.2 %collective-permute-start.8 = (f32[2,2,64,256]{3,2,0,1:T(8,128)S(1)}, f32[2,2,64,256]{3,2,0,1:T(8,128)S(1)}, u32[]{:S(2)}, u32[]{:S(2)}) collective-permute-start(f32[2,2,64,256]{3,2,0,1:T(8,128)S(1)} %pad_maximum_fusion.3), channel_id=1, source_target_pairs={{0,1},{1,0},{2,3},{3,2},{4,5},{5,4},{6,7},{7,6},{8,9},{9,8},{10,11... | collective-permute-start | bytes 786440 | tf_op jit(solution)/shard_map/ppermute | solution.py:33
  93.2 4.4 %collective-permute-start.9 = (f32[2,2,64,256]{3,2,1,0:T(8,128)S(1)}, f32[2,2,64,256]{3,2,1,0:T(8,128)S(1)}, u32[]{:S(2)}, u32[]{:S(2)}) collective-permute-start(f32[2,2,64,256]{3,2,1,0:T(8,128)S(1)} %pad_maximum_fusion.4), channel_id=1, source_target_pairs={{0,64},{32,96},{64,0},{96,32},{1,65},{33,97},{65,1},{97,33},{2,66}... | collective-permute-start | bytes 786440 | tf_op jit(solution)/shard_map/ppermute | solution.py:33
  97.7 13.8 %factored.1 = (f32[256,256]{1,0:T(8,128)}, f32[256,256]{1,0:T(8,128)}) custom-call(s32[1]{0:T(128)} %bitcast.20.idx_ref, f32[8,24,256]{2,1,0:T(8,128)} %copy-done.1, f32[8,24,256]{2,1,0:T(8,128)} %copy-done.4, f32[1280,256]{1,0:T(8,128)} %copy-done.7, f32[1280,256]{1,0:T(8,128)} %copy-done.8), custom_call_target="tpu_custom_call" | custom-call | flops 16000000000 | bytes 1000000 | tf_op jit(solution)/shard_map/factored/pallas_call | solution.py:368
  111.7 1.0 copy-done.10
  112.7 0.3 copy-done
  113.2 5.5 %finish.1 = (f32[512,512]{1,0:T(8,128)}, f32[1,512]{1,0:T(1,128)}) custom-call(s32[6]{0:T(128)S(1)} %compare_select_fusion.7.idx_ref, f32[8,24,256]{2,1,0:T(8,128)S(1)} %copy-done.2, f32[8,24,256]{2,1,0:T(8,128)S(1)} %copy-done.5, f32[1,512]{1,0:T(1,128)S(1)} %bitcast.42, f32[256,256]{1,0:T(8,128)S(1)} %copy-done.11, f32[256,256]{1,0:T(8,128)S(1)} %copy-done.12, ...), custom_call_target="tpu_custom_call" | custom-call | flops 4000000000 | bytes 4000000 | tf_op jit(solution)/shard_map/finish/pallas_call | solution.py:430
  (57 shorter events, 0.8 us)
Async XLA Ops:
  4.5 28.4 %all-to-all-start = ((bf16[8,288,128]{2,1,0:T(8,128)(2,1)}), bf16[8,288,128]{2,1,0:T(8,128)(2,1)S(1)}, u32[]{:S(2)}, u32[]{:S(2)}) async-start(bf16[8,288,128]{2,1,0:T(8,128)(2,1)} %pack.1.x_ref), calls=%async_computation | async-start | bytes 1179648 | tf_op jit(solution)/shard_map/all_to_all | solution.py:463
  32.9 0.8 copy-start.13
  35.8 7.1 %copy-start.14 = (f32[64,256]{1,0:T(8,128)S(1)}, f32[64,256]{1,0:T(8,128)}, u32[]{:S(2)}) copy-start(f32[64,256]{1,0:T(8,128)} %get-tuple-element.37) | copy-start | bytes 196612
  35.8 21.5 %all-to-all-start.1 = ((bf16[16,208,128]{2,1,0:T(8,128)(2,1)}), bf16[16,208,128]{2,1,0:T(8,128)(2,1)S(1)}, u32[]{:S(2)}, u32[]{:S(2)}) async-start(bf16[16,208,128]{2,1,0:T(8,128)(2,1)} %get-tuple-element.36), calls=%async_computation.1 | async-start | bytes 1703936 | tf_op jit(solution)/shard_map/all_to_all | solution.py:467
  42.8 7.3 %collective-permute-start = (f32[64,256]{1,0:T(8,128)S(1)}, f32[64,256]{1,0:T(8,128)S(1)}, u32[]{:S(2)}, u32[]{:S(2)}) collective-permute-start(f32[64,256]{1,0:T(8,128)S(1)} %copy-done.14), channel_id=1, source_target_pairs={{0,8},{8,0},{1,9},{9,1},{2,10},{10,2},{3,11},{11,3},{4,12},{12,4},... | collective-permute-start | bytes 196616 | tf_op jit(solution)/shard_map/ppermute | solution.py:33
  57.2 21.7 %collective-permute-start.3 = (f32[64,256]{1,0:T(8,128)S(1)}, f32[64,256]{1,0:T(8,128)S(1)}, u32[]{:S(2)}, u32[]{:S(2)}) collective-permute-start(f32[64,256]{1,0:T(8,128)S(1)} %broadcast_select_fusion), channel_id=1, source_target_pairs={{0,4},{1,5},{2,6},{3,7},{4,0},{5,1},{6,2},{7,3},{8,12},{9,13},{10,... | collective-permute-start | bytes 196616 | tf_op jit(solution)/shard_map/ppermute | solution.py:33
  57.2 13.1 %collective-permute-start.1 = (f32[64,256]{1,0:T(8,128)S(1)}, f32[64,256]{1,0:T(8,128)S(1)}, u32[]{:S(2)}, u32[]{:S(2)}) collective-permute-start(f32[64,256]{1,0:T(8,128)S(1)} %broadcast_select_fusion), channel_id=1, source_target_pairs={{0,0},{1,16},{2,32},{3,48},{4,64},{5,80},{6,96},{7,112},{8,128},{9... | collective-permute-start | bytes 196616 | tf_op jit(solution)/shard_map/ppermute | solution.py:486
  60.4 10.0 %copy-start.6 = (f32[128]{0:T(128)S(1)}, f32[128]{0:T(128)}, u32[]{:S(2)}) copy-start(f32[128]{0:T(128)} %param.12) | copy-start | bytes 1540
  61.4 17.6 %all-to-all-start.2 = ((f32[8,24,256]{2,1,0:T(8,128)}), f32[8,24,256]{2,1,0:T(8,128)S(1)}, u32[]{:S(2)}, u32[]{:S(2)}) async-start(f32[8,24,256]{2,1,0:T(8,128)} %broadcast_in_dim.87), calls=%async_computation.2 | async-start | bytes 393216 | tf_op jit(solution)/shard_map/all_to_all | solution.py:483
  67.8 11.2 %collective-permute-start.2 = (bf16[2064,128]{1,0:T(8,128)(2,1)}, bf16[2064,128]{1,0:T(8,128)(2,1)S(1)}, u32[]{:S(2)}, u32[]{:S(2)}) collective-permute-start(bf16[2064,128]{1,0:T(8,128)(2,1)} %pad_maximum_fusion), channel_id=1, source_target_pairs={{0,16},{16,0},{1,17},{17,1},{2,18},{18,2},{3,19},{19,3},{4,20},{20... | collective-permute-start | bytes 1585160 | tf_op jit(solution)/shard_map/ppermute | solution.py:33
  70.3 8.6 %collective-permute-start.4 = (f32[64,256]{1,0:T(8,128)S(1)}, f32[64,256]{1,0:T(8,128)S(1)}, u32[]{:S(2)}, u32[]{:S(2)}) collective-permute-start(f32[64,256]{1,0:T(8,128)S(1)} %collective-permute-done.1), channel_id=1, source_target_pairs={{0,16},{16,0},{1,17},{17,1},{2,18},{18,2},{3,19},{19,3},{4,20},{20... | collective-permute-start | bytes 196616 | tf_op jit(solution)/shard_map/ppermute | solution.py:33
  77.9 1.1 copy-start.7
  79.0 11.0 %copy-start.1 = (f32[8,24,256]{2,1,0:T(8,128)}, f32[8,24,256]{2,1,0:T(8,128)S(1)}, u32[]{:S(2)}) copy-start(f32[8,24,256]{2,1,0:T(8,128)S(1)} %all-to-all-done.2.near_ref) | copy-start | bytes 589828
  79.0 12.0 %collective-permute-start.7 = (f32[2,64,256]{2,1,0:T(8,128)S(1)}, f32[2,64,256]{2,1,0:T(8,128)S(1)}, u32[]{:S(2)}, u32[]{:S(2)}) collective-permute-start(f32[2,64,256]{2,1,0:T(8,128)S(1)} %pad_maximum_fusion.5), channel_id=1, source_target_pairs={{0,32},{32,0},{64,96},{96,64},{1,33},{33,1},{65,97},{97,65},{2,34}... | collective-permute-start | bytes 393224 | tf_op jit(solution)/shard_map/ppermute | solution.py:33
  79.1 12.0 %collective-permute-start.5 = (f32[8,24,256]{2,1,0:T(8,128)S(1)}, f32[8,24,256]{2,1,0:T(8,128)S(1)}, u32[]{:S(2)}, u32[]{:S(2)}) collective-permute-start(f32[8,24,256]{2,1,0:T(8,128)S(1)} %all-to-all-done.2.near_ref), channel_id=1, source_target_pairs={{0,16},{16,0},{1,17},{17,1},{2,18},{18,2},{3,19},{19,3},{4,20},{20... | collective-permute-start | bytes 589832 | tf_op jit(solution)/shard_map/ppermute | solution.py:33
  79.9 11.1 %collective-permute-start.6 = (f32[2,64,256]{2,1,0:T(8,128)S(1)}, f32[2,64,256]{2,1,0:T(8,128)S(1)}, u32[]{:S(2)}, u32[]{:S(2)}) collective-permute-start(f32[2,64,256]{2,1,0:T(8,128)S(1)} %get-tuple-element.71), channel_id=1, source_target_pairs={{0,2},{1,3},{2,0},{3,1},{4,6},{5,7},{6,4},{7,5},{8,10},{9,11},{10,... | collective-permute-start | bytes 393224 | tf_op jit(solution)/shard_map/ppermute | solution.py:33
  89.9 1.1 copy-start.8
  91.0 1.0 copy-start.9
  92.0 5.7 %copy-start.4 = (f32[8,24,256]{2,1,0:T(8,128)}, f32[8,24,256]{2,1,0:T(8,128)S(1)}, u32[]{:S(2)}) copy-start(f32[8,24,256]{2,1,0:T(8,128)S(1)} %collective-permute-done.5.far_ref) | copy-start | bytes 589828
  92.0 19.4 %collective-permute-start.8 = (f32[2,2,64,256]{3,2,0,1:T(8,128)S(1)}, f32[2,2,64,256]{3,2,0,1:T(8,128)S(1)}, u32[]{:S(2)}, u32[]{:S(2)}) collective-permute-start(f32[2,2,64,256]{3,2,0,1:T(8,128)S(1)} %pad_maximum_fusion.3), channel_id=1, source_target_pairs={{0,1},{1,0},{2,3},{3,2},{4,5},{5,4},{6,7},{7,6},{8,9},{9,8},{10,11... | collective-permute-start | bytes 786440 | tf_op jit(solution)/shard_map/ppermute | solution.py:33
  93.2 18.4 %collective-permute-start.9 = (f32[2,2,64,256]{3,2,1,0:T(8,128)S(1)}, f32[2,2,64,256]{3,2,1,0:T(8,128)S(1)}, u32[]{:S(2)}, u32[]{:S(2)}) collective-permute-start(f32[2,2,64,256]{3,2,1,0:T(8,128)S(1)} %pad_maximum_fusion.4), channel_id=1, source_target_pairs={{0,64},{32,96},{64,0},{96,32},{1,65},{33,97},{65,1},{97,33},{2,66}... | collective-permute-start | bytes 786440 | tf_op jit(solution)/shard_map/ppermute | solution.py:33
  111.4 1.2 %copy-start.10 = (f32[512,512]{1,0:T(8,128)S(1)}, f32[512,512]{1,0:T(8,128)}, u32[]{:S(2)}) copy-start(f32[512,512]{1,0:T(8,128)} %copy-done.9) | copy-start | bytes 3145732
  111.5 1.5 %copy-start = (f32[512,512]{1,0:T(8,128)S(1)}, f32[512,512]{1,0:T(8,128)}, u32[]{:S(2)}) copy-start(f32[512,512]{1,0:T(8,128)} %prec_ref.3) | copy-start | bytes 3145732
  111.5 1.5 %copy-start.2 = (f32[8,24,256]{2,1,0:T(8,128)S(1)}, f32[8,24,256]{2,1,0:T(8,128)}, u32[]{:S(2)}) copy-start(f32[8,24,256]{2,1,0:T(8,128)} %copy-done.1) | copy-start | bytes 589828
  111.5 1.5 %copy-start.3 = (f32[512]{0:T(512)S(1)}, f32[512]{0:T(512)}, u32[]{:S(2)}) copy-start(f32[512]{0:T(512)} %param.14) | copy-start | bytes 6148
  111.5 1.6 %copy-start.5 = (f32[8,24,256]{2,1,0:T(8,128)S(1)}, f32[8,24,256]{2,1,0:T(8,128)}, u32[]{:S(2)}) copy-start(f32[8,24,256]{2,1,0:T(8,128)} %copy-done.4) | copy-start | bytes 589828
  111.5 1.6 %copy-start.11 = (f32[256,256]{1,0:T(8,128)S(1)}, f32[256,256]{1,0:T(8,128)}, u32[]{:S(2)}) copy-start(f32[256,256]{1,0:T(8,128)} %get-tuple-element.60.low_ref) | copy-start | bytes 786436
  111.5 1.7 %copy-start.12 = (f32[256,256]{1,0:T(8,128)S(1)}, f32[256,256]{1,0:T(8,128)}, u32[]{:S(2)}) copy-start(f32[256,256]{1,0:T(8,128)} %get-tuple-element.61.inv_ref) | copy-start | bytes 786436

commit v4 on v3

--- a/solution.py
+++ b/solution.py
@@ -103,6 +103,7 @@
             out_specs=pl.BlockSpec((8, 288, 128), lambda i, idx, picks: (0, 0, 0)),
         ),
         out_shape=jax.ShapeDtypeStruct((8, 288, 128), BF16),
+        compiler_params=pltpu.CompilerParams(vmem_limit_bytes=12 * 1024 * 1024),
         name="pack",
     )(idx, picks, pool, targets[None, :], prec_old)
 
@@ -145,6 +146,7 @@
         out_shape=jax.ShapeDtypeStruct((16, 128), BF16),
         scratch_shapes=[pltpu.VMEM((1024, 256), BF16), pltpu.VMEM((16, 256), BF16), pltpu.VMEM((8, 128), F32)],
         cost_estimate=pl.CostEstimate(flops=4_000_000_000, bytes_accessed=4_000_000, transcendentals=1_000_000),
+        compiler_params=pltpu.CompilerParams(vmem_limit_bytes=16 * 1024 * 1024),
         name="trace_rows",
     )(inducing, weights[None, :], packed)
 
@@ -188,11 +190,12 @@
         in_specs=[pl.BlockSpec(memory_space=pltpu.SMEM), vmem, vmem, vmem],
         out_specs=[vmem, vmem],
         out_shape=[jax.ShapeDtypeStruct((16, 208, 128), BF16), jax.ShapeDtypeStruct((64, PB), F32)],
+        compiler_params=pltpu.CompilerParams(vmem_limit_bytes=12 * 1024 * 1024),
         name="relay",
     )(idx, z_in, t_rows, mean_old.reshape(4, 128))
 
 
-def gram_kernel(idx_ref, pr_ref, pc_ref, pp_ref, w_ref, x_ref, y_ref, grc_ref, gp_ref, fit_ref, paug, own, xaug, ys):
+def gram_kernel(idx_ref, pr_ref, pc_ref, pp_ref, w_ref, x_ref, y_ref, grc_ref, gp_ref, gpp_ref, fit_ref, paug, own, xaug, ys):
     step = pl.program_id(0)
 
     @pl.when(step == 0)
@@ -210,6 +213,7 @@
             ys[k, 0:4, :] = y_all[4 * k : 4 * k + 4]
         grc_ref[...] = jnp.zeros_like(grc_ref)
         gp_ref[...] = jnp.zeros_like(gp_ref)
+        gpp_ref[...] = jnp.zeros_like(gpp_ref)
         fit_ref[...] = jnp.zeros_like(fit_ref)
         fit_ref[TILE + PB : TILE + PB + 1, :] = jnp.sum(y_all * y_all, axis=0, keepdims=True)
 
@@ -231,7 +235,7 @@
     grc_ref[...] += lax.dot_general(f_r, f_c, NT, preferred_element_type=F32)
     gp_ref[0:TILE, :] += lax.dot_general(f_r, f_p, NT, preferred_element_type=F32)
     gp_ref[TILE : 2 * TILE, :] += lax.dot_general(f_c, f_p, NT, preferred_element_type=F32)
-    gp_ref[2 * TILE :, :] += lax.dot_general(f_p, f_p, NT, preferred_element_type=F32)
+    gpp_ref[...] += lax.dot_general(f_p, f_p, NT, preferred_element_type=F32)
     y = ys[step]
     for at, f in ((0, f_r), (TILE, f_p)):
         acc = fit_ref[at : at + f.shape[0], :]
@@ -241,7 +245,7 @@
 
 
 def gram_part(idx, inducing, weights, source, x_spec, y_spec):
-    shapes = ((TILE, TILE), (2 * TILE + PB, PB), (TILE + PB + 8, 128))
+    shapes = ((TILE, TILE), (2 * TILE, PB), (PB, PB), (TILE + PB + 8, 128))
     return pl.pallas_call(
         gram_kernel,
         grid_spec=pltpu.PrefetchScalarGridSpec(
@@ -264,7 +268,7 @@
             ],
         ),
         out_shape=[jax.ShapeDtypeStruct(s, F32) for s in shapes],
-        compiler_params=pltpu.CompilerParams(vmem_limit_bytes=48 * 1024 * 1024),
+        compiler_params=pltpu.CompilerParams(vmem_limit_bytes=28 * 1024 * 1024),
         cost_estimate=pl.CostEstimate(flops=12_000_000_000, bytes_accessed=8_000_000, transcendentals=2_600_000),
         name="gram_part",
     )(idx, inducing, inducing, inducing, weights[None, :], source, source)
@@ -291,7 +295,7 @@
     on = low == lane
     under = jnp.where(low > lane, both, 0.0)
     over = jnp.where(low < lane, both, 0.0)
-    gram = scale * (gp1_ref[2 * TILE :, :] + gp2_ref[2 * TILE :, :])
+    gram = scale * (gp1_ref[...] + gp2_ref[...])
     work[0:128, 0:128] = RATE * (under + under.T + jnp.where(on, both, 0.0)) + gram[0:128, 0:128]
     work[0:128, 128:256] = RATE * low_left.T + gram[0:128, 128:256]
     work[128:256, 0:128] = RATE * low_left + gram[128:256, 0:128]
@@ -377,13 +381,14 @@
             pltpu.VMEM((64, 128), F32),
         ],
         cost_estimate=pl.CostEstimate(flops=16_000_000_000, bytes_accessed=1_000_000, transcendentals=1000),
+        compiler_params=pltpu.CompilerParams(vmem_limit_bytes=12 * 1024 * 1024),
         name="factored",
     )(idx, near, far, gp1, gp2)
 
 
 def finish_kernel(
     idx_ref, near_ref, far_ref, mo_ref, low_ref, inv_ref, g1_ref, g2_ref, gp1_ref, gp2_ref, fit1_ref, fit2_ref,
-    gr_ref, gc_ref, prec_ref, out_ref, mean_ref, jr, jc,
+    gr_ref, hr_ref, gc_ref, hc_ref, prec_ref, out_ref, mean_ref, jr, jc,
 ):
     my_z, my_xc, half, in_row, in_col, here = (idx_ref[k] for k in range(6))
     trace_scale = trace_scale_of(near_ref, far_ref)
@@ -393,12 +398,15 @@
     mean_scale = RATE / jnp.sqrt(trace_scale * (power * (1.0 / B_TOTAL) + EPSILON))
     inv = inv_ref[...]
     for j in range(8):
+        at_r, at_c = j ^ my_z, j ^ my_xc
+        from_r = jnp.where(at_r % 2 == 0, gr_ref[at_r // 2], hr_ref[at_r // 2])
+        from_c = jnp.where(at_c < 4, gc_ref[at_c % 4], hc_ref[at_c % 4])
         for q in range(4):
             rows = slice(128 * q + 16 * j, 128 * q + 16 * j + 16)
             part = slice(16 * q, 16 * q + 16)
             far = slice(TILE + 128 * q + 16 * j, TILE + 128 * q + 16 * j + 16)
-            jr[rows, :] = RATE * gr_ref[j ^ my_z, part, :] + scale * (gp1_ref[rows, :] + gp2_ref[rows, :])
-            jc[rows, :] = RATE * gc_ref[j ^ my_xc, part, :] + scale * (gp1_ref[far, :] + gp2_ref[far, :])
+            jr[rows, :] = RATE * from_r[part] + scale * (gp1_ref[rows, :] + gp2_ref[rows, :])
+            jc[rows, :] = RATE * from_c[part] + scale * (gp1_ref[far, :] + gp2_ref[far, :])
     wide_r = lax.dot_general(jr[...], inv, NT, precision=HIGHEST, preferred_element_type=F32)
     wide_ct = lax.dot_general(inv, jc[...], NT, precision=HIGHEST, preferred_element_type=F32)
     taken = jnp.dot(wide_r, wide_ct, precision=HIGHEST, preferred_element_type=F32)
@@ -433,7 +441,7 @@
         out_specs=[vmem, vmem],
         out_shape=[jax.ShapeDtypeStruct((TILE, TILE), F32), jax.ShapeDtypeStruct((1, TILE), F32)],
         scratch_shapes=[pltpu.VMEM((TILE, PB), F32), pltpu.VMEM((TILE, PB), F32)],
-        compiler_params=pltpu.CompilerParams(vmem_limit_bytes=48 * 1024 * 1024),
+        compiler_params=pltpu.CompilerParams(vmem_limit_bytes=28 * 1024 * 1024),
         cost_estimate=pl.CostEstimate(flops=4_000_000_000, bytes_accessed=4_000_000, transcendentals=1000),
         name="finish",
     )(idx, *args)
@@ -466,7 +474,8 @@
     xy_out, chunk = relay(ints(o_z, half, my_z), z_in, t_rows, mean_old)
     xy_in = lax.all_to_all(xy_out, XY, 0, 0, tiled=True)
     chunk = jnp.where(my_yl == o_yl, chunk, swapped(chunk, "yl", 2, 1))
-    xy_in, chunk = lax.optimization_barrier((xy_in, chunk))
+    crossed = lax.ppermute(chunk, ALL, [(16 * i + j, 16 * j + i) for i in range(16) for j in range(16)])
+    far_r = swapped(chunk, "z", 8, 4)
 
     chosen = lax.dynamic_index_in_dim(xy_in, o_xy, 0, keepdims=False).astype(F32)
     trace_xy = jnp.sum(xy_in[:, 133:136].astype(F32), axis=(0, 1))
@@ -483,8 +492,6 @@
     near = lax.all_to_all(jnp.broadcast_to(mine[None], (8, 24, PB)), "z", 0, 0, tiled=True)
     core_out = jnp.concatenate([xy_in[:, :128].reshape(HALF, 128), xy_in[:, 128]], axis=0)
     core_in = swapped(core_out, "core", 2, 1)
-    crossed = lax.ppermute(chunk, ALL, [(16 * i + j, 16 * j + i) for i in range(16) for j in range(16)])
-    far_r = swapped(chunk, "z", 8, 4)
     xy_in, crossed = lax.optimization_barrier((xy_in, crossed))
     two_c = jnp.stack([crossed, swapped(crossed, "core", 2, 1)])
     idx = ints(my_row, my_col, panel[0])
@@ -502,7 +509,7 @@
 
     far = swapped(near, "core", 2, 1)
     two_r = jnp.stack([chunk, far_r])
-    two_r = jnp.stack([two_r, swapped(two_r, "z", 8, 2)], axis=1)
+    two_r = jnp.stack([two_r, swapped(two_r, "z", 8, 2)], axis=1).reshape(4, 64, PB)
     four_c = jnp.stack([two_c, swapped(two_c, "x", 4, 1)])
     part2 = gram_part(
         idx,
@@ -512,12 +519,13 @@
         pl.BlockSpec((CHUNK, 128), lambda i, idx: (i, 0)),
         pl.BlockSpec((16, 128), lambda i, idx: (HALF // 16, 0)),
     )
+    four_c = four_c.reshape(4, 64, PB)
     part1, part2, near, far, two_r, four_c = lax.optimization_barrier((part1, part2, near, far, two_r, four_c))
 
-    got_r = jnp.stack([two_r, swapped(two_r, "z", 8, 1)], axis=2)
-    got_c = jnp.stack([four_c, swapped(four_c, "x", 4, 2)])
+    more_r = swapped(two_r, "z", 8, 1)
+    more_c = swapped(four_c, "x", 4, 2)
     here = my_core == o_core
-    factor, inv_factor = factored(ints(here), near, far, part1[1], part2[1])
+    factor, inv_factor = factored(ints(here), near, far, part1[2], part2[2])
     updated, mean_next = finish(
         ints(my_z, 2 * my_x + my_core, half, my_row == owner, my_col == owner, here),
         near,
@@ -529,10 +537,12 @@
         part2[0],
         part1[1],
         part2[1],
-        part1[2],
-        part2[2],
-        got_r.reshape(8, 64, PB),
-        got_c.reshape(8, 64, PB),
+        part1[3],
+        part2[3],
+        two_r,
+        more_r,
+        four_c,
+        more_c,
         prec_old,
     )
     return (updated, mean_next.reshape(TILE))

time: 119 us -> 117 us (0.983)
  Pallas kernels: 45.9 us -> 35.3 us
  starting transfers between devices: 37.6 us -> 45 us
  local copies, waits for them, and re-layouts: 6.56 us -> 11.7 us
  waiting for transfers between devices: 24.8 us -> 21.2 us
    all_to_all x1, starting transfers between devices: 5.59 us -> 12.3 us  [local(): lax.all_to_all(jnp.broadcast_to(mine[None], (8, 24, PB)), 'z', 0, 0, tile...]
    all_to_all x1, waiting for transfers between devices: 7.08 us -> 1.36 us  [local(): xy_in = lax.all_to_all(xy_out, XY, 0, 0, tiled=True)]
    unnamed x30 -> x25, local copies, waits for them, and re-layouts: 5.47 us -> 10.8 us
    pallas_call x1, Pallas kernels: 7.07 us -> 4.12 us  [trace_rows(): pl.pallas_call(trace_kernel, grid=(M // 1024,), in_specs=[pl.BlockSpec((1...]
    pallas_call x1, Pallas kernels: 13.8 us -> 11.1 us  [factored(): pl.pallas_call(factor_kernel, in_specs=[pl.BlockSpec(memory_space=pltpu.S...]
    ppermute x1, starting transfers between devices: 2.97 us -> 5.61 us  [local(): lax.ppermute(chunk, ALL, [(16 * i + j, 16 * j + i) for i in range(16) for...]
    pallas_call x2, Pallas kernels: 14.8 us -> 12.6 us  [gram_part(): pl.pallas_call(gram_kernel, grid_spec=pltpu.PrefetchScalarGridSpec(num_sc...]
    ppermute x9, starting transfers between devices: 13.2 us -> 11.4 us  [swapped(): return lax.ppermute(value, axis, [(i, i ^ bit) for i in range(size)])]
  transfers between devices with their start and end apart: 13 -> 13, of which waited for: 3 -> 4; matrix products, arithmetic and copies ran while one was open for 2% -> 2% of each run, Pallas kernels for 30% -> 24%
where the time goes in v4:
time: 117 us
  starting transfers between devices  45 us (38%)
  Pallas kernels  35.3 us (30%)
  waiting for transfers between devices  21.2 us (18%)
  local copies, waits for them, and re-layouts  11.7 us (10%)
  other arithmetic  1.92 us (2%)
  between operations  1.68 us (1%)
    all_to_all x1, waiting for transfers between devices, local(): z_in = lax.all_to_all(z_out, 'z', 0, 0, tiled=True)  13 us
    pallas_call x2, Pallas kernels, gram_part(): pl.pallas_call(gram_kernel, grid_spec=pltpu.PrefetchScalarGridSpec(num_sc...  12.6 us
    all_to_all x1, starting transfers between devices, local(): lax.all_to_all(jnp.broadcast_to(mine[None], (8, 24, PB)), 'z', 0, 0, tile...  12.3 us
    ppermute x9, starting transfers between devices, swapped(): return lax.ppermute(value, axis, [(i, i ^ bit) for i in range(size)])  11.4 us
    pallas_call x1, Pallas kernels, factored(): pl.pallas_call(factor_kernel, in_specs=[pl.BlockSpec(memory_space=pltpu.S...  11.1 us
    unnamed x25, local copies, waits for them, and re-layouts  10.8 us
    all_to_all x1, starting transfers between devices, local(): z_in = lax.all_to_all(z_out, 'z', 0, 0, tiled=True)  9 us
    all_to_all x1, starting transfers between devices, local(): xy_in = lax.all_to_all(xy_out, XY, 0, 0, tiled=True)  6.75 us
  transfers between devices with their start and end apart: 13, of which 4 were waited for; matrix products, arithmetic and copies ran while one was open for 2% of the time, Pallas kernels for 24%

profile of v4, /device:TPU:1, one launch (start us, length us, event | category | flops | bytes accessed | tf_op | source)
XLA Modules:
  0.0 116.8 jit_solution(3697101969774148690)
XLA Ops:
  1.3 1.2 %copy-done = f32[512,512]{1,0:T(8,128)S(1)} copy-done((f32[512,512]{1,0:T(8,128)S(1)}, f32[512,512]{1,0:T(8,128)}, u32[]{:S(2)}) %copy-start) | copy-done | bytes 1048600
  2.5 0.8 copy-done.2
  3.3 0.7 copy-done.4
  4.0 0.7 copy-done.5
  4.6 1.5 %pack.1.x_ref = bf16[8,288,128]{2,1,0:T(8,128)(2,1)} custom-call(s32[2]{0:T(128)S(1)} %compare_select_fusion.1.idx_ref, s32[16]{0:T(128)S(1)} %copy-done.4, bf16[128,128]{1,0:T(8,128)(2,1)S(1)} %copy-done.2, bf16[1,128]{1,0:T(2,128)(2,1)S(1)} %bitcast.42, f32[512,512]{1,0:T(8,128)S(1)} %copy-done), custom_call_target="tpu_custom_call" | custom-call | tf_op jit(solution)/shard_map/pack/pallas_call | solution.py:93
  6.1 9.0 %all-to-all-start = ((bf16[8,288,128]{2,1,0:T(8,128)(2,1)}), bf16[8,288,128]{2,1,0:T(8,128)(2,1)S(1)}, u32[]{:S(2)}, u32[]{:S(2)}) async-start(bf16[8,288,128]{2,1,0:T(8,128)(2,1)} %pack.1.x_ref), calls=%async_computation | async-start | bytes 1179648 | tf_op jit(solution)/shard_map/all_to_all | solution.py:471
  15.1 2.2 %copy-done.6 = f32[8192,128]{1,0:T(8,128)S(1)} copy-done((f32[8192,128]{1,0:T(8,128)S(1)}, f32[8192,128]{1,0:T(8,128)}, u32[]{:S(2)}) %copy-start.6) | copy-done | bytes 4194328
  17.3 4.1 %trace_rows.1.t_ref = bf16[16,128]{1,0:T(8,128)(2,1)S(1)} custom-call(f32[8192,128]{1,0:T(8,128)S(1)} %copy-done.6, f32[1,128]{1,0:T(1,128)S(1)} %bitcast.43, bf16[8,288,128]{2,1,0:T(8,128)(2,1)} %pack.1.x_ref), custom_call_target="tpu_custom_call" | custom-call | flops 4000000000 | bytes 4000000 | tf_op jit(solution)/shard_map/trace_rows/pallas_call | solution.py:137
  21.4 13.0 %all-to-all-done.z_ref = bf16[8,288,128]{2,1,0:T(8,128)(2,1)S(1)} async-done(((bf16[8,288,128]{2,1,0:T(8,128)(2,1)}), bf16[8,288,128]{2,1,0:T(8,128)(2,1)S(1)}, u32[]{:S(2)}, u32[]{:S(2)}) %all-to-all-start) | async-done | bytes 589856 | tf_op jit(solution)/shard_map/all_to_all | solution.py:471
  34.5 1.5 %relay.1 = (bf16[16,208,128]{2,1,0:T(8,128)(2,1)}, f32[64,256]{1,0:T(8,128)S(1)}) custom-call(s32[3]{0:T(128)S(1)} %compare_select_fusion.12.idx_ref, bf16[8,288,128]{2,1,0:T(8,128)(2,1)S(1)} %all-to-all-done.z_ref, bf16[16,128]{1,0:T(8,128)(2,1)S(1)} %trace_rows.1.t_ref, f32[4,128]{1,0:T(4,128)S(1)} %bitcast.40), custom_call_target="tpu_custom_call" | custom-call | tf_op jit(solution)/shard_map/relay/pallas_call | solution.py:188
  36.0 6.8 %all-to-all-start.1 = ((bf16[16,208,128]{2,1,0:T(8,128)(2,1)}), bf16[16,208,128]{2,1,0:T(8,128)(2,1)S(1)}, u32[]{:S(2)}, u32[]{:S(2)}) async-start(bf16[16,208,128]{2,1,0:T(8,128)(2,1)} %get-tuple-element.39), calls=%async_computation.1 | async-start | bytes 1703936 | tf_op jit(solution)/shard_map/all_to_all | solution.py:475
  42.9 1.3 %collective-permute-start = (f32[64,256]{1,0:T(8,128)S(1)}, f32[64,256]{1,0:T(8,128)S(1)}, u32[]{:S(2)}, u32[]{:S(2)}) collective-permute-start(f32[64,256]{1,0:T(8,128)S(1)} %get-tuple-element.40), channel_id=1, source_target_pairs={{0,8},{8,0},{1,9},{9,1},{2,10},{10,2},{3,11},{11,3},{4,12},{12,4},... | collective-permute-start | bytes 196616 | tf_op jit(solution)/shard_map/ppermute | solution.py:33
  44.3 6.0 %collective-permute-done = f32[64,256]{1,0:T(8,128)S(1)} collective-permute-done((f32[64,256]{1,0:T(8,128)S(1)}, f32[64,256]{1,0:T(8,128)S(1)}, u32[]{:S(2)}, u32[]{:S(2)}) %collective-permute-start) | collective-permute-done | bytes 65568 | tf_op jit(solution)/shard_map/ppermute | solution.py:33
  50.4 5.6 %collective-permute-start.1 = (f32[64,256]{1,0:T(8,128)S(1)}, f32[64,256]{1,0:T(8,128)S(1)}, u32[]{:S(2)}, u32[]{:S(2)}) collective-permute-start(f32[64,256]{1,0:T(8,128)S(1)} %broadcast_select_fusion), channel_id=1, source_target_pairs={{0,0},{1,16},{2,32},{3,48},{4,64},{5,80},{6,96},{7,112},{8,128},{9... | collective-permute-start | bytes 196616 | tf_op jit(solution)/shard_map/ppermute | solution.py:477
  56.0 1.4 %all-to-all-done.1.x_ref.y_ref = bf16[16,208,128]{2,1,0:T(8,128)(2,1)S(1)} async-done(((bf16[16,208,128]{2,1,0:T(8,128)(2,1)}), bf16[16,208,128]{2,1,0:T(8,128)(2,1)S(1)}, u32[]{:S(2)}, u32[]{:S(2)}) %all-to-all-start.1) | async-done | bytes 852000 | tf_op jit(solution)/shard_map/all_to_all | solution.py:475
  57.4 0.8 collective-permute-done.1
  58.2 1.2 %collective-permute-start.4 = (f32[64,256]{1,0:T(8,128)S(1)}, f32[64,256]{1,0:T(8,128)}, u32[]{:S(2)}, u32[]{:S(2)}) collective-permute-start(f32[64,256]{1,0:T(8,128)S(1)} %collective-permute-done.1), channel_id=1, source_target_pairs={{0,16},{16,0},{1,17},{17,1},{2,18},{18,2},{3,19},{19,3},{4,20},{20... | collective-permute-start | bytes 196616 | tf_op jit(solution)/shard_map/ppermute | solution.py:33
  59.6 0.7 broadcast_in_dim.87
  60.3 12.3 %all-to-all-start.2 = ((f32[8,24,256]{2,1,0:T(8,128)}), f32[8,24,256]{2,1,0:T(8,128)S(1)}, u32[]{:S(2)}, u32[]{:S(2)}) async-start(f32[8,24,256]{2,1,0:T(8,128)} %broadcast_in_dim.87), calls=%async_computation.2 | async-start | bytes 393216 | tf_op jit(solution)/shard_map/all_to_all | solution.py:492
  72.6 0.8 pad_maximum_fusion
  73.7 2.2 %copy-done.7 = f32[8192,128]{1,0:T(8,128)S(1)} copy-done((f32[8192,128]{1,0:T(8,128)S(1)}, f32[8192,128]{1,0:T(8,128)}, u32[]{:S(2)}) %copy-start.7) | copy-done | bytes 4194328
  75.9 6.4 %gram_part.2 = (f32[512,512]{1,0:T(8,128)S(1)}, f32[1024,256]{1,0:T(8,128)S(1)}, f32[256,256]{1,0:T(8,128)S(1)}, f32[776,128]{1,0:T(8,128)S(1)}) custom-call(s32[3]{0:T(128)S(1)} %compare_select_fusion.13.idx_ref, f32[8192,128]{1,0:T(8,128)S(1)} %copy-done.7, f32[8192,128]{1,0:T(8,128)S(1)} %copy-done.7, f32[8192,128]{1,0:T(8,128)S(1)} %copy-done.7, ...), custom_call_target="tpu_custom_call" | custom-call | flops 12000000000 | bytes 8000000 | tf_op jit(solution)/shard_map/gram_part/pallas_call | solution.py:249
  82.4 1.0 copy-done.10
  83.3 0.8 pad_maximum_fusion.3
  84.2 2.2 %collective-permute-start.7 = (f32[2,64,256]{2,1,0:T(8,128)S(1)}, f32[2,64,256]{2,1,0:T(8,128)S(1)}, u32[]{:S(2)}, u32[]{:S(2)}) collective-permute-start(f32[2,64,256]{2,1,0:T(8,128)S(1)} %pad_maximum_fusion.3), channel_id=1, source_target_pairs={{0,32},{32,0},{64,96},{96,64},{1,33},{33,1},{65,97},{97,65},{2,34}... | collective-permute-start | bytes 393224 | tf_op jit(solution)/shard_map/ppermute | solution.py:33
  87.0 2.5 %collective-permute-start.6 = (f32[2,64,256]{2,1,0:T(8,128)S(1)}, f32[2,64,256]{2,1,0:T(8,128)S(1)}, u32[]{:S(2)}, u32[]{:S(2)}) collective-permute-start(f32[2,64,256]{2,1,0:T(8,128)S(1)} %get-tuple-element.77), channel_id=1, source_target_pairs={{0,2},{1,3},{2,0},{3,1},{4,6},{5,7},{6,4},{7,5},{8,10},{9,11},{10,... | collective-permute-start | bytes 393224 | tf_op jit(solution)/shard_map/ppermute | solution.py:33
  89.5 2.2 %copy-done.8 = f32[8192,128]{1,0:T(8,128)S(1)} copy-done((f32[8192,128]{1,0:T(8,128)S(1)}, f32[8192,128]{1,0:T(8,128)}, u32[]{:S(2)}) %copy-start.8) | copy-done | bytes 4194328
  91.7 6.2 %gram_part.3 = (f32[512,512]{1,0:T(8,128)S(1)}, f32[1024,256]{1,0:T(8,128)S(1)}, f32[256,256]{1,0:T(8,128)S(1)}, f32[776,128]{1,0:T(8,128)S(1)}) custom-call(s32[3]{0:T(128)S(1)} %compare_select_fusion.13.idx_ref, f32[8192,128]{1,0:T(8,128)S(1)} %copy-done.8, f32[8192,128]{1,0:T(8,128)S(1)} %copy-done.8, f32[8192,128]{1,0:T(8,128)S(1)} %copy-done.8, ...), custom_call_target="tpu_custom_call" | custom-call | flops 12000000000 | bytes 8000000 | tf_op jit(solution)/shard_map/gram_part/pallas_call | solution.py:249
  98.0 1.3 %collective-permute-start.8 = (f32[4,64,256]{2,1,0:T(8,128)S(1)}, f32[4,64,256]{2,1,0:T(8,128)S(1)}, u32[]{:S(2)}, u32[]{:S(2)}) collective-permute-start(f32[4,64,256]{2,1,0:T(8,128)S(1)} %bitcast.36), channel_id=1, source_target_pairs={{0,1},{1,0},{2,3},{3,2},{4,5},{5,4},{6,7},{7,6},{8,9},{9,8},{10,11... | collective-permute-start | bytes 786440 | tf_op jit(solution)/shard_map/ppermute | solution.py:33
  99.3 1.9 %collective-permute-start.9 = (f32[4,64,256]{2,1,0:T(8,128)S(1)}, f32[4,64,256]{2,1,0:T(8,128)S(1)}, u32[]{:S(2)}, u32[]{:S(2)}) collective-permute-start(f32[4,64,256]{2,1,0:T(8,128)S(1)} %bitcast.38), channel_id=1, source_target_pairs={{0,64},{32,96},{64,0},{96,32},{1,65},{33,97},{65,1},{97,33},{2,66}... | collective-permute-start | bytes 786440 | tf_op jit(solution)/shard_map/ppermute | solution.py:33
  101.2 11.1 %factored.1 = (f32[256,256]{1,0:T(8,128)S(1)}, f32[256,256]{1,0:T(8,128)S(1)}) custom-call(s32[1]{0:T(128)} %bitcast.22.idx_ref, f32[8,24,256]{2,1,0:T(8,128)S(1)} %all-to-all-done.2.near_ref, f32[8,24,256]{2,1,0:T(8,128)S(1)} %collective-permute-done.5.far_ref, f32[256,256]{1,0:T(8,128)S(1)} %get-tuple-element.62.gp1_ref, ...), custom_call_target="tpu_custom_call" | custom-call | flops 16000000000 | bytes 1000000 | tf_op jit(solution)/shard_map/factored/pallas_call | solution.py:372
  112.3 4.4 %finish.1 = (f32[512,512]{1,0:T(8,128)}, f32[1,512]{1,0:T(1,128)}) custom-call(s32[6]{0:T(128)S(1)} %compare_select_fusion.7.idx_ref, f32[8,24,256]{2,1,0:T(8,128)S(1)} %all-to-all-done.2.near_ref, f32[8,24,256]{2,1,0:T(8,128)S(1)} %collective-permute-done.5.far_ref, f32[1,512]{1,0:T(1,128)S(1)} %bitcast.41, f32[256,256]{1,0:T(8,128)S(1)} %get-tuple-element.64.low_ref, ...), custom_call_target="tpu_custom_call" | custom-call | flops 4000000000 | bytes 4000000 | tf_op jit(solution)/shard_map/finish/pallas_call | solution.py:438
  (49 shorter events, 1.3 us)
Async XLA Ops:
  1.3 1.2 %copy-start = (f32[512,512]{1,0:T(8,128)S(1)}, f32[512,512]{1,0:T(8,128)}, u32[]{:S(2)}) copy-start(f32[512,512]{1,0:T(8,128)} %prec_ref.3) | copy-start | bytes 3145732
  2.5 0.8 copy-start.2
  3.3 0.7 copy-start.4
  4.0 0.7 copy-start.5
  4.6 10.5 %copy-start.9 = (f32[128]{0:T(128)S(1)}, f32[128]{0:T(128)}, u32[]{:S(2)}) copy-start(f32[128]{0:T(128)} %param.12) | copy-start | bytes 1540
  6.1 28.4 %all-to-all-start = ((bf16[8,288,128]{2,1,0:T(8,128)(2,1)}), bf16[8,288,128]{2,1,0:T(8,128)(2,1)S(1)}, u32[]{:S(2)}, u32[]{:S(2)}) async-start(bf16[8,288,128]{2,1,0:T(8,128)(2,1)} %pack.1.x_ref), calls=%async_computation | async-start | bytes 1179648 | tf_op jit(solution)/shard_map/all_to_all | solution.py:471
  15.1 2.2 %copy-start.6 = (f32[8192,128]{1,0:T(8,128)S(1)}, f32[8192,128]{1,0:T(8,128)}, u32[]{:S(2)}) copy-start(f32[8192,128]{1,0:T(8,128)} %pp_ref.3) | copy-start | bytes 12582916
  17.3 17.2 %copy-start.3 = (f32[512]{0:T(512)S(1)}, f32[512]{0:T(512)}, u32[]{:S(2)}) copy-start(f32[512]{0:T(512)} %param.14) | copy-start | bytes 6148
  36.0 21.3 %all-to-all-start.1 = ((bf16[16,208,128]{2,1,0:T(8,128)(2,1)}), bf16[16,208,128]{2,1,0:T(8,128)(2,1)S(1)}, u32[]{:S(2)}, u32[]{:S(2)}) async-start(bf16[16,208,128]{2,1,0:T(8,128)(2,1)} %get-tuple-element.39), calls=%async_computation.1 | async-start | bytes 1703936 | tf_op jit(solution)/shard_map/all_to_all | solution.py:475
  42.9 7.3 %collective-permute-start = (f32[64,256]{1,0:T(8,128)S(1)}, f32[64,256]{1,0:T(8,128)S(1)}, u32[]{:S(2)}, u32[]{:S(2)}) collective-permute-start(f32[64,256]{1,0:T(8,128)S(1)} %get-tuple-element.40), channel_id=1, source_target_pairs={{0,8},{8,0},{1,9},{9,1},{2,10},{10,2},{3,11},{11,3},{4,12},{12,4},... | collective-permute-start | bytes 196616 | tf_op jit(solution)/shard_map/ppermute | solution.py:33
  50.3 33.9 %collective-permute-start.3 = (f32[64,256]{1,0:T(8,128)S(1)}, f32[64,256]{1,0:T(8,128)S(1)}, u32[]{:S(2)}, u32[]{:S(2)}) collective-permute-start(f32[64,256]{1,0:T(8,128)S(1)} %broadcast_select_fusion), channel_id=1, source_target_pairs={{0,4},{1,5},{2,6},{3,7},{4,0},{5,1},{6,2},{7,3},{8,12},{9,13},{10,... | collective-permute-start | bytes 196616 | tf_op jit(solution)/shard_map/ppermute | solution.py:33
  50.4 7.8 %collective-permute-start.1 = (f32[64,256]{1,0:T(8,128)S(1)}, f32[64,256]{1,0:T(8,128)S(1)}, u32[]{:S(2)}, u32[]{:S(2)}) collective-permute-start(f32[64,256]{1,0:T(8,128)S(1)} %broadcast_select_fusion), channel_id=1, source_target_pairs={{0,0},{1,16},{2,32},{3,48},{4,64},{5,80},{6,96},{7,112},{8,128},{9... | collective-permute-start | bytes 196616 | tf_op jit(solution)/shard_map/ppermute | solution.py:477
  58.2 25.1 %collective-permute-start.4 = (f32[64,256]{1,0:T(8,128)S(1)}, f32[64,256]{1,0:T(8,128)}, u32[]{:S(2)}, u32[]{:S(2)}) collective-permute-start(f32[64,256]{1,0:T(8,128)S(1)} %collective-permute-done.1), channel_id=1, source_target_pairs={{0,16},{16,0},{1,17},{17,1},{2,18},{18,2},{3,19},{19,3},{4,20},{20... | collective-permute-start | bytes 196616 | tf_op jit(solution)/shard_map/ppermute | solution.py:33
  60.3 23.9 %all-to-all-start.2 = ((f32[8,24,256]{2,1,0:T(8,128)}), f32[8,24,256]{2,1,0:T(8,128)S(1)}, u32[]{:S(2)}, u32[]{:S(2)}) async-start(f32[8,24,256]{2,1,0:T(8,128)} %broadcast_in_dim.87), calls=%async_computation.2 | async-start | bytes 393216 | tf_op jit(solution)/shard_map/all_to_all | solution.py:492
  73.4 10.8 %collective-permute-start.2 = (bf16[2064,128]{1,0:T(8,128)(2,1)}, bf16[2064,128]{1,0:T(8,128)(2,1)S(1)}, u32[]{:S(2)}, u32[]{:S(2)}) collective-permute-start(bf16[2064,128]{1,0:T(8,128)(2,1)} %pad_maximum_fusion), channel_id=1, source_target_pairs={{0,16},{16,0},{1,17},{17,1},{2,18},{18,2},{3,19},{19,3},{4,20},{20... | collective-permute-start | bytes 1585160 | tf_op jit(solution)/shard_map/ppermute | solution.py:33
  73.7 2.2 %copy-start.7 = (f32[8192,128]{1,0:T(8,128)S(1)}, f32[8192,128]{1,0:T(8,128)}, u32[]{:S(2)}) copy-start(f32[8192,128]{1,0:T(8,128)} %pp_ref.3) | copy-start | bytes 12582916
  82.4 1.0 copy-start.10
  84.2 13.7 %collective-permute-start.7 = (f32[2,64,256]{2,1,0:T(8,128)S(1)}, f32[2,64,256]{2,1,0:T(8,128)S(1)}, u32[]{:S(2)}, u32[]{:S(2)}) collective-permute-start(f32[2,64,256]{2,1,0:T(8,128)S(1)} %pad_maximum_fusion.3), channel_id=1, source_target_pairs={{0,32},{32,0},{64,96},{96,64},{1,33},{33,1},{65,97},{97,65},{2,34}... | collective-permute-start | bytes 393224 | tf_op jit(solution)/shard_map/ppermute | solution.py:33
  86.5 11.5 %collective-permute-start.5 = (f32[8,24,256]{2,1,0:T(8,128)S(1)}, f32[8,24,256]{2,1,0:T(8,128)S(1)}, u32[]{:S(2)}, u32[]{:S(2)}) collective-permute-start(f32[8,24,256]{2,1,0:T(8,128)S(1)} %all-to-all-done.2.near_ref), channel_id=1, source_target_pairs={{0,16},{16,0},{1,17},{17,1},{2,18},{18,2},{3,19},{19,3},{4,20},{20... | collective-permute-start | bytes 589832 | tf_op jit(solution)/shard_map/ppermute | solution.py:33
  87.0 10.9 %collective-permute-start.6 = (f32[2,64,256]{2,1,0:T(8,128)S(1)}, f32[2,64,256]{2,1,0:T(8,128)S(1)}, u32[]{:S(2)}, u32[]{:S(2)}) collective-permute-start(f32[2,64,256]{2,1,0:T(8,128)S(1)} %get-tuple-element.77), channel_id=1, source_target_pairs={{0,2},{1,3},{2,0},{3,1},{4,6},{5,7},{6,4},{7,5},{8,10},{9,11},{10,... | collective-permute-start | bytes 393224 | tf_op jit(solution)/shard_map/ppermute | solution.py:33
  89.5 2.2 %copy-start.8 = (f32[8192,128]{1,0:T(8,128)S(1)}, f32[8192,128]{1,0:T(8,128)}, u32[]{:S(2)}) copy-start(f32[8192,128]{1,0:T(8,128)} %pp_ref.3) | copy-start | bytes 12582916
  98.0 14.3 %collective-permute-start.8 = (f32[4,64,256]{2,1,0:T(8,128)S(1)}, f32[4,64,256]{2,1,0:T(8,128)S(1)}, u32[]{:S(2)}, u32[]{:S(2)}) collective-permute-start(f32[4,64,256]{2,1,0:T(8,128)S(1)} %bitcast.36), channel_id=1, source_target_pairs={{0,1},{1,0},{2,3},{3,2},{4,5},{5,4},{6,7},{7,6},{8,9},{9,8},{10,11... | collective-permute-start | bytes 786440 | tf_op jit(solution)/shard_map/ppermute | solution.py:33
  99.3 13.0 %collective-permute-start.9 = (f32[4,64,256]{2,1,0:T(8,128)S(1)}, f32[4,64,256]{2,1,0:T(8,128)S(1)}, u32[]{:S(2)}, u32[]{:S(2)}) collective-permute-start(f32[4,64,256]{2,1,0:T(8,128)S(1)} %bitcast.38), channel_id=1, source_target_pairs={{0,64},{32,96},{64,0},{96,32},{1,65},{33,97},{65,1},{97,33},{2,66}... | collective-permute-start | bytes 786440 | tf_op jit(solution)/shard_map/ppermute | solution.py:33
  101.2 11.1 %copy-start.1 = (f32[512,512]{1,0:T(8,128)S(1)}, f32[512,512]{1,0:T(8,128)}, u32[]{:S(2)}) copy-start(f32[512,512]{1,0:T(8,128)} %prec_ref.3) | copy-start | bytes 3145732
  101.2 11.1 %copy-start.11 = (f32[1024,256]{1,0:T(8,128)S(1)}, f32[1024,256]{1,0:T(8,128)}, u32[]{:S(2)}) copy-start(f32[1024,256]{1,0:T(8,128)} %copy-done.10) | copy-start | bytes 3145732
